TPU v7x, 32 devices: a whole 2x2x4 slice. The times are simulated.
32 devices in a mesh: dp: 8 (over y, x, core), seq: 4 (over z).
Axes of the slice: x: 2, y: 2, z: 4, core: 2. Of those that a mesh axis runs over, the one named last changes fastest.
Arguments:
- tokens: bfloat16 [8, 2048, 2048], P('dp', 'seq'), may hold values from -6 to 6
- lengths: int32 [8], P('dp'), may hold values from 1024 to 2048, as said below
- cotangent: bfloat16 [8, 2048, 2048], P('dp', 'seq'), may hold values from -6 to 6
- w_query: bfloat16 [2048, 2048], P('dp', 'seq'), may hold values from -0.125 to 0.125
- key_weight: bfloat16 [2048, 1024], P('dp', 'seq'), may hold values from -0.125 to 0.125
- value_weight: bfloat16 [2048, 1024], P('dp', 'seq'), may hold values from -0.125 to 0.125
- w_out: bfloat16 [2048, 2048], P('seq', 'dp'), may hold values from -0.75 to 0.75
- w_gate: bfloat16 [2048, 6144], P('dp', 'seq'), may hold values from -0.125 to 0.125
- w_up: bfloat16 [2048, 6144], P('dp', 'seq'), may hold values from -0.125 to 0.125
- w_down: bfloat16 [6144, 2048], P('seq', 'dp'), may hold values from -0.078125 to 0.078125
- norm_attn: bfloat16 [2048], P('dp'), may hold values from 0.5 to 1.5
- norm_mlp: bfloat16 [2048], P('dp'), may hold values from 0.5 to 1.5
- norm_query: bfloat16 [128], P('dp'), may hold values from 1 to 2.5
- norm_key: bfloat16 [128], P('dp'), may hold values from 0.5 to 1.5
Outputs:
- layer_output: bfloat16 [8, 2048, 2048], P('dp', 'seq')
- grad_tokens: bfloat16 [8, 2048, 2048], P('dp', 'seq')
- grad_query: float32 [2048, 2048], P('dp', 'seq')
- grad_key: float32 [2048, 1024], P('dp', 'seq')
- grad_value: float32 [2048, 1024], P('dp', 'seq')
- grad_out: float32 [2048, 2048], P('seq', 'dp')
- grad_gate: float32 [2048, 6144], P('dp', 'seq')
- grad_up: float32 [2048, 6144], P('dp', 'seq')
- grad_down: float32 [6144, 2048], P('seq', 'dp')
- grad_norm_attn: float32 [2048], P('dp')
- grad_norm_mlp: float32 [2048], P('dp')
- grad_norm_query: float32 [128], P('dp')
- grad_norm_key: float32 [128], P('dp')
Inputs may be any that keep to these rules, and one draw needn't show every extreme that they name: lengths[s] real tokens stand at the start of slot s; positions from lengths[s] to 2047 are padding. Some slot is full and some other slot holds exactly 1024 tokens.
All inputs are finite; a program needn't handle non-finite values.
Results may differ from a plain program's by a relative error of at most 0.023.
Values may be sent and summed in bfloat16 or wider, within the bound.
No kernel may reach another device: no remote copies, remote signals or barrier semaphores. Data moves between devices by JAX's collectives and lax.ppermute only.
A program may use at most 448 MiB of HBM per device.

v0:
```python
import jax
import jax.numpy as jnp
from jax import lax
from jax.sharding import PartitionSpec as P

QUERY_HEADS = 16
KEY_VALUE_HEADS = 8
HEAD_SIZE = 128
SLOT_POSITIONS = 2048


EPS = 1e-06
BASE = 1000000.0
MASKED = -1e30


def for_sending(value):

    def short(part):
        return part.astype(jnp.bfloat16) if part.dtype == jnp.float32 else part

    return jax.tree.map(short, value)


def norm_rows(value_rows, gain):
    return (
        value_rows
        * lax.rsqrt(jnp.mean(value_rows * value_rows, axis=-1, keepdims=True) + EPS)
        * gain
    )


def rotate(value_rows, cosine, sine_table):
    half_dim = value_rows.shape[-1] // 2
    turned = jnp.concatenate([-value_rows[..., half_dim:], value_rows[..., :half_dim]], axis=-1)
    return value_rows * cosine + turned * sine_table


def angles(positions):
    frequency = BASE ** (-(jnp.arange(HEAD_SIZE // 2, dtype=jnp.float32) * 2.0 / HEAD_SIZE))
    phases = positions[:, None] * frequency[None, :]
    phases = jnp.concatenate([phases, phases], axis=-1)
    return (jnp.cos(phases)[:, None, :], jnp.sin(phases)[:, None, :])


def gating(gate_proj, up_proj):
    return gate_proj * jax.nn.sigmoid(gate_proj) * up_proj


def matrix_product(left, right):
    return jnp.dot(left, right, preferred_element_type=jnp.float32)


def left_product(left, right):
    return lax.dot_general(
        left, right, (((0,), (0,)), ((), ())), preferred_element_type=jnp.float32
    )


def right_product(left, right):
    return lax.dot_general(
        left, right, (((1,), (1,)), ((), ())), preferred_element_type=jnp.float32
    )


def masked_scores(query_block, keys_slot, row_start, length, key_count):
    block_rows = query_block.shape[0]
    scores = jnp.einsum(
        "qhgd,khd->hgqk", query_block, keys_slot, preferred_element_type=jnp.float32
    ) * HEAD_SIZE ** (-0.5)
    rows_at = row_start + jnp.arange(block_rows)
    cols_at = jnp.arange(key_count)
    allowed = (cols_at[None, :] <= rows_at[:, None]) & (cols_at[None, :] < length)
    return jnp.where(allowed, scores, MASKED)


def attend_block(query_block, keys_slot, values_slot, row_start, length, key_count):
    scores = masked_scores(query_block, keys_slot, row_start, length, key_count)
    top = jnp.max(scores, axis=-1, keepdims=True)
    raised = jnp.exp(scores - top)
    total = jnp.sum(raised, axis=-1, keepdims=True)
    attend = (raised / total).astype(jnp.bfloat16)
    context = jnp.einsum("hgqk,khd->qhgd", attend, values_slot, preferred_element_type=jnp.float32)
    return (context.astype(jnp.bfloat16), (top + jnp.log(total))[..., 0])


def attend_back(
    query_block, keys_slot, values_slot, grad_block, log_total, row_start, length, key_count
):
    scores = masked_scores(query_block, keys_slot, row_start, length, key_count)
    attend = jnp.exp(scores - log_total[..., None])
    grad_attend = jnp.einsum(
        "qhgd,khd->hgqk", grad_block, values_slot, preferred_element_type=jnp.float32
    )
    center = jnp.sum(attend * grad_attend, axis=-1, keepdims=True)
    grad_scores = (attend * (grad_attend - center)).astype(jnp.bfloat16)
    grad_query = jnp.einsum(
        "hgqk,khd->qhgd", grad_scores, keys_slot, preferred_element_type=jnp.float32
    ) * HEAD_SIZE ** (-0.5)
    grad_keys = jnp.einsum(
        "hgqk,qhgd->khd", grad_scores, query_block, preferred_element_type=jnp.float32
    ) * HEAD_SIZE ** (-0.5)
    grad_values = jnp.einsum(
        "hgqk,qhgd->khd",
        attend.astype(jnp.bfloat16),
        grad_block,
        preferred_element_type=jnp.float32,
    )
    return (grad_query, grad_keys, grad_values)


def on_device(
    tokens,
    lengths,
    cotangent,
    w_query,
    key_weight,
    value_weight,
    w_out,
    w_gate,
    w_up,
    w_down,
    norm_attn,
    norm_mlp,
    norm_query,
    norm_key,
):
    current_slots, sequence_rows, width = tokens.shape
    token_rows = current_slots * sequence_rows
    block_rows = min(512, SLOT_POSITIONS)
    num_blocks = SLOT_POSITIONS // block_rows
    seq_count = lax.axis_size("seq")
    shards = (
        lax.all_gather(w_query, "dp", axis=0, tiled=True),
        lax.all_gather(key_weight, "dp", axis=0, tiled=True),
        lax.all_gather(value_weight, "dp", axis=0, tiled=True),
        lax.all_gather(w_out, "dp", axis=1, tiled=True),
        lax.all_gather(w_gate, "dp", axis=0, tiled=True),
        lax.all_gather(w_up, "dp", axis=0, tiled=True),
        lax.all_gather(w_down, "dp", axis=1, tiled=True),
        lax.all_gather(norm_attn, "dp", axis=0, tiled=True),
        lax.all_gather(norm_mlp, "dp", axis=0, tiled=True),
        lax.all_gather(norm_query, "dp", axis=0, tiled=True),
        lax.all_gather(norm_key, "dp", axis=0, tiled=True),
    )
    part_gate, part_up, part_down = (shards[4], shards[5], shards[6])
    gain_attn = shards[7].astype(jnp.float32)
    gain_mlp = shards[8].astype(jnp.float32)
    gain_query = shards[9].astype(jnp.float32)
    gain_key = shards[10].astype(jnp.float32)
    full_query, full_key, whole_value, full_out = (
        lax.all_gather(shards[0], "seq", axis=1, tiled=True),
        lax.all_gather(shards[1], "seq", axis=1, tiled=True),
        lax.all_gather(shards[2], "seq", axis=1, tiled=True),
        lax.all_gather(shards[3], "seq", axis=0, tiled=True),
    )
    inputs = tokens.reshape(token_rows, width).astype(jnp.float32)
    normed_first, first_back = jax.vjp(norm_rows, inputs, gain_attn)
    attention_normed = normed_first.astype(jnp.bfloat16)
    query_raw = matrix_product(attention_normed, full_query)
    key_plain = matrix_product(attention_normed, full_key)
    value_send = (
        matrix_product(attention_normed, whole_value)
        .astype(jnp.bfloat16)
        .reshape(current_slots, sequence_rows, KEY_VALUE_HEADS, HEAD_SIZE)
    )
    place_int = lax.axis_index("seq") * sequence_rows + jnp.arange(sequence_rows, dtype=jnp.int32)
    cosine, sine_table = angles(place_int.astype(jnp.float32))
    valid_rows = (place_int[None, :] < lengths[:, None]).astype(jnp.float32).reshape(token_rows, 1)

    def head_prep(raw_proj, gain):
        return rotate(
            norm_rows(raw_proj.reshape(current_slots, sequence_rows, -1, HEAD_SIZE), gain),
            cosine,
            sine_table,
        )

    query_rot, query_back = jax.vjp(head_prep, query_raw, gain_query)
    key_rot, key_back = jax.vjp(head_prep, key_plain, gain_key)
    query_heads, key_heads, value_heads = (
        lax.all_to_all(
            query_rot.astype(jnp.bfloat16), "seq", split_axis=2, concat_axis=1, tiled=True
        ),
        lax.all_to_all(
            key_rot.astype(jnp.bfloat16), "seq", split_axis=2, concat_axis=1, tiled=True
        ),
        lax.all_to_all(value_send, "seq", split_axis=2, concat_axis=1, tiled=True),
    )
    kv_local = key_heads.shape[2]
    groups = query_heads.shape[2] // kv_local
    query_heads = query_heads.reshape(current_slots, SLOT_POSITIONS, kv_local, groups, HEAD_SIZE)

    def forward_slot(slot_item):
        query_slot, keys_slot, values_slot, length = slot_item
        contexts = []
        totals = []
        for block_index in range(num_blocks):
            row_start = block_index * block_rows
            query_block = query_slot[row_start : row_start + block_rows]
            context, log_total = attend_block(
                query_block, keys_slot, values_slot, row_start, length, SLOT_POSITIONS
            )
            contexts.append(context)
            totals.append(log_total)
        return (jnp.concatenate(contexts, axis=0), jnp.concatenate(totals, axis=-1))

    context_heads, total_heads = lax.map(
        forward_slot, (query_heads, key_heads, value_heads, lengths)
    )
    context_heads = context_heads.reshape(
        current_slots, SLOT_POSITIONS, kv_local * groups, HEAD_SIZE
    )
    context_tok = (
        lax.all_to_all(for_sending(context_heads), "seq", split_axis=1, concat_axis=2, tiled=True)
        .astype(context_heads.dtype)
        .reshape(token_rows, QUERY_HEADS * HEAD_SIZE)
    )
    resid = inputs + matrix_product(context_tok, full_out)
    normed_second, second_back = jax.vjp(norm_rows, resid, gain_mlp)
    normed_mlp = normed_second.astype(jnp.bfloat16)
    grad_rows = cotangent.reshape(token_rows, width).astype(jnp.float32) * valid_rows
    grad_rows_low = grad_rows.astype(jnp.bfloat16)
    full_gate, full_up, full_down = (
        lax.all_gather(part_gate, "seq", axis=1, tiled=True),
        lax.all_gather(part_up, "seq", axis=1, tiled=True),
        lax.all_gather(part_down, "seq", axis=0, tiled=True),
    )
    gate_proj = matrix_product(normed_mlp, full_gate)
    up_proj = matrix_product(normed_mlp, full_up)
    hidden_full, gating_back = jax.vjp(gating, gate_proj, up_proj)
    hidden = hidden_full.astype(jnp.bfloat16)
    mlp_out = matrix_product(hidden, full_down)
    layer_output = (
        (valid_rows * (resid + mlp_out))
        .astype(jnp.bfloat16)
        .reshape(current_slots, sequence_rows, width)
    )
    grad_hidden = right_product(grad_rows_low, full_down)
    grad_gate_full, grad_up_full = gating_back(grad_hidden)
    grad_gate_low = grad_gate_full.astype(jnp.bfloat16)
    grad_up_low = grad_up_full.astype(jnp.bfloat16)
    grad_normed_mlp = right_product(grad_gate_low, full_gate) + right_product(grad_up_low, full_up)
    grad_gate_part, grad_up_part, grad_down_part = (
        lax.psum_scatter(
            left_product(normed_mlp, grad_gate_low).astype(jnp.bfloat16),
            "seq",
            scatter_dimension=1,
            tiled=True,
        ).astype(jnp.float32),
        lax.psum_scatter(
            left_product(normed_mlp, grad_up_low).astype(jnp.bfloat16),
            "seq",
            scatter_dimension=1,
            tiled=True,
        ).astype(jnp.float32),
        lax.psum_scatter(
            left_product(hidden, grad_rows_low).astype(jnp.bfloat16),
            "seq",
            scatter_dimension=0,
            tiled=True,
        ).astype(jnp.float32),
    )
    grad_resid_norm, gain_mlp_term = second_back(grad_normed_mlp)
    grad_resid = grad_rows + grad_resid_norm
    grad_attn_low = grad_resid.astype(jnp.bfloat16)
    grad_out_whole = left_product(context_tok, grad_attn_low)
    grad_context = (
        right_product(grad_attn_low, full_out)
        .astype(jnp.bfloat16)
        .reshape(current_slots, sequence_rows, QUERY_HEADS, HEAD_SIZE)
    )
    grad_heads = lax.all_to_all(grad_context, "seq", split_axis=2, concat_axis=1, tiled=True)
    grad_heads = grad_heads.reshape(current_slots, SLOT_POSITIONS, kv_local, groups, HEAD_SIZE)

    def backward_slot(slot_item):
        query_slot, keys_slot, values_slot, grad_slot, total_slot, length = slot_item
        grad_keys = jnp.zeros((SLOT_POSITIONS, kv_local, HEAD_SIZE), jnp.float32)
        grad_values = jnp.zeros((SLOT_POSITIONS, kv_local, HEAD_SIZE), jnp.float32)
        grad_queries = []
        for block_index in range(num_blocks):
            row_start = block_index * block_rows
            query_block = query_slot[row_start : row_start + block_rows]
            grad_block = grad_slot[row_start : row_start + block_rows]
            log_total = total_slot[..., row_start : row_start + block_rows]
            key_count = SLOT_POSITIONS
            grad_query, key_part, value_part = attend_back(
                query_block,
                keys_slot,
                values_slot,
                grad_block,
                log_total,
                row_start,
                length,
                key_count,
            )
            grad_queries.append(grad_query.astype(jnp.bfloat16))
            grad_keys = grad_keys.at[:key_count].add(key_part)
            grad_values = grad_values.at[:key_count].add(value_part)
        grad_query_slot = jnp.concatenate(grad_queries, axis=0).reshape(
            SLOT_POSITIONS, kv_local * groups, HEAD_SIZE
        )
        return (grad_query_slot, grad_keys.astype(jnp.bfloat16), grad_values.astype(jnp.bfloat16))

    grad_query_heads, grad_key_heads, grad_value_heads = lax.map(
        backward_slot, (query_heads, key_heads, value_heads, grad_heads, total_heads, lengths)
    )
    grad_query_tok, grad_key_tok, value_gradient_token = (
        lax.all_to_all(
            for_sending(grad_query_heads), "seq", split_axis=1, concat_axis=2, tiled=True
        ).astype(grad_query_heads.dtype),
        lax.all_to_all(grad_key_heads, "seq", split_axis=1, concat_axis=2, tiled=True),
        lax.all_to_all(grad_value_heads, "seq", split_axis=1, concat_axis=2, tiled=True),
    )
    grad_query_full, gain_query_term = query_back(grad_query_tok.astype(jnp.float32))
    grad_key_full, gain_key_term = key_back(grad_key_tok.astype(jnp.float32))
    grad_query_raw = grad_query_full.astype(jnp.bfloat16)
    grad_key_raw = grad_key_full.astype(jnp.bfloat16)
    value_gradient_plain = value_gradient_token.reshape(token_rows, KEY_VALUE_HEADS * HEAD_SIZE)
    grad_normed_attn = (
        right_product(grad_query_raw, full_query)
        + right_product(grad_key_raw, full_key)
        + right_product(value_gradient_plain, whole_value)
    )
    grad_input_norm, gain_attn_term = first_back(grad_normed_attn)
    grad_tokens = (
        (grad_resid + grad_input_norm)
        .astype(jnp.bfloat16)
        .reshape(current_slots, sequence_rows, width)
    )

    def copies(term):
        return jnp.broadcast_to(term[None, :], (seq_count, term.shape[0]))

    seq_sums = (
        lax.psum_scatter(
            left_product(attention_normed, grad_query_raw).astype(jnp.bfloat16),
            "seq",
            scatter_dimension=1,
            tiled=True,
        ).astype(jnp.float32),
        lax.psum_scatter(
            left_product(attention_normed, grad_key_raw).astype(jnp.bfloat16),
            "seq",
            scatter_dimension=1,
            tiled=True,
        ).astype(jnp.float32),
        lax.psum_scatter(
            left_product(attention_normed, value_gradient_plain).astype(jnp.bfloat16),
            "seq",
            scatter_dimension=1,
            tiled=True,
        ).astype(jnp.float32),
        lax.psum_scatter(
            grad_out_whole.astype(jnp.bfloat16), "seq", scatter_dimension=0, tiled=True
        ).astype(jnp.float32),
        lax.psum_scatter(
            copies(gain_attn_term).astype(jnp.bfloat16), "seq", scatter_dimension=0, tiled=True
        ).astype(jnp.float32),
        lax.psum_scatter(
            copies(gain_mlp_term).astype(jnp.bfloat16), "seq", scatter_dimension=0, tiled=True
        ).astype(jnp.float32),
        lax.psum_scatter(
            copies(gain_query_term).astype(jnp.bfloat16), "seq", scatter_dimension=0, tiled=True
        ).astype(jnp.float32),
        lax.psum_scatter(
            copies(gain_key_term).astype(jnp.bfloat16), "seq", scatter_dimension=0, tiled=True
        ).astype(jnp.float32),
    )
    owned = (
        lax.psum_scatter(
            seq_sums[0].astype(jnp.bfloat16), "dp", scatter_dimension=0, tiled=True
        ).astype(jnp.float32),
        lax.psum_scatter(
            seq_sums[1].astype(jnp.bfloat16), "dp", scatter_dimension=0, tiled=True
        ).astype(jnp.float32),
        lax.psum_scatter(
            seq_sums[2].astype(jnp.bfloat16), "dp", scatter_dimension=0, tiled=True
        ).astype(jnp.float32),
        lax.psum_scatter(
            seq_sums[3].astype(jnp.bfloat16), "dp", scatter_dimension=1, tiled=True
        ).astype(jnp.float32),
        lax.psum_scatter(
            grad_gate_part.astype(jnp.bfloat16), "dp", scatter_dimension=0, tiled=True
        ).astype(jnp.float32),
        lax.psum_scatter(
            grad_up_part.astype(jnp.bfloat16), "dp", scatter_dimension=0, tiled=True
        ).astype(jnp.float32),
        lax.psum_scatter(
            grad_down_part.astype(jnp.bfloat16), "dp", scatter_dimension=1, tiled=True
        ).astype(jnp.float32),
        lax.psum_scatter(
            seq_sums[4][0].astype(jnp.bfloat16), "dp", scatter_dimension=0, tiled=True
        ).astype(jnp.float32),
        lax.psum_scatter(
            seq_sums[5][0].astype(jnp.bfloat16), "dp", scatter_dimension=0, tiled=True
        ).astype(jnp.float32),
        lax.psum_scatter(
            seq_sums[6][0].astype(jnp.bfloat16), "dp", scatter_dimension=0, tiled=True
        ).astype(jnp.float32),
        lax.psum_scatter(
            seq_sums[7][0].astype(jnp.bfloat16), "dp", scatter_dimension=0, tiled=True
        ).astype(jnp.float32),
    )
    return (
        layer_output,
        grad_tokens,
        owned[0],
        owned[1],
        owned[2],
        owned[3],
        owned[4],
        owned[5],
        owned[6],
        owned[7],
        owned[8],
        owned[9],
        owned[10],
    )


def solution(mesh):
    return jax.shard_map(
        on_device,
        mesh=mesh,
        in_specs=(
            P("dp", "seq", None),
            P("dp"),
            P("dp", "seq", None),
            P("dp", "seq"),
            P("dp", "seq"),
            P("dp", "seq"),
            P("seq", "dp"),
            P("dp", "seq"),
            P("dp", "seq"),
            P("seq", "dp"),
            P("dp"),
            P("dp"),
            P("dp"),
            P("dp"),
        ),
        out_specs=(
            P("dp", "seq", None),
            P("dp", "seq", None),
            P("dp", "seq"),
            P("dp", "seq"),
            P("dp", "seq"),
            P("seq", "dp"),
            P("dp", "seq"),
            P("dp", "seq"),
            P("seq", "dp"),
            P("dp"),
            P("dp"),
            P("dp"),
            P("dp"),
        ),
        check_vma=False,
    )
```

profile of v0, /device:TPU:0, one launch (start us, length us, event | category | flops | bytes accessed | tf_op | source)
XLA Modules:
  0.0 4567.8 jit_solution(14176295945565498645)
XLA Ops:
  121.4 47.2 %all-gather.37.cloned.1.call-done = bf16[2048,1536]{1,0:T(8,128)(2,1)} async-done(((bf16[256,1536]{1,0:T(8,128)(2,1)}), bf16[2048,1536]{1,0:T(8,128)(2,1)}) %all-gather.37.cloned.1.call-update) | async-done | bytes 6291472 | tf_op jit(solution)/shard_map/all_gather | solution.py:139
  168.7 47.2 %all-gather.33.cloned.1.call-done = bf16[2048,1536]{1,0:T(8,128)(2,1)} async-done(((bf16[256,1536]{1,0:T(8,128)(2,1)}), bf16[2048,1536]{1,0:T(8,128)(2,1)}) %all-gather.33.cloned.1.call-update) | async-done | bytes 6291472 | tf_op jit(solution)/shard_map/all_gather | solution.py:138
  216.0 48.4 %all-gather.41.cloned.1.call-done = bf16[1536,2048]{1,0:T(8,128)(2,1)} async-done(((bf16[1536,256]{1,0:T(8,128)(2,1)}), bf16[1536,2048]{1,0:T(8,128)(2,1)}) %all-gather.41.cloned.1.call-update) | async-done | bytes 6291472 | tf_op jit(solution)/shard_map/all_gather | solution.py:140
  289.9 56.7 %all-gather.19.cloned.1.call-done = bf16[2048,1024]{1,0:T(8,128)(2,1)} async-done(((bf16[2048,256]{1,0:T(8,128)(2,1)}), bf16[2048,1024]{1,0:T(8,128)(2,1)}) %all-gather.19.cloned.1.call-update) | async-done | bytes 4194320 | tf_op jit(solution)/shard_map/all_gather | solution.py:154
  357.1 93.7 %all-gather.23.cloned.1.call-done = bf16[2048,1024]{1,0:T(8,128)(2,1)} async-done(((bf16[2048,256]{1,0:T(8,128)(2,1)}), bf16[2048,1024]{1,0:T(8,128)(2,1)}) %all-gather.23.cloned.1.call-update) | async-done | bytes 4194320 | tf_op jit(solution)/shard_map/all_gather | solution.py:153
  464.5 137.3 %all-gather.27.cloned.1.call-done = bf16[2048,2048]{1,0:T(8,128)(2,1)} async-done(((bf16[2048,512]{1,0:T(8,128)(2,1)}), bf16[2048,2048]{1,0:T(8,128)(2,1)}) %all-gather.27.cloned.1.call-update) | async-done | bytes 8388624 | tf_op jit(solution)/shard_map/all_gather | solution.py:152
  634.9 37.1 all-to-all-done.1
  685.8 92.9 %all-to-all-done.2 = bf16[1,512,16,128]{3,1,0,2:T(8,128)(2,1)S(1)} async-done(((bf16[1,512,16,128]{3,1,0,2:T(8,128)(2,1)}), bf16[1,512,16,128]{3,1,0,2:T(8,128)(2,1)S(1)}, u32[]{:S(2)}, u32[]{:S(2)}) %all-to-all-start.2) | async-done | bytes 2097184 | tf_op jit(solution)/shard_map/all_to_all | solution.py:181
  895.5 95.0 %all-to-all-done.3 = bf16[1,2048,4,128]{3,2,0,1:T(4,128)(2,1)} async-done(((bf16[1,2048,4,128]{3,2,0,1:T(4,128)(2,1)}), bf16[1,2048,4,128]{3,2,0,1:T(4,128)(2,1)}, u32[]{:S(2)}, u32[]{:S(2)}) %all-to-all-start.3) | async-done | bytes 2097184 | tf_op jit(solution)/shard_map/all_to_all | solution.py:214
  1008.0 280.0 %all-gather.39.cloned.1.call-done = bf16[2048,6144]{1,0:T(8,128)(2,1)} async-done(((bf16[2048,1536]{1,0:T(8,128)(2,1)}), bf16[2048,6144]{1,0:T(8,128)(2,1)}) %all-gather.39.cloned.1.call-update) | async-done | bytes 25165840 | tf_op jit(solution)/shard_map/all_gather | solution.py:225
  1308.6 404.2 %all-gather.35.cloned.1.call-done = bf16[2048,6144]{1,0:T(8,128)(2,1)} async-done(((bf16[2048,1536]{1,0:T(8,128)(2,1)}), bf16[2048,6144]{1,0:T(8,128)(2,1)}) %all-gather.35.cloned.1.call-update) | async-done | bytes 25165840 | tf_op jit(solution)/shard_map/all_gather | solution.py:224
  1733.6 404.1 %all-gather.43.cloned.1.call-done = bf16[6144,2048]{1,0:T(8,128)(2,1)} async-done(((bf16[1536,2048]{1,0:T(8,128)(2,1)}), bf16[6144,2048]{1,0:T(8,128)(2,1)}) %all-gather.43.cloned.1.call-update) | async-done | bytes 25165840 | tf_op jit(solution)/shard_map/all_gather | solution.py:226
  2231.0 46.6 %all-to-all-done.4 = bf16[1,512,16,128]{3,1,0,2:T(8,128)(2,1)} async-done(((bf16[1,512,16,128]{3,1,0,2:T(8,128)(2,1)}), bf16[1,512,16,128]{3,1,0,2:T(8,128)(2,1)}, u32[]{:S(2)}, u32[]{:S(2)}) %all-to-all-start.4) | async-done | bytes 2097184 | tf_op jit(solution)/shard_map/all_to_all | solution.py:272
  2467.6 49.0 %all_to_all.108 = bf16[1,2048,2,128]{3,2,0,1:T(2,128)(2,1)S(1)} all-to-all(bf16[1,2048,2,128]{3,2,0,1:T(2,128)(2,1)S(1)} %copy.409), channel_id=1, replica_groups=mesh['dp'=8,'seq'=4] {'seq'}, dimensions={1} | all-to-all | bytes 2097152 | tf_op jit(solution)/shard_map/all_to_all | solution.py:311
  2559.1 88.7 %all_to_all.109 = bf16[1,2048,4,128]{3,2,0,1:T(4,128)(2,1)} all-to-all(bf16[1,2048,4,128]{3,2,0,1:T(4,128)(2,1)} %copy.397), channel_id=1, replica_groups=mesh['dp'=8,'seq'=4] {'seq'}, dimensions={1} | all-to-all | bytes 4194304 | tf_op jit(solution)/shard_map/all_to_all | solution.py:308
  2736.9 52.7 %reduce-scatter.27.cloned.1.call-done = bf16[512,2048]{1,0:T(8,128)(2,1)} async-done(((bf16[2048,2048]{1,0:T(8,128)(2,1)}), bf16[512,2048]{1,0:T(8,128)(2,1)}) %reduce-scatter.27.cloned.1.call-update) | async-done | bytes 2097168 | tf_op jit(solution)/shard_map/reduce_scatter | solution.py:353
  2789.7 147.4 %reduce-scatter.15.cloned.1.call-done = bf16[2048,512]{1,0:T(8,128)(2,1)} async-done(((bf16[2048,2048]{1,0:T(8,128)(2,1)}), bf16[2048,512]{1,0:T(8,128)(2,1)}) %reduce-scatter.15.cloned.1.call-update) | async-done | bytes 2097168 | tf_op jit(solution)/shard_map/reduce_scatter | solution.py:335
  2937.2 417.4 %reduce-scatter.39.cloned.1.call-done = bf16[1536,2048]{1,0:T(8,128)(2,1)} async-done(((bf16[6144,2048]{1,0:T(8,128)(2,1)}), bf16[1536,2048]{1,0:T(8,128)(2,1)}) %reduce-scatter.39.cloned.1.call-update) | async-done | bytes 6291472 | tf_op jit(solution)/shard_map/reduce_scatter | solution.py:256
  3354.6 418.5 %reduce-scatter.35.cloned.1.call-done = bf16[2048,1536]{1,0:T(8,128)(2,1)} async-done(((bf16[2048,6144]{1,0:T(8,128)(2,1)}), bf16[2048,1536]{1,0:T(8,128)(2,1)}) %reduce-scatter.35.cloned.1.call-update) | async-done | bytes 6291472 | tf_op jit(solution)/shard_map/reduce_scatter | solution.py:250
  3773.4 418.3 %reduce-scatter.31.cloned.1.call-done = bf16[2048,1536]{1,0:T(8,128)(2,1)} async-done(((bf16[2048,6144]{1,0:T(8,128)(2,1)}), bf16[2048,1536]{1,0:T(8,128)(2,1)}) %reduce-scatter.31.cloned.1.call-update) | async-done | bytes 6291472 | tf_op jit(solution)/shard_map/reduce_scatter | solution.py:244
  4319.5 42.7 reduce-scatter.17.cloned.1.call-done
  4364.1 63.6 %reduce-scatter.41.cloned.1.call-done = bf16[1536,256]{1,0:T(8,128)(2,1)} async-done(((bf16[1536,2048]{1,0:T(8,128)(2,1)}), bf16[1536,256]{1,0:T(8,128)(2,1)}) %reduce-scatter.41.cloned.1.call-update) | async-done | bytes 786448 | tf_op jit(solution)/shard_map/reduce_scatter | solution.py:388
  4430.1 62.6 %reduce-scatter.37.cloned.1.call-done = bf16[256,1536]{1,0:T(8,128)(2,1)} async-done(((bf16[2048,1536]{1,0:T(8,128)(2,1)}), bf16[256,1536]{1,0:T(8,128)(2,1)}) %reduce-scatter.37.cloned.1.call-update) | async-done | bytes 786448 | tf_op jit(solution)/shard_map/reduce_scatter | solution.py:385
  4495.1 63.1 %reduce-scatter.33.cloned.1.call-done = bf16[256,1536]{1,0:T(8,128)(2,1)} async-done(((bf16[2048,1536]{1,0:T(8,128)(2,1)}), bf16[256,1536]{1,0:T(8,128)(2,1)}) %reduce-scatter.33.cloned.1.call-update) | async-done | bytes 786448 | tf_op jit(solution)/shard_map/reduce_scatter | solution.py:382
  (486 shorter events, 934.2 us)
Async XLA Ops:
  10.6 205.3 %all-gather.33.cloned.1.call-start = ((), (), s32[]{:S(2)}) async-start(), calls=%async_computation.30 | async-start | bytes 7077888 | tf_op jit(solution)/shard_map/all_gather | solution.py:138
  11.1 253.3 %all-gather.41.cloned.1.call-start = ((), (), s32[]{:S(2)}) async-start(), calls=%async_computation.34 | async-start | bytes 7077888 | tf_op jit(solution)/shard_map/all_gather | solution.py:140
  11.9 334.7 %all-gather.19.cloned.1.call-start = ((), (), s32[]{:S(2)}) async-start(), calls=%async_computation.23 | async-start | bytes 5242880 | tf_op jit(solution)/shard_map/all_gather | solution.py:154
  36.2 414.7 %all-gather.23.cloned.1.call-start = ((), (), s32[]{:S(2)}) async-start(), calls=%async_computation.25 | async-start | bytes 5242880 | tf_op jit(solution)/shard_map/all_gather | solution.py:153
  61.6 540.3 %all-gather.27.cloned.1.call-start = ((), (), s32[]{:S(2)}) async-start(), calls=%async_computation.27 | async-start | bytes 10485760 | tf_op jit(solution)/shard_map/all_gather | solution.py:152
  91.4 906.4 %all-gather.31.cloned.1.call-start = ((), (), s32[]{:S(2)}) async-start(), calls=%async_computation.29 | async-start | bytes 10485760 | tf_op jit(solution)/shard_map/all_gather | solution.py:155
  121.3 1166.6 %all-gather.39.cloned.1.call-start = ((), (), s32[]{:S(2)}) async-start(), calls=%async_computation.33 | async-start | bytes 31457280 | tf_op jit(solution)/shard_map/all_gather | solution.py:225
  168.6 1544.2 %all-gather.35.cloned.1.call-start = ((), (), s32[]{:S(2)}) async-start(), calls=%async_computation.31 | async-start | bytes 31457280 | tf_op jit(solution)/shard_map/all_gather | solution.py:224
  216.0 1921.7 %all-gather.43.cloned.1.call-start = ((), (), s32[]{:S(2)}) async-start(), calls=%async_computation.35 | async-start | bytes 31457280 | tf_op jit(solution)/shard_map/all_gather | solution.py:226
  352.6 259.7 %all-to-all-start = ((bf16[1,512,8,128]{3,1,0,2:T(8,128)(2,1)}), bf16[1,512,8,128]{3,1,0,2:T(8,128)(2,1)}, u32[]{:S(2)}, u32[]{:S(2)}) async-start(bf16[1,512,8,128]{3,1,0,2:T(8,128)(2,1)} %copy.368), calls=%async_computation | async-start | bytes 2097152 | tf_op jit(solution)/shard_map/all_to_all | solution.py:187
  2357.3 378.2 %reduce-scatter.23.cloned.1.call-start = ((), (), s32[]{:S(2)}) async-start(), calls=%async_computation.40 | async-start | bytes 5242880 | tf_op jit(solution)/shard_map/reduce_scatter | solution.py:347
  2416.4 319.8 %reduce-scatter.19.cloned.1.call-start = ((), (), s32[]{:S(2)}) async-start(), calls=%async_computation.38 | async-start | bytes 5242880 | tf_op jit(solution)/shard_map/reduce_scatter | solution.py:341
  2527.2 262.4 %reduce-scatter.27.cloned.1.call-start = ((), (), s32[]{:S(2)}) async-start(), calls=%async_computation.42 | async-start | bytes 10485760 | tf_op jit(solution)/shard_map/reduce_scatter | solution.py:353
  2538.3 398.8 %reduce-scatter.15.cloned.1.call-start = ((), (), s32[]{:S(2)}) async-start(), calls=%async_computation.36 | async-start | bytes 10485760 | tf_op jit(solution)/shard_map/reduce_scatter | solution.py:335
  2671.8 682.7 %reduce-scatter.39.cloned.1.call-start = ((), (), s32[]{:S(2)}) async-start(), calls=%async_computation.48 | async-start | bytes 31457280 | tf_op jit(solution)/shard_map/reduce_scatter | solution.py:256
  2693.3 1079.8 %reduce-scatter.35.cloned.1.call-start = ((), (), s32[]{:S(2)}) async-start(), calls=%async_computation.46 | async-start | bytes 31457280 | tf_op jit(solution)/shard_map/reduce_scatter | solution.py:250
  2714.3 1477.5 %reduce-scatter.31.cloned.1.call-start = ((), (), s32[]{:S(2)}) async-start(), calls=%async_computation.44 | async-start | bytes 31457280 | tf_op jit(solution)/shard_map/reduce_scatter | solution.py:244
  2735.4 1543.7 %reduce-scatter.25.cloned.1.call-start = ((), (), s32[]{:S(2)}) async-start(), calls=%async_computation.41 | async-start | bytes 1179648 | tf_op jit(solution)/shard_map/reduce_scatter | solution.py:376
  2736.1 1544.5 %reduce-scatter.21.cloned.1.call-start = ((), (), s32[]{:S(2)}) async-start(), calls=%async_computation.39 | async-start | bytes 1179648 | tf_op jit(solution)/shard_map/reduce_scatter | solution.py:373
  2736.9 1580.9 %reduce-scatter.29.cloned.1.call-start = ((), (), s32[]{:S(2)}) async-start(), calls=%async_computation.43 | async-start | bytes 2359296 | tf_op jit(solution)/shard_map/reduce_scatter | solution.py:379
  2789.6 1572.6 %reduce-scatter.17.cloned.1.call-start = ((), (), s32[]{:S(2)}) async-start(), calls=%async_computation.37 | async-start | bytes 2359296 | tf_op jit(solution)/shard_map/reduce_scatter | solution.py:370
  2937.1 1490.5 %reduce-scatter.41.cloned.1.call-start = ((), (), s32[]{:S(2)}) async-start(), calls=%async_computation.49 | async-start | bytes 7077888 | tf_op jit(solution)/shard_map/reduce_scatter | solution.py:388
  3354.6 1138.1 %reduce-scatter.37.cloned.1.call-start = ((), (), s32[]{:S(2)}) async-start(), calls=%async_computation.47 | async-start | bytes 7077888 | tf_op jit(solution)/shard_map/reduce_scatter | solution.py:385
  3773.2 785.0 %reduce-scatter.33.cloned.1.call-start = ((), (), s32[]{:S(2)}) async-start(), calls=%async_computation.45 | async-start | bytes 7077888 | tf_op jit(solution)/shard_map/reduce_scatter | solution.py:382
  (133 other events, 7025.4 us)
Sparse Core Ops, SparseCore 0:
  123.0 45.5 all-gather.36
  170.3 45.5 all-gather.32
  217.8 46.6 all-gather.40
  266.0 80.5 all-gather.18
  348.2 102.5 all-gather.22
  452.2 149.5 all-gather.26
  603.4 214.8 all-gather.30
  819.7 468.1 all-gather.38
  1289.5 423.2 all-gather.34
  1714.3 423.3 all-gather.42
  2416.6 93.8 reduce-scatter.22
  2527.4 107.9 reduce-scatter.18
  2637.5 152.0 reduce-scatter.26
  2791.8 145.2 reduce-scatter.14
  2939.4 415.0 reduce-scatter.38
  3356.9 416.1 reduce-scatter.34
  3775.5 416.1 reduce-scatter.30
  4195.2 37.8 reduce-scatter.24
  4236.6 36.4 reduce-scatter.20
  4276.6 41.1 reduce-scatter.28
  4321.0 41.1 reduce-scatter.16
  4365.9 61.7 reduce-scatter.40
  4430.9 61.7 reduce-scatter.36
  4496.4 61.7 reduce-scatter.32
  (4 shorter events, 105.5 us)
where the time goes:
time: 4570 us
  waiting for transfers between devices  3630 us (79%)
  matrix products  464 us (10%)
  blocking collectives  201 us (4%)
  other arithmetic  139 us (3%)
  local copies, waits for them, and re-layouts  84.7 us (2%)
    reduce_scatter x1, waiting for transfers between devices, on_device(): lax.psum_scatter(left_product(normed_mlp, grad_up_low).astype(jnp.bfloat1...  418 us
    reduce_scatter x1, waiting for transfers between devices, on_device(): lax.psum_scatter(left_product(normed_mlp, grad_gate_low).astype(jnp.bfloa...  418 us
    reduce_scatter x1, waiting for transfers between devices, on_device(): lax.psum_scatter(left_product(hidden, grad_rows_low).astype(jnp.bfloat16)...  417 us
    all_gather x1, waiting for transfers between devices, on_device(): lax.all_gather(part_gate, 'seq', axis=1, tiled=True)  404 us
    all_gather x1, waiting for transfers between devices, on_device(): lax.all_gather(part_down, 'seq', axis=0, tiled=True)  404 us
    all_gather x1, waiting for transfers between devices, on_device(): lax.all_gather(part_up, 'seq', axis=1, tiled=True)  280 us
    reduce_scatter x1, waiting for transfers between devices, on_device(): lax.psum_scatter(left_product(attention_normed, grad_query_raw).astype(jn...  147 us
    all_gather x1, waiting for transfers between devices, on_device(): lax.all_gather(shards[0], 'seq', axis=1, tiled=True)  137 us
  transfers between devices with their start and end apart: 34, of which 27 were waited for; matrix products, arithmetic and copies ran while one was open for 11% of the time, Pallas kernels for 0%

commit v1 on v0

v1 whole, which is shorter than its diff:
```python
import functools
import math

import jax
import jax.numpy as jnp
from jax import lax
from jax.experimental import pallas as pl
from jax.experimental.pallas import tpu as pltpu
from jax.sharding import PartitionSpec as P

HEAD_SIZE = 128
EPS = 1e-06
BASE = 1000000.0
MASKED = -1e30
QUERY_SCALE = HEAD_SIZE**-0.5 * math.log2(math.e)
PAIR = 2


def norm_rows(value_rows, gain):
    return (
        value_rows
        * lax.rsqrt(jnp.mean(value_rows * value_rows, axis=-1, keepdims=True) + EPS)
        * gain
    )


def rotate(value_rows, cosine, sine_table):
    half_dim = value_rows.shape[-1] // 2
    turned = jnp.concatenate([-value_rows[..., half_dim:], value_rows[..., :half_dim]], axis=-1)
    return value_rows * cosine + turned * sine_table


def angles(positions):
    frequency = BASE ** (-(jnp.arange(HEAD_SIZE // 2, dtype=jnp.float32) * 2.0 / HEAD_SIZE))
    phases = positions[:, None] * frequency[None, :]
    cosine, sine_table = jnp.cos(phases), jnp.sin(phases)
    return (
        jnp.concatenate([cosine, cosine], axis=-1)[:, None, :],
        jnp.concatenate([sine_table, sine_table], axis=-1)[:, None, :],
    )


def gating(gate_proj, up_proj):
    return gate_proj * jax.nn.sigmoid(gate_proj) * up_proj


def nn(left, right):
    return lax.dot_general(
        left, right, (((1,), (0,)), ((), ())), preferred_element_type=jnp.float32
    )


def nt(left, right):
    return lax.dot_general(
        left, right, (((1,), (1,)), ((), ())), preferred_element_type=jnp.float32
    )


def tn(left, right):
    return lax.dot_general(
        left, right, (((0,), (0,)), ((), ())), preferred_element_type=jnp.float32
    )


def forward_kernel(
    block, groups, length_ref, query_ref, key_ref, value_ref, out_ref, total_ref, wide_ref
):
    at_query = pl.program_id(1)
    length = length_ref[0]
    size = HEAD_SIZE

    @pl.when(at_query == 0)
    def _():
        wide_ref[:, :size] = value_ref[...]
        wide_ref[:, size:] = jnp.ones_like(value_ref)

    whole = jnp.minimum(at_query, length // block)
    some = jnp.minimum(at_query + 1, (length + block - 1) // block)
    queries = [query_ref[:, g * size : (g + 1) * size] for g in range(groups)]

    def step(at_key, sums, masked):
        start = pl.multiple_of(at_key * block, block)
        keys = key_ref[pl.ds(start, block), :]
        wide = wide_ref[pl.ds(start, block), :]
        if masked:
            rows = at_query * block + lax.broadcasted_iota(jnp.int32, (block, block), 0)
            cols = start + lax.broadcasted_iota(jnp.int32, (block, block), 1)
            allowed = (cols <= rows) & (cols < length)
        after = []
        for g in range(groups):
            scores = nt(queries[g], keys)
            if masked:
                scores = jnp.where(allowed, scores, MASKED)
            after.append(sums[g] + nn(jnp.exp2(scores).astype(jnp.bfloat16), wide))
        return tuple(after)

    sums = tuple(jnp.zeros((block, 2 * size), jnp.float32) for _ in range(groups))
    sums = lax.fori_loop(0, whole, lambda j, c: step(j, c, False), sums)
    sums = lax.fori_loop(whole, some, lambda j, c: step(j, c, True), sums)
    for g in range(groups):
        total = sums[g][:, size:]
        out_ref[:, g * size : (g + 1) * size] = (sums[g][:, :size] / total).astype(out_ref.dtype)
        total_ref[g, :, :] = jnp.transpose(jnp.log2(total))[:8, :]


def attend_forward(queries, keys, values, lengths, block=512):
    positions, width = queries.shape
    kv_count = keys.shape[1] // HEAD_SIZE
    groups = width // keys.shape[1]
    size = HEAD_SIZE
    return pl.pallas_call(
        functools.partial(forward_kernel, block, groups),
        grid_spec=pltpu.PrefetchScalarGridSpec(
            num_scalar_prefetch=1,
            grid=(kv_count, positions // block),
            in_specs=[
                pl.BlockSpec((block, groups * size), lambda h, i, s: (i, h)),
                pl.BlockSpec((positions, size), lambda h, i, s: (0, h)),
                pl.BlockSpec((positions, size), lambda h, i, s: (0, h)),
            ],
            out_specs=[
                pl.BlockSpec((block, groups * size), lambda h, i, s: (i, h)),
                pl.BlockSpec((groups, 8, block), lambda h, i, s: (h, 0, i)),
            ],
            scratch_shapes=[pltpu.VMEM((positions, 2 * size), jnp.bfloat16)],
        ),
        out_shape=(
            jax.ShapeDtypeStruct((positions, width), jnp.bfloat16),
            jax.ShapeDtypeStruct((kv_count * groups, 8, positions), jnp.float32),
        ),
        compiler_params=pltpu.CompilerParams(
            dimension_semantics=("arbitrary", "arbitrary"), vmem_limit_bytes=48 << 20
        ),
        cost_estimate=pl.CostEstimate(
            flops=4 * positions * positions * width,
            bytes_accessed=8 * positions * width,
            transcendentals=positions * positions * width // size // 2,
        ),
        name="attend_forward",
    )(lengths, queries, keys, values)


def backward_kernel(
    block,
    groups,
    positions,
    length_ref,
    query_ref,
    key_ref,
    value_ref,
    grad_ref,
    out_ref,
    total_ref,
    grad_query_ref,
    grad_key_ref,
    grad_value_ref,
    sums_ref,
    center_ref,
):
    length = length_ref[0]
    size = HEAD_SIZE
    blocks = positions // block
    for i in range(blocks):
        rows = slice(i * block, (i + 1) * block)
        for g in range(groups):
            lanes = slice(g * size, (g + 1) * size)
            terms = grad_ref[rows, lanes].astype(jnp.float32) * out_ref[rows, lanes].astype(
                jnp.float32
            )
            center_ref[g, :, rows] = jnp.broadcast_to(
                jnp.sum(jnp.transpose(terms), axis=0, keepdims=True), (8, block)
            )
    sums_ref[...] = jnp.zeros_like(sums_ref)
    whole = length // block
    some = (length + block - 1) // block

    def key_block(j, _):
        start = pl.multiple_of(j * block, block)
        keys = key_ref[pl.ds(start, block), :]
        values = value_ref[pl.ds(start, block), :]

        def step(i, carry, masked):
            grad_keys, grad_values = carry
            at = pl.multiple_of(i * block, block)
            if masked:
                key_at = start + lax.broadcasted_iota(jnp.int32, (block, block), 0)
                query_at = at + lax.broadcasted_iota(jnp.int32, (block, block), 1)
                allowed = (key_at <= query_at) & (key_at < length)
            for g in range(groups):
                queries = query_ref[pl.ds(at, block), g * size : (g + 1) * size]
                grads = grad_ref[pl.ds(at, block), g * size : (g + 1) * size]
                scores = nt(keys, queries) - total_ref[g, 0:1, pl.ds(at, block)]
                if masked:
                    scores = jnp.where(allowed, scores, MASKED)
                probs = jnp.exp2(scores)
                grad_attend = nt(values, grads)
                grad_scores = (
                    probs * (grad_attend - center_ref[g, 0:1, pl.ds(at, block)])
                ).astype(jnp.bfloat16)
                grad_values = grad_values + nn(probs.astype(jnp.bfloat16), grads)
                grad_keys = grad_keys + nn(grad_scores, queries)
                sums_ref[g, pl.ds(at, block), :] += tn(grad_scores, keys)
            return grad_keys, grad_values

        zero = jnp.zeros((block, size), jnp.float32)
        first = jnp.where(j < whole, jnp.minimum(j + 1, blocks), blocks)
        carry = lax.fori_loop(j, first, lambda i, c: step(i, c, True), (zero, zero))
        grad_keys, grad_values = lax.fori_loop(
            first, blocks, lambda i, c: step(i, c, False), carry
        )
        grad_key_ref[pl.ds(start, block), :] = (grad_keys * (1.0 / math.log2(math.e))).astype(
            grad_key_ref.dtype
        )
        grad_value_ref[pl.ds(start, block), :] = grad_values.astype(grad_value_ref.dtype)
        return 0

    lax.fori_loop(0, some, key_block, 0)

    def padding(j, _):
        start = pl.multiple_of(j * block, block)
        zero = jnp.zeros((block, size), grad_key_ref.dtype)
        grad_key_ref[pl.ds(start, block), :] = zero
        grad_value_ref[pl.ds(start, block), :] = zero
        return 0

    lax.fori_loop(some, blocks, padding, 0)
    for g in range(groups):
        grad_query_ref[:, g * size : (g + 1) * size] = (sums_ref[g] * HEAD_SIZE**-0.5).astype(
            grad_query_ref.dtype
        )


def attend_backward(queries, keys, values, grads, context, totals, lengths, block=512):
    positions, width = queries.shape
    kv_count = keys.shape[1] // HEAD_SIZE
    groups = width // keys.shape[1]
    size = HEAD_SIZE
    wide = pl.BlockSpec((positions, groups * size), lambda h, s: (0, h))
    thin = pl.BlockSpec((positions, size), lambda h, s: (0, h))
    return pl.pallas_call(
        functools.partial(backward_kernel, block, groups, positions),
        grid_spec=pltpu.PrefetchScalarGridSpec(
            num_scalar_prefetch=1,
            grid=(kv_count,),
            in_specs=[
                wide,
                thin,
                thin,
                wide,
                wide,
                pl.BlockSpec((groups, 8, positions), lambda h, s: (h, 0, 0)),
            ],
            out_specs=[wide, thin, thin],
            scratch_shapes=[
                pltpu.VMEM((groups, positions, size), jnp.float32),
                pltpu.VMEM((groups, 8, positions), jnp.float32),
            ],
        ),
        out_shape=(
            jax.ShapeDtypeStruct((positions, width), jnp.bfloat16),
            jax.ShapeDtypeStruct(keys.shape, jnp.bfloat16),
            jax.ShapeDtypeStruct(keys.shape, jnp.bfloat16),
        ),
        compiler_params=pltpu.CompilerParams(
            dimension_semantics=("arbitrary",), vmem_limit_bytes=56 << 20
        ),
        cost_estimate=pl.CostEstimate(
            flops=10 * positions * positions * width,
            bytes_accessed=16 * positions * width,
            transcendentals=positions * positions * width // size // 2,
        ),
        name="attend_backward",
    )(lengths, queries, keys, values, grads, context, totals)


def line_gather(value, count):
    me = lax.axis_index("seq")
    right, left = value, value
    from_left, from_right = [], []
    for hop in range(1, count):
        right = lax.ppermute(right, "seq", [(i, i + 1) for i in range(hop - 1, count - 1)])
        left = lax.ppermute(left, "seq", [(i, i - 1) for i in range(1, count - hop + 1)])
        from_left.append(right)
        from_right.append(left)
    return [value] + [
        jnp.where(me + k < count, from_right[k - 1], from_left[count - k - 1])
        for k in range(1, count)
    ]


def in_order(blocks):
    count, rows = len(blocks), blocks[0].shape[0]
    me = lax.axis_index("seq")
    whole = jnp.zeros((count * rows,) + blocks[0].shape[1:], blocks[0].dtype)
    for k, block in enumerate(blocks):
        whole = lax.dynamic_update_slice_in_dim(whole, block, lax.rem(me + k, count) * rows, 0)
    return whole


def line_scatter(parts):
    count = len(parts)
    right, left = None, None
    for hop in range(count - 1):
        to_right, to_left = parts[count - 1 - hop], parts[hop + 1]
        if hop:
            to_right, to_left = to_right + right, to_left + left
        right = lax.ppermute(
            to_right.astype(jnp.bfloat16), "seq", [(i, i + 1) for i in range(hop + 1)]
        ).astype(jnp.float32)
        left = lax.ppermute(
            to_left.astype(jnp.bfloat16),
            "seq",
            [(i, i - 1) for i in range(count - 1 - hop, count)],
        ).astype(jnp.float32)
    return parts[0] + right + left


def swap(value, count):
    return lax.ppermute(value, "seq", [(i, i ^ 1) for i in range(count)])


def fetch(value, count, step):
    return lax.ppermute(value, "seq", [((i + step) % count, i) for i in range(count)])


def give(value, count, step):
    return lax.ppermute(value, "seq", [(i, (i + step) % count) for i in range(count)])


def on_device(
    tokens,
    lengths,
    cotangent,
    w_query,
    key_weight,
    value_weight,
    w_out,
    w_gate,
    w_up,
    w_down,
    norm_attn,
    norm_mlp,
    norm_query,
    norm_key,
):
    slots, rows, width = tokens.shape
    assert slots == 1
    count = lax.axis_size("seq")
    owners = lax.axis_size("dp")
    positions = count * rows
    me = lax.axis_index("seq")
    tokens_low = tokens.reshape(rows, width)
    cotangent_low = cotangent.reshape(rows, width)
    length = lengths[0]
    low = jnp.bfloat16

    gain_parts = (norm_attn, norm_mlp, norm_query, norm_key)
    gain_sizes = [part.shape[0] for part in gain_parts]
    gathered_gains = lax.all_gather(jnp.concatenate(gain_parts), "dp", axis=0)
    gains, at = [], 0
    for part_size in gain_sizes:
        gains.append(gathered_gains[:, at : at + part_size].reshape(-1).astype(jnp.float32))
        at += part_size
    gain_attn, gain_mlp, gain_query, gain_key = gains

    query_width, key_width = w_query.shape[1], key_weight.shape[1]
    heads_weight = lax.all_gather(
        jnp.concatenate([w_query, key_weight, value_weight], axis=1), "dp", axis=0, tiled=True
    )
    token_blocks = line_gather(tokens_low, count)

    steps = range(0, count, PAIR)

    def mates(weight, axis):
        return jnp.concatenate(
            [weight] + [fetch(weight, count, step) for step in steps[1:]], axis=axis
        )

    gate_weight = lax.all_gather(mates(w_gate, 1), "dp", axis=0, tiled=True)
    up_weight = lax.all_gather(mates(w_up, 1), "dp", axis=0, tiled=True)
    down_weight = lax.all_gather(mates(w_down, 0), "dp", axis=1, tiled=True)
    out_weight = lax.all_gather(in_order(line_gather(w_out, count)), "dp", axis=1, tiled=True)

    inputs = tokens_low.astype(jnp.float32)
    normed_attn = in_order(
        [norm_rows(block.astype(jnp.float32), gain_attn).astype(low) for block in token_blocks]
    )
    raw = nn(normed_attn, heads_weight)
    cosine, sine_table = angles(jnp.arange(positions, dtype=jnp.float32))

    def head_prep(raw_proj, gain):
        return rotate(
            norm_rows(raw_proj.reshape(positions, -1, HEAD_SIZE), gain), cosine, sine_table
        ).reshape(positions, -1)

    query_rot, query_back = jax.vjp(head_prep, raw[:, :query_width], gain_query)
    key_rot, key_back = jax.vjp(head_prep, raw[:, query_width : query_width + key_width], gain_key)
    queries = (query_rot * QUERY_SCALE).astype(low)
    keys = key_rot.astype(low)
    values = raw[:, query_width + key_width :].astype(low)
    context, totals = attend_forward(queries, keys, values, lengths)
    context_tok = lax.all_to_all(context, "seq", split_axis=0, concat_axis=1, tiled=True)

    resid = inputs + nn(context_tok, out_weight)
    normed_second, second_back = jax.vjp(norm_rows, resid, gain_mlp)
    normed_mlp = normed_second.astype(low)

    place = jnp.arange(rows, dtype=jnp.int32)[:, None] + me * rows
    valid_rows = (place < length).astype(jnp.float32)
    grad_rows = cotangent_low.astype(jnp.float32) * valid_rows
    grad_rows_low = grad_rows.astype(low)
    pair_normed = jnp.concatenate([normed_mlp, swap(normed_mlp, count)], axis=0)
    pair_grads = jnp.concatenate([grad_rows_low, swap(grad_rows_low, count)], axis=0)
    gate_proj = nn(pair_normed, gate_weight)
    up_proj = nn(pair_normed, up_weight)
    hidden_full, gating_back = jax.vjp(gating, gate_proj, up_proj)
    hidden = hidden_full.astype(low)
    grad_hidden = nt(pair_grads, down_weight)
    grad_gate_full, grad_up_full = gating_back(grad_hidden)
    grad_gate_low = grad_gate_full.astype(low)
    grad_up_low = grad_up_full.astype(low)
    grad_normed_pair = nt(grad_gate_low, gate_weight) + nt(grad_up_low, up_weight)
    grad_normed_mlp = grad_normed_pair[:rows] + swap(
        grad_normed_pair[rows:].astype(low), count
    ).astype(jnp.float32)
    mlp_pair = nn(hidden, down_weight)
    mlp_out = mlp_pair[:rows] + swap(mlp_pair[rows:].astype(low), count).astype(jnp.float32)
    layer_output = (valid_rows * (resid + mlp_out)).astype(low).reshape(slots, rows, width)

    def owned(partial, axis):
        mine = lax.psum_scatter(
            partial.astype(low), "dp", scatter_dimension=axis, tiled=True
        )
        pieces = jnp.split(mine, len(steps), axis=1 - axis)
        total = pieces[0].astype(jnp.float32)
        for step, piece in zip(steps[1:], pieces[1:]):
            total = total + give(piece, count, step).astype(jnp.float32)
        return total

    grad_gate = owned(tn(pair_normed, grad_gate_low), 0)
    grad_up = owned(tn(pair_normed, grad_up_low), 0)
    grad_down = owned(tn(hidden, pair_grads), 1)

    grad_resid_norm, gain_mlp_term = second_back(grad_normed_mlp)
    grad_resid = grad_rows + grad_resid_norm
    grad_attn_low = grad_resid.astype(low)
    grad_context = lax.all_to_all(
        nt(grad_attn_low, out_weight).astype(low), "seq", split_axis=1, concat_axis=0, tiled=True
    )
    out_partial = lax.psum_scatter(
        tn(context_tok, grad_attn_low).astype(low), "dp", scatter_dimension=1, tiled=True
    )
    out_rows = out_partial.shape[0] // count
    grad_out = line_scatter(
        [
            lax.dynamic_slice_in_dim(
                out_partial, lax.rem(me + k, count) * out_rows, out_rows, 0
            ).astype(jnp.float32)
            for k in range(count)
        ]
    )

    grad_query_rot, grad_key_rot, grad_values = attend_backward(
        queries, keys, values, grad_context, context, totals, lengths
    )
    grad_query_full, gain_query_term = query_back(grad_query_rot.astype(jnp.float32))
    grad_key_full, gain_key_term = key_back(grad_key_rot.astype(jnp.float32))
    grad_raw = jnp.concatenate(
        [grad_query_full.astype(low), grad_key_full.astype(low), grad_values], axis=1
    )
    grad_heads = lax.psum_scatter(
        tn(normed_attn, grad_raw).astype(low), "dp", scatter_dimension=0, tiled=True
    ).astype(jnp.float32)
    grad_query = grad_heads[:, :query_width]
    grad_key = grad_heads[:, query_width : query_width + key_width]
    grad_value = grad_heads[:, query_width + key_width :]

    shares = [
        nt(
            lax.dynamic_slice_in_dim(grad_raw, lax.rem(me + k, count) * rows, rows, 0),
            heads_weight,
        )
        for k in range(count)
    ]
    grad_normed_attn = line_scatter(shares)
    first_back = jax.vjp(norm_rows, inputs, gain_attn)[1]
    grad_input_norm, gain_attn_term = first_back(grad_normed_attn)
    grad_tokens = (grad_resid + grad_input_norm).astype(low).reshape(slots, rows, width)

    terms = (gain_attn_term, gain_mlp_term, gain_query_term, gain_key_term)
    sums = lax.psum(jnp.concatenate(terms), ("dp", "seq"))
    gain_grads, at = [], 0
    for term, part_size in zip(terms, gain_sizes):
        gain_grads.append(
            lax.dynamic_slice_in_dim(
                sums[at : at + term.shape[0]], lax.axis_index("dp") * part_size, part_size, 0
            )
        )
        at += term.shape[0]
    return (
        layer_output,
        grad_tokens,
        grad_query,
        grad_key,
        grad_value,
        grad_out,
        grad_gate,
        grad_up,
        grad_down,
        *gain_grads,
    )


def solution(mesh):
    return jax.shard_map(
        on_device,
        mesh=mesh,
        in_specs=(
            P("dp", "seq", None),
            P("dp"),
            P("dp", "seq", None),
            P("dp", "seq"),
            P("dp", "seq"),
            P("dp", "seq"),
            P("seq", "dp"),
            P("dp", "seq"),
            P("dp", "seq"),
            P("seq", "dp"),
            P("dp"),
            P("dp"),
            P("dp"),
            P("dp"),
        ),
        out_specs=(
            P("dp", "seq", None),
            P("dp", "seq", None),
            P("dp", "seq"),
            P("dp", "seq"),
            P("dp", "seq"),
            P("seq", "dp"),
            P("dp", "seq"),
            P("dp", "seq"),
            P("seq", "dp"),
            P("dp"),
            P("dp"),
            P("dp"),
            P("dp"),
        ),
        check_vma=False,
    )
```

time: 4570 us -> 1460 us (0.32)
  waiting for transfers between devices: 3630 us -> 564 us
  matrix products: 464 us -> 254 us
  starting transfers between devices: 33.1 us -> 186 us
  blocking collectives: 201 us -> 74.8 us
  Pallas kernels: 0 us -> 65.3 us
  other arithmetic: 139 us -> 200 us
    reduce_scatter x14 -> x5, waiting for transfers between devices: 1720 us -> 0.03 us  [the longest x1 0.02 us: on_device(): lax.psum_scatter(tn(context_tok, grad_attn_low).astype(low), 'dp', scatte...]
    all_gather x14 -> x5, waiting for transfers between devices: 1630 us -> 0.01 us  [the longest x1 0.01 us: on_device(): lax.all_gather(jnp.concatenate([w_query, key_weight, value_weight], axis=...]
    ppermute x0 -> x34, waiting for transfers between devices: none -> 485 us  [the longest x4 114 us: swap(): return lax.ppermute(value, 'seq', [(i, i ^ 1) for i in range(count)])]
    dot_general x45 -> x18, matrix products: 464 us -> 254 us  [the longest x8 86.5 us: nt(): lax.dot_general(left, right, (((1,), (1,)), ((), ())), preferred_element_...]
    all_to_all x6 -> x2, waiting for transfers between devices: 272 us -> 78.3 us  [the longest x1 42.8 us: on_device(): lax.all_to_all(context, 'seq', split_axis=0, concat_axis=1, tiled=True)]
    ppermute x0 -> x34, starting transfers between devices: none -> 177 us  [the longest x6 112 us: line_scatter(): lax.ppermute(to_right.astype(jnp.bfloat16), 'seq', [(i, i + 1) for i in r...]
    all_to_all x2 -> x0, blocking collectives: 138 us -> none  [the longest x1 88.7 us: on_device(): lax.all_to_all(for_sending(grad_query_heads), 'seq', split_axis=1, concat...]
    pallas_call x0 -> x2, Pallas kernels: none -> 65.3 us  [the longest x1 39.9 us: attend_backward(): pl.pallas_call(functools.partial(backward_kernel, block, groups, position...]
  transfers between devices with their start and end apart: 34 -> 46, of which waited for: 27 -> 22; matrix products, arithmetic and copies ran while one was open for 11% -> 30% of each run, Pallas kernels for 0% -> 5%
where the time goes in v1:
time: 1460 us; the launch traced here: 1450 us
  waiting for transfers between devices  564 us (39%)
  matrix products  254 us (17%)
  other arithmetic  200 us (14%)
  starting transfers between devices  186 us (13%)
  local copies, waits for them, and re-layouts  85.6 us (6%)
  blocking collectives  74.8 us (5%)
  Pallas kernels  65.3 us (4%)
  between operations  17.1 us (1%)
    ppermute x4, waiting for transfers between devices, swap(): return lax.ppermute(value, 'seq', [(i, i ^ 1) for i in range(count)])  114 us
    ppermute x6, starting transfers between devices, line_scatter(): lax.ppermute(to_right.astype(jnp.bfloat16), 'seq', [(i, i + 1) for i in r...  112 us
    ppermute x6, waiting for transfers between devices, line_scatter(): lax.ppermute(to_right.astype(jnp.bfloat16), 'seq', [(i, i + 1) for i in r...  93.4 us
    ppermute x6, waiting for transfers between devices, line_gather(): lax.ppermute(left, 'seq', [(i, i - 1) for i in range(1, count - hop + 1)])  93.3 us
    dot_general x8, matrix products, nt(): lax.dot_general(left, right, (((1,), (1,)), ((), ())), preferred_element_...  86.5 us
    dot_general x5, matrix products, nn(): lax.dot_general(left, right, (((1,), (0,)), ((), ())), preferred_element_...  84.9 us
    dot_general x5, matrix products, tn(): lax.dot_general(left, right, (((0,), (0,)), ((), ())), preferred_element_...  82.9 us
    ppermute x3, waiting for transfers between devices, fetch(): lax.ppermute(value, 'seq', [((i + step) % count, i) for i in range(count)])  68.9 us
  transfers between devices with their start and end apart: 46, of which 22 were waited for; matrix products, arithmetic and copies ran while one was open for 30% of the time, Pallas kernels for 5%

profile of v1, /device:TPU:0, one launch (start us, length us, event | category | flops | bytes accessed | tf_op | source)
XLA Modules:
  0.0 1446.6 jit_solution(4297010359935688637)
XLA Ops:
  42.6 33.2 %collective-permute-done.15 = bf16[1536,256]{1,0:T(8,128)(2,1)S(1)} collective-permute-done((bf16[1536,256]{1,0:T(8,128)(2,1)S(1)}, bf16[1536,256]{1,0:T(8,128)(2,1)S(1)}, u32[]{:S(2)}, u32[]{:S(2)}) %collective-permute-start.15) | collective-permute-done | bytes 786464 | tf_op jit(solution)/shard_map/ppermute | solution.py:323
  77.2 35.7 %collective-permute-done.14 = bf16[256,1536]{1,0:T(8,128)(2,1)S(1)} collective-permute-done((bf16[256,1536]{1,0:T(8,128)(2,1)}, bf16[256,1536]{1,0:T(8,128)(2,1)S(1)}, u32[]{:S(2)}, u32[]{:S(2)}) %collective-permute-start.14) | collective-permute-done | bytes 786464 | tf_op jit(solution)/shard_map/ppermute | solution.py:323
  119.9 42.2 %collective-permute-done.1 = bf16[512,2048]{1,0:T(8,128)(2,1)} collective-permute-done((bf16[512,2048]{1,0:T(8,128)(2,1)S(1)}, bf16[512,2048]{1,0:T(8,128)(2,1)}, u32[]{:S(2)}, u32[]{:S(2)}) %collective-permute-start.1) | collective-permute-done | bytes 2097184 | tf_op jit(solution)/shard_map/ppermute | solution.py:281
  171.5 23.2 %all-reduce.4 = bf16[4352]{0:T(1024)(128)(2,1)S(1)} all-reduce(bf16[4352]{0:T(1024)(128)(2,1)S(1)} %dynamic-update-slice), channel_id=2, replica_groups=mesh['dp'=8,'seq'=4] {'dp'}, use_global_device_ids=true, to_apply=%add.4 | all-reduce | flops 4352 | bytes 17408
  205.4 42.8 %collective-permute-done.4 = bf16[512,2048]{1,0:T(8,128)(2,1)} collective-permute-done((bf16[512,2048]{1,0:T(8,128)(2,1)}, bf16[512,2048]{1,0:T(8,128)(2,1)}, u32[]{:S(2)}, u32[]{:S(2)}) %collective-permute-start.4) | collective-permute-done | bytes 2097184 | tf_op jit(solution)/shard_map/ppermute | solution.py:282
  263.4 34.5 %collective-permute-done.5 = bf16[512,2048]{1,0:T(8,128)(2,1)} collective-permute-done((bf16[512,2048]{1,0:T(8,128)(2,1)}, bf16[512,2048]{1,0:T(8,128)(2,1)}, u32[]{:S(2)}, u32[]{:S(2)}) %collective-permute-start.5) | collective-permute-done | bytes 2097184 | tf_op jit(solution)/shard_map/ppermute | solution.py:282
  390.6 25.4 %attend_forward.1 = (bf16[2048,512]{1,0:T(8,128)(2,1)S(1)}, f32[4,8,2048]{2,1,0:T(8,128)S(1)}) custom-call(s32[1]{0:T(128)} %copy.91.length_ref, bf16[2048,512]{1,0:T(8,128)(2,1)} %fusion.24.query_ref, bf16[2048,256]{1,0:T(8,128)(2,1)S(1)} %fusion.38.key_ref, bf16[2048,256]{1,0:T(8,128)(2,1)S(1)} %slice.142.value_ref), custom_call_target="tpu_custom_call" | custom-call | flops 8589934592 | bytes 8388608 | tf_op jit(solution)/shard_map/attend_forward/pallas_call | solution.py:111
  429.8 42.8 %all-to-all-done = bf16[4,512,512]{1,2,0:T(8,128)(2,1)} async-done(((bf16[4,512,512]{1,2,0:T(8,128)(2,1)}), bf16[4,512,512]{1,2,0:T(8,128)(2,1)}, u32[]{:S(2)}, u32[]{:S(2)}) %all-to-all-start) | async-done | bytes 2097184 | tf_op jit(solution)/shard_map/all_to_all | solution.py:402
  482.9 23.9 %collective-permute-done.17 = bf16[512,2048]{1,0:T(8,128)(2,1)} collective-permute-done((bf16[512,2048]{1,0:T(8,128)(2,1)}, bf16[512,2048]{1,0:T(8,128)(2,1)}, u32[]{:S(2)}, u32[]{:S(2)}) %collective-permute-start.17) | collective-permute-done | bytes 2097184 | tf_op jit(solution)/shard_map/ppermute | solution.py:319
  526.1 24.1 %collective-permute-done.12 = bf16[512,2048]{1,0:T(8,128)(2,1)} collective-permute-done((bf16[512,2048]{1,0:T(8,128)(2,1)S(1)}, bf16[512,2048]{1,0:T(8,128)(2,1)}, u32[]{:S(2)}, u32[]{:S(2)}) %collective-permute-start.12) | collective-permute-done | bytes 2097184 | tf_op jit(solution)/shard_map/ppermute | solution.py:319
  568.7 29.1 %fusion.2 = (bf16[1024,3072]{1,0:T(8,128)(2,1)}, bf16[1024,3072]{1,0:T(8,128)(2,1)}, bf16[1024,3072]{1,0:T(8,128)(2,1)}) fusion(f32[1024,3072]{1,0:T(8,128)} %fusion.30, f32[1024,3072]{1,0:T(8,128)} %fusion.65, bf16[2048,3072]{1,0:T(8,128)(2,1)} %all-gather.11.cloned.1.call-done, bf16[512,2048]{1,0:T(8,128)(2,1)} %collective-permute-done.12, ...), kind=kOutput, calls=%fused_computation.3 | convolution fusion | flops 12943622144 | bytes 60817408 | tf_op jit(solution)/shard_map/dot_general | solution.py:48
  662.2 26.0 %collective-permute-done.18 = bf16[512,2048]{1,0:T(8,128)(2,1)S(1)} collective-permute-done((bf16[512,2048]{1,0:T(8,128)(2,1)S(1)}, bf16[512,2048]{1,0:T(8,128)(2,1)S(1)}, u32[]{:S(2)}, u32[]{:S(2)}) %collective-permute-start.18) | collective-permute-done | bytes 2097184 | tf_op jit(solution)/shard_map/ppermute | solution.py:319
  690.2 40.4 %collective-permute-done.16 = bf16[512,2048]{1,0:T(8,128)(2,1)S(1)} collective-permute-done((bf16[512,2048]{1,0:T(8,128)(2,1)S(1)}, bf16[512,2048]{1,0:T(8,128)(2,1)S(1)}, u32[]{:S(2)}, u32[]{:S(2)}) %collective-permute-start.16) | collective-permute-done | bytes 2097184 | tf_op jit(solution)/shard_map/ppermute | solution.py:319
  761.4 35.5 %all-to-all-done.1 = bf16[512,4,512]{2,0,1:T(8,128)(2,1)S(1)} async-done(((bf16[512,4,512]{2,0,1:T(8,128)(2,1)}), bf16[512,4,512]{2,0,1:T(8,128)(2,1)S(1)}, u32[]{:S(2)}, u32[]{:S(2)}) %all-to-all-start.1) | async-done | bytes 2097184 | tf_op jit(solution)/shard_map/all_to_all | solution.py:447
  798.3 39.9 %attend_backward.1 = (bf16[2048,512]{1,0:T(8,128)(2,1)}, bf16[2048,256]{1,0:T(8,128)(2,1)}, bf16[2048,256]{1,0:T(8,128)(2,1)}) custom-call(s32[1]{0:T(128)} %copy.91.length_ref, bf16[2048,512]{1,0:T(8,128)(2,1)} %fusion.24.query_ref, bf16[2048,256]{1,0:T(8,128)(2,1)} %copy-done.1, bf16[2048,256]{1,0:T(8,128)(2,1)} %copy-done.2, bf16[2048,512]{1,0:T(8,128)(2,1)} %bitcast.120, ...), custom_call_target="tpu_custom_call" | custom-call | flops 21474836480 | bytes 16777216 | tf_op jit(solution)/shard_map/attend_backward/pallas_call | solution.py:240
  845.9 33.2 %multiply_reduce_fusion.6 = (f32[128]{0:T(128)}, f32[2048,2]{1,0:T(8,128)}, f32[2048,2,128]{2,1,0:T(2,128)}) fusion(f32[2048,2,128]{2,1,0:T(2,128)S(1)} %copy-done.7, f32[2048,2]{1,0:T(8,128)S(1)} %copy-done.19, f32[128]{0:T(128)S(1)} %copy-done.68, f32[2048,2,64]{2,1,0:T(2,128)S(1)} %get-tuple-element.47, f32[2048,2,64]{2,1,0:T(2,128)S(1)} %get-tuple-element.46, ...), kind=kLoop, calls=%fused_computation.102 | loop fusion | flops 4714368 | bytes 9470976 | tf_op jit(solution)/shard_map/transpose(jvp())/reduce_sum | solution.py:21
  893.6 32.4 %multiply_reduce_fusion = (f32[128]{0:T(128)S(1)}, f32[2048,4]{1,0:T(8,128)}, f32[2048,4,128]{2,1,0:T(4,128)}) fusion(f32[2048,4,128]{2,1,0:T(4,128)S(1)} %copy-done.5, f32[2048,4]{1,0:T(8,128)S(1)} %copy-done.12, f32[128]{0:T(128)S(1)} %copy-done.64, f32[2048,4,64]{2,1,0:T(4,128)S(1)} %get-tuple-element.43, f32[2048,4,64]{2,1,0:T(4,128)S(1)} %get-tuple-element.42, ...), kind=kLoop, calls=%fused_computation.66 | loop fusion | flops 9428864 | bytes 17892352 | tf_op jit(solution)/shard_map/transpose(jvp())/reduce_sum | solution.py:21
  1004.5 20.2 %convolution_convert_fusion.2 = bf16[2048,3072]{1,0:T(8,128)(2,1)} fusion(bf16[1024,3072]{1,0:T(8,128)(2,1)} %get-tuple-element.35, bf16[512,2048]{1,0:T(8,128)(2,1)} %collective-permute-done.12, bf16[512,2048]{1,0:T(8,128)(2,1)S(1)} %copy-done.36), kind=kOutput, calls=%fused_computation.10 | convolution fusion | flops 12899581952 | bytes 23068672 | tf_op jit(solution)/shard_map/dot_general | solution.py:60
  1032.8 44.5 %collective-permute-done.19 = bf16[512,2048]{1,0:T(8,128)(2,1)S(1)} collective-permute-done((bf16[512,2048]{1,0:T(8,128)(2,1)S(1)}, bf16[512,2048]{1,0:T(8,128)(2,1)S(1)}, u32[]{:S(2)}, u32[]{:S(2)}) %collective-permute-start.19) | collective-permute-done | bytes 2097184 | tf_op jit(solution)/shard_map/ppermute | solution.py:307
  1086.8 41.2 %collective-permute-done.20 = bf16[512,2048]{1,0:T(8,128)(2,1)S(1)} collective-permute-done((bf16[512,2048]{1,0:T(8,128)(2,1)S(1)}, bf16[512,2048]{1,0:T(8,128)(2,1)S(1)}, u32[]{:S(2)}, u32[]{:S(2)}) %collective-permute-start.20) | collective-permute-done | bytes 2097184 | tf_op jit(solution)/shard_map/ppermute | solution.py:307
  1143.5 90.3 %collective-permute-start.25 = (bf16[512,256]{1,0:T(8,128)(2,1)S(1)}, bf16[512,256]{1,0:T(8,128)(2,1)S(1)}, u32[]{:S(2)}, u32[]{:S(2)}) collective-permute-start(bf16[512,256]{1,0:T(8,128)(2,1)S(1)} %constant_dynamic-slice_fusion), channel_id=1, source_target_pairs={{0,1},{4,5},{8,9},{12,13},{16,17},{20,21},{24,25},{28,29}} | collective-permute-start | bytes 786440 | tf_op jit(solution)/shard_map/ppermute | solution.py:307
  1288.3 24.1 %collective-permute-start.33 = (bf16[1536,256]{1,0:T(8,128)(2,1)}, bf16[1536,256]{1,0:T(8,128)(2,1)}, u32[]{:S(2)}, u32[]{:S(2)}) collective-permute-start(bf16[1536,256]{1,0:T(8,128)(2,1)} %split.49), channel_id=1, source_target_pairs={{0,2},{1,3},{2,0},{3,1},{4,6},{5,7},{6,4},{7,5},{8,10},{9,11},{10,... | collective-permute-start | bytes 2359304 | tf_op jit(solution)/shard_map/ppermute | solution.py:327
  1312.4 51.7 %psum.7 = f32[4352]{0:T(1024)S(1)} all-reduce(f32[4352]{0:T(1024)S(1)} %pad_maximum_fusion.10), channel_id=1, replica_groups=mesh['dp'=8,'seq'=4] {'dp','seq'}, use_global_device_ids=true, to_apply=%region_20.21 | all-reduce | flops 4352 | bytes 34816 | tf_op jit(solution)/shard_map/psum | solution.py:491
  1377.2 44.3 %collective-permute-done.32 = bf16[256,1536]{1,0:T(8,128)(2,1)} collective-permute-done((bf16[256,1536]{1,0:T(8,128)(2,1)}, bf16[256,1536]{1,0:T(8,128)(2,1)}, u32[]{:S(2)}, u32[]{:S(2)}) %collective-permute-start.32) | collective-permute-done | bytes 786464 | tf_op jit(solution)/shard_map/ppermute | solution.py:327
  (383 shorter events, 548.9 us)
Async XLA Ops:
  7.2 305.6 %all-gather.7.cloned.1.call-start = ((), (), s32[]{:S(2)}) async-start(), calls=%async_computation.7 | async-start | bytes 4718592 | tf_op jit(solution)/shard_map/all_gather | solution.py:367
  9.3 463.3 %all-gather.9.cloned.1.call-start = ((), (), s32[]{:S(2)}) async-start(), calls=%async_computation.8 | async-start | bytes 9437184 | tf_op jit(solution)/shard_map/all_gather | solution.py:382
  42.4 464.3 %all-gather.15.cloned.1.call-start = ((), (), s32[]{:S(2)}) async-start(), calls=%async_computation.11 | async-start | bytes 14155776 | tf_op jit(solution)/shard_map/all_gather | solution.py:381
  77.1 473.2 %all-gather.13.cloned.1.call-start = ((), (), s32[]{:S(2)}) async-start(), calls=%async_computation.10 | async-start | bytes 14155776 | tf_op jit(solution)/shard_map/all_gather | solution.py:380
  115.4 453.3 %all-gather.11.cloned.1.call-start = ((), (), s32[]{:S(2)}) async-start(), calls=%async_computation.9 | async-start | bytes 14155776 | tf_op jit(solution)/shard_map/all_gather | solution.py:379
  118.6 76.1 %collective-permute-start = (bf16[512,2048]{1,0:T(8,128)(2,1)S(1)}, bf16[512,2048]{1,0:T(8,128)(2,1)}, u32[]{:S(2)}, u32[]{:S(2)}) collective-permute-start(bf16[512,2048]{1,0:T(8,128)(2,1)S(1)} %bitcast.109), channel_id=1, source_target_pairs={{1,0},{2,1},{3,2},{5,4},{6,5},{7,6},{9,8},{10,9},{11,10},{13,12},{... | collective-permute-start | bytes 6291464 | tf_op jit(solution)/shard_map/ppermute | solution.py:282
  164.1 92.1 %collective-permute-start.13 = (bf16[256,1536]{1,0:T(8,128)(2,1)S(1)}, bf16[256,1536]{1,0:T(8,128)(2,1)}, u32[]{:S(2)}, u32[]{:S(2)}) collective-permute-start(bf16[256,1536]{1,0:T(8,128)(2,1)S(1)} %copy-done.45), channel_id=1, source_target_pairs={{2,0},{3,1},{0,2},{1,3},{6,4},{7,5},{4,6},{5,7},{10,8},{11,9},{8,1... | collective-permute-start | bytes 2359304 | tf_op jit(solution)/shard_map/ppermute | solution.py:323
  194.8 53.4 %collective-permute-start.4 = (bf16[512,2048]{1,0:T(8,128)(2,1)}, bf16[512,2048]{1,0:T(8,128)(2,1)}, u32[]{:S(2)}, u32[]{:S(2)}) collective-permute-start(bf16[512,2048]{1,0:T(8,128)(2,1)} %collective-permute-done), channel_id=1, source_target_pairs={{1,0},{2,1},{5,4},{6,5},{9,8},{10,9},{13,12},{14,13},{17,16},{18,1... | collective-permute-start | bytes 6291464 | tf_op jit(solution)/shard_map/ppermute | solution.py:282
  202.6 58.4 %collective-permute-start.3 = (bf16[512,2048]{1,0:T(8,128)(2,1)}, bf16[512,2048]{1,0:T(8,128)(2,1)}, u32[]{:S(2)}, u32[]{:S(2)}) collective-permute-start(bf16[512,2048]{1,0:T(8,128)(2,1)} %collective-permute-done.2), channel_id=1, source_target_pairs={{2,3},{6,7},{10,11},{14,15},{18,19},{22,23},{26,27},{30,31}} | collective-permute-start | bytes 6291464 | tf_op jit(solution)/shard_map/ppermute | solution.py:281
  427.8 79.0 %collective-permute-start.17 = (bf16[512,2048]{1,0:T(8,128)(2,1)}, bf16[512,2048]{1,0:T(8,128)(2,1)}, u32[]{:S(2)}, u32[]{:S(2)}) collective-permute-start(bf16[512,2048]{1,0:T(8,128)(2,1)} %fusion.29), channel_id=1, source_target_pairs={{0,1},{1,0},{2,3},{3,2},{4,5},{5,4},{6,7},{7,6},{8,9},{9,8},{10,11... | collective-permute-start | bytes 6291464 | tf_op jit(solution)/shard_map/ppermute | solution.py:319
  482.8 67.4 %collective-permute-start.12 = (bf16[512,2048]{1,0:T(8,128)(2,1)S(1)}, bf16[512,2048]{1,0:T(8,128)(2,1)}, u32[]{:S(2)}, u32[]{:S(2)}) collective-permute-start(bf16[512,2048]{1,0:T(8,128)(2,1)S(1)} %multiply_convert_fusion.2), channel_id=1, source_target_pairs={{0,1},{1,0},{2,3},{3,2},{4,5},{5,4},{6,7},{7,6},{8,9},{9,8},{10,11... | collective-permute-start | bytes 6291464 | tf_op jit(solution)/shard_map/ppermute | solution.py:319
  660.5 70.2 %collective-permute-start.16 = (bf16[512,2048]{1,0:T(8,128)(2,1)S(1)}, bf16[512,2048]{1,0:T(8,128)(2,1)S(1)}, u32[]{:S(2)}, u32[]{:S(2)}) collective-permute-start(bf16[512,2048]{1,0:T(8,128)(2,1)S(1)} %slice.141), channel_id=1, source_target_pairs={{0,1},{1,0},{2,3},{3,2},{4,5},{5,4},{6,7},{7,6},{8,9},{9,8},{10,11... | collective-permute-start | bytes 6291464 | tf_op jit(solution)/shard_map/ppermute | solution.py:319
  750.8 391.7 %reduce-scatter.8.cloned.1.call-start = ((), (), s32[]{:S(2)}) async-start(), calls=%async_computation.13 | async-start | bytes 9437184 | tf_op jit(solution)/shard_map/reduce_scatter | solution.py:450
  761.4 491.2 %reduce-scatter.6.cloned.1.call-start = ((), (), s32[]{:S(2)}) async-start(), calls=%async_computation.12 | async-start | bytes 4718592 | tf_op jit(solution)/shard_map/reduce_scatter | solution.py:471
  963.2 322.9 %reduce-scatter.14.cloned.1.call-start = ((), (), s32[]{:S(2)}) async-start(), calls=%async_computation.16 | async-start | bytes 14155776 | tf_op jit(solution)/shard_map/reduce_scatter | solution.py:431
  983.1 383.4 %reduce-scatter.12.cloned.1.call-start = ((), (), s32[]{:S(2)}) async-start(), calls=%async_computation.15 | async-start | bytes 14155776 | tf_op jit(solution)/shard_map/reduce_scatter | solution.py:431
  1004.5 366.0 %reduce-scatter.10.cloned.1.call-start = ((), (), s32[]{:S(2)}) async-start(), calls=%async_computation.14 | async-start | bytes 14155776 | tf_op jit(solution)/shard_map/reduce_scatter | solution.py:431
  1132.6 131.3 %collective-permute-start.21 = (bf16[512,2048]{1,0:T(8,128)(2,1)}, bf16[512,2048]{1,0:T(8,128)(2,1)}, u32[]{:S(2)}, u32[]{:S(2)}) collective-permute-start(bf16[512,2048]{1,0:T(8,128)(2,1)} %get-tuple-element.40), channel_id=1, source_target_pairs={{0,1},{1,2},{2,3},{4,5},{5,6},{6,7},{8,9},{9,10},{10,11},{12,13},{... | collective-permute-start | bytes 6291464 | tf_op jit(solution)/shard_map/ppermute | solution.py:307
  1140.9 132.9 %collective-permute-start.24 = (bf16[512,2048]{1,0:T(8,128)(2,1)}, bf16[512,2048]{1,0:T(8,128)(2,1)}, u32[]{:S(2)}, u32[]{:S(2)}) collective-permute-start(bf16[512,2048]{1,0:T(8,128)(2,1)} %add_convert_fusion), channel_id=1, source_target_pairs={{1,0},{2,1},{3,2},{5,4},{6,5},{7,6},{9,8},{10,9},{11,10},{13,12},{... | collective-permute-start | bytes 6291464 | tf_op jit(solution)/shard_map/ppermute | solution.py:310
  1143.5 94.2 %collective-permute-start.25 = (bf16[512,256]{1,0:T(8,128)(2,1)S(1)}, bf16[512,256]{1,0:T(8,128)(2,1)S(1)}, u32[]{:S(2)}, u32[]{:S(2)}) collective-permute-start(bf16[512,256]{1,0:T(8,128)(2,1)S(1)} %constant_dynamic-slice_fusion), channel_id=1, source_target_pairs={{0,1},{4,5},{8,9},{12,13},{16,17},{20,21},{24,25},{28,29}} | collective-permute-start | bytes 786440 | tf_op jit(solution)/shard_map/ppermute | solution.py:307
  1256.2 112.4 %collective-permute-start.27 = (bf16[512,256]{1,0:T(8,128)(2,1)}, bf16[512,256]{1,0:T(8,128)(2,1)S(1)}, u32[]{:S(2)}, u32[]{:S(2)}) collective-permute-start(bf16[512,256]{1,0:T(8,128)(2,1)} %get-tuple-element.31), channel_id=1, source_target_pairs={{0,1},{1,2},{2,3},{4,5},{5,6},{6,7},{8,9},{9,10},{10,11},{12,13},{... | collective-permute-start | bytes 786440 | tf_op jit(solution)/shard_map/ppermute | solution.py:307
  1262.3 106.3 %collective-permute-start.30 = (bf16[512,256]{1,0:T(8,128)(2,1)}, bf16[512,256]{1,0:T(8,128)(2,1)}, u32[]{:S(2)}, u32[]{:S(2)}) collective-permute-start(bf16[512,256]{1,0:T(8,128)(2,1)} %add_convert_fusion.4), channel_id=1, source_target_pairs={{1,0},{2,1},{3,2},{5,4},{6,5},{7,6},{9,8},{10,9},{11,10},{13,12},{... | collective-permute-start | bytes 786440 | tf_op jit(solution)/shard_map/ppermute | solution.py:310
  1288.3 86.5 %collective-permute-start.33 = (bf16[1536,256]{1,0:T(8,128)(2,1)}, bf16[1536,256]{1,0:T(8,128)(2,1)}, u32[]{:S(2)}, u32[]{:S(2)}) collective-permute-start(bf16[1536,256]{1,0:T(8,128)(2,1)} %split.49), channel_id=1, source_target_pairs={{0,2},{1,3},{2,0},{3,1},{4,6},{5,7},{6,4},{7,5},{8,10},{9,11},{10,... | collective-permute-start | bytes 2359304 | tf_op jit(solution)/shard_map/ppermute | solution.py:327
  1371.8 66.4 %collective-permute-start.31 = (bf16[256,1536]{1,0:T(8,128)(2,1)S(1)}, bf16[256,1536]{1,0:T(8,128)(2,1)S(1)}, u32[]{:S(2)}, u32[]{:S(2)}) collective-permute-start(bf16[256,1536]{1,0:T(8,128)(2,1)S(1)} %split.45), channel_id=1, source_target_pairs={{0,2},{1,3},{2,0},{3,1},{4,6},{5,7},{6,4},{7,5},{8,10},{9,11},{10,... | collective-permute-start | bytes 2359304 | tf_op jit(solution)/shard_map/ppermute | solution.py:327
  (103 other events, 3827.9 us)
Sparse Core Ops, SparseCore 0:
  10.5 39.4 all-gather.6
  51.8 55.9 all-gather.8
  110.3 74.6 all-gather.14
  187.2 72.1 all-gather.12
  261.8 72.1 all-gather.10
  761.5 72.3 reduce-scatter.7
  963.4 49.9 reduce-scatter.5
  1016.8 92.3 reduce-scatter.13
  1112.7 92.3 reduce-scatter.11
  1208.5 92.3 reduce-scatter.9

commit v2 on v1

v2 whole, which is shorter than its diff:
```python
import functools
import math

import jax
import jax.numpy as jnp
from jax import lax
from jax.experimental import pallas as pl
from jax.experimental.pallas import tpu as pltpu
from jax.sharding import PartitionSpec as P

HEAD_SIZE = 128
EPS = 1e-06
BASE = 1000000.0
MASKED = -1e30
QUERY_SCALE = HEAD_SIZE**-0.5 * math.log2(math.e)
PAIR = 2
LANES = 128
COST_SCALE = 0.05


def norm_rows(value_rows, gain):
    return (
        value_rows
        * lax.rsqrt(jnp.mean(value_rows * value_rows, axis=-1, keepdims=True) + EPS)
        * gain
    )


def angles(positions):
    frequency = BASE ** (-(jnp.arange(HEAD_SIZE // 2, dtype=jnp.float32) * 2.0 / HEAD_SIZE))
    phases = positions[:, None] * frequency[None, :]
    cosine, sine_table = jnp.cos(phases), jnp.sin(phases)
    return (
        jnp.concatenate([cosine, cosine], axis=-1),
        jnp.concatenate([-sine_table, sine_table], axis=-1),
    )


def nn(left, right):
    return lax.dot_general(
        left, right, (((1,), (0,)), ((), ())), preferred_element_type=jnp.float32
    )


def nt(left, right):
    return lax.dot_general(
        left, right, (((1,), (1,)), ((), ())), preferred_element_type=jnp.float32
    )


def tn(left, right):
    return lax.dot_general(
        left, right, (((0,), (0,)), ((), ())), preferred_element_type=jnp.float32
    )


def arbitrary(axes, megabytes):
    return pltpu.CompilerParams(
        dimension_semantics=("arbitrary",) * axes, vmem_limit_bytes=megabytes << 20
    )


def cost(flops, moved, exps=0):
    return pl.CostEstimate(
        flops=int(flops * COST_SCALE),
        bytes_accessed=int(moved * COST_SCALE),
        transcendentals=int(exps * COST_SCALE),
    )


def fixed(shape):
    return pl.BlockSpec(shape, lambda *_: (0,) * len(shape))


def project_kernel(
    groups,
    kv_count,
    place_ref,
    first_ref,
    second_ref,
    gain_ref,
    weight_ref,
    cosine_ref,
    sine_ref,
    head_gain_ref,
    *refs,
):
    normed_ref, heads_ref, raw_ref = refs[-3:]
    size = HEAD_SIZE
    rows = jnp.where(place_ref[1] != 0, first_ref[...], second_ref[...]).astype(jnp.float32)
    scale = lax.rsqrt(jnp.mean(rows * rows, axis=-1, keepdims=True) + EPS)
    normed = (rows * scale * gain_ref[...]).astype(jnp.bfloat16)
    normed_ref[...] = normed
    raw = nn(normed, weight_ref[...])
    cosine, sine_table = cosine_ref[...], sine_ref[...]
    for h in range(kv_count):
        start = h * (groups + 2) * size
        for g in range(groups + 1):
            column = start + g * size
            value = raw[:, column : column + size]
            held = (h * (groups + 1) + g) * size
            raw_ref[:, held : held + size] = value
            which = 0 if g < groups else 1
            value = value * lax.rsqrt(jnp.mean(value * value, axis=-1, keepdims=True) + EPS)
            value = value * head_gain_ref[which : which + 1, :]
            value = value * cosine + pltpu.roll(value, size // 2, 1) * sine_table
            if g < groups:
                value = value * QUERY_SCALE
            heads_ref[:, column : column + size] = value.astype(jnp.bfloat16)
        column = start + (groups + 1) * size
        heads_ref[:, column : column + size] = raw[:, column : column + size].astype(jnp.bfloat16)


def project(
    place, first, second, gain, weight, cosine, sine_table, head_gains, groups, before, count
):
    rows, width = first.shape
    positions = count * rows
    columns = weight.shape[1]
    kv_count = columns // ((groups + 2) * HEAD_SIZE)
    held = kv_count * (groups + 1) * HEAD_SIZE
    block = min(256, rows)
    parts = rows // block
    same = lambda i, s: (0, 0)
    here = lambda i, s: (i, 0)
    there = lambda i, s: (s[0] * parts + i, 0)
    in_specs = [
        pl.BlockSpec((block, width), here),
        pl.BlockSpec((block, width), here),
        pl.BlockSpec((1, width), same),
        pl.BlockSpec((width, columns), same),
        pl.BlockSpec((block, HEAD_SIZE), there),
        pl.BlockSpec((block, HEAD_SIZE), there),
        pl.BlockSpec((2, HEAD_SIZE), same),
    ]
    args = [first, second, gain, weight, cosine, sine_table, head_gains]
    aliases = {}
    if before is not None:
        in_specs += [pl.BlockSpec(memory_space=pl.ANY)] * 3
        aliases = {len(args) + 1 + k: k for k in range(3)}
        args += list(before)
    return pl.pallas_call(
        functools.partial(project_kernel, groups, kv_count),
        grid_spec=pltpu.PrefetchScalarGridSpec(
            num_scalar_prefetch=1,
            grid=(parts,),
            in_specs=in_specs,
            out_specs=[
                pl.BlockSpec((block, width), there),
                pl.BlockSpec((block, columns), there),
                pl.BlockSpec((block, held), there),
            ],
        ),
        out_shape=(
            jax.ShapeDtypeStruct((positions, width), jnp.bfloat16),
            jax.ShapeDtypeStruct((positions, columns), jnp.bfloat16),
            jax.ShapeDtypeStruct((positions, held), jnp.float32),
        ),
        input_output_aliases=aliases,
        compiler_params=arbitrary(1, 40),
        cost_estimate=cost(2 * rows * width * columns, 2 * width * columns + 12 * rows * width),
        name="project",
    )(place, *args)


def forward_kernel(block, groups, place_ref, heads_ref, out_ref, total_ref, wide_ref):
    at_query = pl.program_id(1)
    length = place_ref[0]
    size = HEAD_SIZE
    key_lanes = slice(groups * size, (groups + 1) * size)

    @pl.when(at_query == 0)
    def _():
        wide_ref[:, :size] = heads_ref[:, (groups + 1) * size :]
        wide_ref[:, size:] = jnp.ones((wide_ref.shape[0], size), wide_ref.dtype)

    whole = jnp.minimum(at_query, length // block)
    some = jnp.minimum(at_query + 1, (length + block - 1) // block)
    here = pl.ds(pl.multiple_of(at_query * block, block), block)
    queries = [heads_ref[here, g * size : (g + 1) * size] for g in range(groups)]

    def step(at_key, sums, masked):
        start = pl.multiple_of(at_key * block, block)
        keys = heads_ref[pl.ds(start, block), key_lanes]
        wide = wide_ref[pl.ds(start, block), :]
        if masked:
            rows = at_query * block + lax.broadcasted_iota(jnp.int32, (block, block), 0)
            cols = start + lax.broadcasted_iota(jnp.int32, (block, block), 1)
            allowed = (cols <= rows) & (cols < length)
        after = []
        for g in range(groups):
            scores = nt(queries[g], keys)
            if masked:
                scores = jnp.where(allowed, scores, MASKED)
            after.append(sums[g] + nn(jnp.exp2(scores).astype(jnp.bfloat16), wide))
        return tuple(after)

    sums = tuple(jnp.zeros((block, 2 * size), jnp.float32) for _ in range(groups))
    sums = lax.fori_loop(0, whole, lambda j, c: step(j, c, False), sums)
    sums = lax.fori_loop(whole, some, lambda j, c: step(j, c, True), sums)
    for g in range(groups):
        total = sums[g][:, size:]
        out_ref[:, g * size : (g + 1) * size] = (sums[g][:, :size] / total).astype(out_ref.dtype)
        total_ref[g, :, :] = jnp.transpose(jnp.log2(total))[:8, :]


def attend_forward(place, heads, groups, count):
    positions = heads.shape[0]
    rows = positions // count
    block = min(512, rows)
    parts = rows // block
    group_width = (groups + 2) * HEAD_SIZE
    kv_count = heads.shape[1] // group_width
    size = HEAD_SIZE
    width = kv_count * groups * size
    return pl.pallas_call(
        functools.partial(forward_kernel, block, groups),
        grid_spec=pltpu.PrefetchScalarGridSpec(
            num_scalar_prefetch=1,
            grid=(kv_count, positions // block),
            in_specs=[pl.BlockSpec((positions, group_width), lambda h, i, s: (0, h))],
            out_specs=[
                pl.BlockSpec(
                    (None, block, groups * size),
                    lambda h, i, s: (
                        lax.rem(i // parts + count - s[1], count),
                        lax.rem(i, parts),
                        h,
                    ),
                ),
                pl.BlockSpec((groups, 8, block), lambda h, i, s: (h, 0, i)),
            ],
            scratch_shapes=[pltpu.VMEM((positions, 2 * size), jnp.bfloat16)],
        ),
        out_shape=(
            jax.ShapeDtypeStruct((count, rows, width), jnp.bfloat16),
            jax.ShapeDtypeStruct((kv_count * groups, 8, positions), jnp.float32),
        ),
        compiler_params=arbitrary(2, 48),
        cost_estimate=cost(
            4 * positions * positions * width,
            8 * positions * width,
            positions * positions * width // size // 2,
        ),
        name="attend_forward",
    )(place, heads)


def backward_kernel(
    block,
    groups,
    positions,
    count,
    place_ref,
    heads_ref,
    raw_ref,
    cosine_ref,
    sine_ref,
    head_gain_ref,
    out_ref,
    total_ref,
    *refs,
):
    piece_refs = refs[:count]
    grad_raw_ref, gain_ref, query_sums_ref, key_sums_ref, center_ref, grad_ref = refs[count:]
    length = place_ref[0]
    size = HEAD_SIZE
    rows_each = positions // count
    blocks = positions // block
    key_lanes = slice(groups * size, (groups + 1) * size)
    value_lanes = slice((groups + 1) * size, (groups + 2) * size)
    for k in range(count):
        place = lax.rem(place_ref[1] + k, count) * rows_each
        piece_ref = piece_refs[(count - k) % count]
        grad_ref[pl.ds(pl.multiple_of(place, rows_each), rows_each), :] = piece_ref[...]
        for g in range(groups):
            lanes = slice(g * size, (g + 1) * size)
            terms = piece_ref[:, lanes].astype(jnp.float32) * out_ref[k, :, lanes].astype(
                jnp.float32
            )
            center_ref[g, :, pl.ds(pl.multiple_of(place, rows_each), rows_each)] = (
                jnp.broadcast_to(
                    jnp.sum(jnp.transpose(terms), axis=0, keepdims=True), (8, rows_each)
                )
            )
    query_sums_ref[...] = jnp.zeros_like(query_sums_ref)
    whole = length // block
    some = (length + block - 1) // block

    def key_block(j, _):
        start = pl.multiple_of(j * block, block)
        keys = heads_ref[pl.ds(start, block), key_lanes]
        values = heads_ref[pl.ds(start, block), value_lanes]

        def step(i, carry, masked):
            grad_keys, grad_values = carry
            at = pl.multiple_of(i * block, block)
            if masked:
                key_at = start + lax.broadcasted_iota(jnp.int32, (block, block), 0)
                query_at = at + lax.broadcasted_iota(jnp.int32, (block, block), 1)
                allowed = (key_at <= query_at) & (key_at < length)
            for g in range(groups):
                queries = heads_ref[pl.ds(at, block), g * size : (g + 1) * size]
                grads = grad_ref[pl.ds(at, block), g * size : (g + 1) * size]
                scores = nt(keys, queries) - total_ref[g, 0:1, pl.ds(at, block)]
                if masked:
                    scores = jnp.where(allowed, scores, MASKED)
                probs = jnp.exp2(scores)
                grad_attend = nt(values, grads)
                grad_scores = (
                    probs * (grad_attend - center_ref[g, 0:1, pl.ds(at, block)])
                ).astype(jnp.bfloat16)
                grad_values = grad_values + nn(probs.astype(jnp.bfloat16), grads)
                grad_keys = grad_keys + nn(grad_scores, queries)
                query_sums_ref[g, pl.ds(at, block), :] += tn(grad_scores, keys)
            return grad_keys, grad_values

        zero = jnp.zeros((block, size), jnp.float32)
        first = jnp.where(j < whole, jnp.minimum(j + 1, blocks), blocks)
        carry = lax.fori_loop(j, first, lambda i, c: step(i, c, True), (zero, zero))
        grad_keys, grad_values = lax.fori_loop(
            first, blocks, lambda i, c: step(i, c, False), carry
        )
        key_sums_ref[pl.ds(start, block), :] = grad_keys
        grad_raw_ref[pl.ds(start, block), value_lanes] = grad_values.astype(grad_raw_ref.dtype)
        return 0

    lax.fori_loop(0, some, key_block, 0)

    def padding(j, _):
        start = pl.multiple_of(j * block, block)
        key_sums_ref[pl.ds(start, block), :] = jnp.zeros((block, size), jnp.float32)
        grad_raw_ref[pl.ds(start, block), value_lanes] = jnp.zeros(
            (block, size), grad_raw_ref.dtype
        )
        return 0

    lax.fori_loop(some, blocks, padding, 0)

    def head_back(i, carry):
        rows = pl.ds(pl.multiple_of(i * block, block), block)
        cosine, sine_table = cosine_ref[rows, :], sine_ref[rows, :]
        sums = list(carry)
        for g in range(groups + 1):
            lanes = slice(g * size, (g + 1) * size)
            if g < groups:
                grad = query_sums_ref[g, rows, :] * size**-0.5
            else:
                grad = key_sums_ref[rows, :] * (1.0 / math.log2(math.e))
            which = 0 if g < groups else 1
            grad = grad.astype(jnp.bfloat16).astype(jnp.float32)
            grad = grad * cosine - pltpu.roll(grad, size // 2, 1) * sine_table
            value = raw_ref[rows, lanes]
            scale = lax.rsqrt(jnp.mean(value * value, axis=-1, keepdims=True) + EPS)
            unit = value * scale
            sums[which] = sums[which] + jnp.sum(grad * unit, axis=0, keepdims=True)
            grad = grad * head_gain_ref[which : which + 1, :]
            inner = jnp.mean(grad * unit, axis=-1, keepdims=True)
            grad_raw_ref[rows, lanes] = (scale * (grad - unit * inner)).astype(grad_raw_ref.dtype)
        return tuple(sums)

    zero = jnp.zeros((1, size), jnp.float32)
    sums = lax.fori_loop(0, blocks, head_back, (zero, zero))
    gain_ref[0, 0:1, :] = sums[0]
    gain_ref[0, 1:2, :] = sums[1]


def attend_backward(
    place, heads, raw, cosine, sine_table, head_gains, groups, context, totals, pieces
):
    count = len(pieces)
    positions = heads.shape[0]
    rows = positions // count
    block = min(512, positions)
    size = HEAD_SIZE
    kv_count = heads.shape[1] // ((groups + 2) * size)

    def of_group(lines, columns):
        return pl.BlockSpec((lines, columns * size), lambda h, s: (0, h))

    width = kv_count * groups * size
    return pl.pallas_call(
        functools.partial(backward_kernel, block, groups, positions, count),
        grid_spec=pltpu.PrefetchScalarGridSpec(
            num_scalar_prefetch=1,
            grid=(kv_count,),
            in_specs=[
                of_group(positions, groups + 2),
                of_group(positions, groups + 1),
                fixed(cosine.shape),
                fixed(sine_table.shape),
                fixed(head_gains.shape),
                pl.BlockSpec((count, rows, groups * size), lambda h, s: (0, 0, h)),
                pl.BlockSpec((groups, 8, positions), lambda h, s: (h, 0, 0)),
            ]
            + [of_group(rows, groups)] * count,
            out_specs=[
                of_group(positions, groups + 2),
                pl.BlockSpec((1, 2, size), lambda h, s: (h, 0, 0)),
            ],
            scratch_shapes=[
                pltpu.VMEM((groups, positions, size), jnp.float32),
                pltpu.VMEM((positions, size), jnp.float32),
                pltpu.VMEM((groups, 8, positions), jnp.float32),
                pltpu.VMEM((positions, groups * size), jnp.bfloat16),
            ],
        ),
        out_shape=(
            jax.ShapeDtypeStruct(heads.shape, jnp.bfloat16),
            jax.ShapeDtypeStruct((kv_count, 2, size), jnp.float32),
        ),
        compiler_params=arbitrary(1, 56),
        cost_estimate=cost(
            positions * positions * width,
            2 * positions * width,
            positions * positions * width // size // 20,
        ),
        name="attend_backward",
    )(
        place,
        heads,
        raw,
        cosine,
        sine_table,
        head_gains,
        context,
        totals,
        *pieces,
    )


def tile_of(hidden_units):
    return next(t for t in (512, 384, 256, 128) if hidden_units % t == 0)


def separate(both, tile):
    pieces = [both[:, at : at + tile] for at in range(0, both.shape[1], tile)]
    return jnp.concatenate(pieces[0::2], axis=1), jnp.concatenate(pieces[1::2], axis=1)


def out_norm_kernel(count, weight_ref, rows_ref, gain_ref, *refs):
    resid_ref, normed_ref = refs[count:]
    part = refs[0].shape[-1]
    resid = rows_ref[...].astype(jnp.float32)
    for k in range(count):
        at = (count - k) % count * part
        resid = resid + nn(refs[k][...], weight_ref[at : at + part, :])
    resid_ref[...] = resid
    normed_ref[...] = norm_rows(resid, gain_ref[...]).astype(normed_ref.dtype)


def out_norm(pieces, weight, tokens, gain):
    count = len(pieces)
    rows, part = pieces[0].shape
    width = weight.shape[1]
    block = min(256, rows)
    across = pl.BlockSpec((block, width), lambda i: (i, 0))
    return pl.pallas_call(
        functools.partial(out_norm_kernel, count),
        grid=(rows // block,),
        in_specs=[fixed(weight.shape), across, fixed(gain.shape)]
        + [pl.BlockSpec((block, part), lambda i: (i, 0))] * count,
        out_specs=[across, across],
        out_shape=(
            jax.ShapeDtypeStruct((rows, width), jnp.float32),
            jax.ShapeDtypeStruct((rows, width), jnp.bfloat16),
        ),
        compiler_params=arbitrary(1, 48),
        cost_estimate=cost(2 * rows * count * part * width, 2 * weight.size + 10 * rows * width),
        name="out_norm",
    )(weight, tokens, gain, *pieces)


def hidden_kernel(tile, own_ref, away_ref, weight_ref, *refs):
    both_ref, hidden_ref = refs[-2:]
    rows = own_ref.shape[0]
    for half, rows_ref in enumerate((own_ref, away_ref)):
        here = slice(half * rows, (half + 1) * rows)
        both = nn(rows_ref[...], weight_ref[...])
        both_ref[here, :] = both
        gate, up = both[:, :tile], both[:, tile:]
        hidden_ref[here, :] = (gate * jax.nn.sigmoid(gate) * up).astype(hidden_ref.dtype)


def hidden_units(own, away, weight, tile, at, total, before):
    rows, width = own.shape
    columns = weight.shape[1]
    tiles = columns // (2 * tile)
    in_specs = [
        fixed(own.shape),
        fixed(away.shape),
        pl.BlockSpec((width, 2 * tile), lambda j: (0, j)),
    ]
    args, aliases = [own, away, weight], {}
    if before is not None:
        in_specs.append(pl.BlockSpec(memory_space=pl.ANY))
        args.append(before)
        aliases = {3: 1}
    return pl.pallas_call(
        functools.partial(hidden_kernel, tile),
        grid=(tiles,),
        in_specs=in_specs,
        out_specs=[
            pl.BlockSpec((2 * rows, 2 * tile), lambda j: (0, j)),
            pl.BlockSpec((2 * rows, tile), lambda j: (0, at * tiles + j)),
        ],
        out_shape=(
            jax.ShapeDtypeStruct((2 * rows, columns), jnp.float32),
            jax.ShapeDtypeStruct((2 * rows, total), jnp.bfloat16),
        ),
        input_output_aliases=aliases,
        compiler_params=arbitrary(1, 56),
        cost_estimate=cost(4 * rows * width * columns, 2 * width * columns + 10 * rows * columns),
        name="hidden_units",
    )(*args)


def hidden_back_kernel(tile, own_ref, away_ref, down_ref, both_ref, out_ref):
    rows = own_ref.shape[0]
    for half, grads_ref in enumerate((own_ref, away_ref)):
        here = slice(half * rows, (half + 1) * rows)
        grad_hidden = nt(grads_ref[...], down_ref[...])
        gate, up = both_ref[here, :tile], both_ref[here, tile:]
        sigmoid = jax.nn.sigmoid(gate)
        silu = gate * sigmoid
        out_ref[here, :tile] = (grad_hidden * up * (sigmoid + silu * (1.0 - sigmoid))).astype(
            out_ref.dtype
        )
        out_ref[here, tile:] = (grad_hidden * silu).astype(out_ref.dtype)


def hidden_back(own, away, down, both, tile):
    rows, width = own.shape
    columns = both.shape[1]
    pair = pl.BlockSpec((2 * rows, 2 * tile), lambda j: (0, j))
    return pl.pallas_call(
        functools.partial(hidden_back_kernel, tile),
        grid=(columns // (2 * tile),),
        in_specs=[
            fixed(own.shape),
            fixed(away.shape),
            pl.BlockSpec((tile, width), lambda j: (j, 0)),
            pair,
        ],
        out_specs=pair,
        out_shape=jax.ShapeDtypeStruct((2 * rows, columns), jnp.bfloat16),
        compiler_params=arbitrary(1, 56),
        cost_estimate=cost(2 * rows * width * columns, width * columns + 12 * rows * columns),
        name="hidden_back",
    )(own, away, down, both)


def unit_grads_kernel(own_ref, away_ref, grads_ref, out_ref):
    rows = own_ref.shape[0]
    out_ref[...] = (
        tn(own_ref[...], grads_ref[:rows, :]) + tn(away_ref[...], grads_ref[rows:, :])
    ).astype(out_ref.dtype)


def unit_grads(own, away, grads):
    rows, width = own.shape
    columns = grads.shape[1]
    tile = tile_of(columns)
    return pl.pallas_call(
        unit_grads_kernel,
        grid=(columns // tile,),
        in_specs=[
            fixed(own.shape),
            fixed(away.shape),
            pl.BlockSpec((2 * rows, tile), lambda j: (0, j)),
        ],
        out_specs=pl.BlockSpec((width, tile), lambda j: (0, j)),
        out_shape=jax.ShapeDtypeStruct((width, columns), jnp.bfloat16),
        compiler_params=arbitrary(1, 56),
        cost_estimate=cost(4 * rows * width * columns, 2 * width * columns + 4 * rows * columns),
        name="unit_grads",
    )(own, away, grads)


def down_grads_kernel(hidden_ref, own_ref, away_ref, out_ref):
    rows = own_ref.shape[0]
    out_ref[...] = (
        tn(hidden_ref[:rows, :], own_ref[...]) + tn(hidden_ref[rows:, :], away_ref[...])
    ).astype(out_ref.dtype)


def down_grads(hidden, own, away):
    rows, width = own.shape
    units = hidden.shape[1]
    tile = tile_of(units)
    return pl.pallas_call(
        down_grads_kernel,
        grid=(units // tile,),
        in_specs=[
            pl.BlockSpec((2 * rows, tile), lambda j: (0, j)),
            fixed(own.shape),
            fixed(away.shape),
        ],
        out_specs=pl.BlockSpec((tile, width), lambda j: (j, 0)),
        out_shape=jax.ShapeDtypeStruct((units, width), jnp.bfloat16),
        compiler_params=arbitrary(1, 56),
        cost_estimate=cost(4 * rows * width * units, 2 * width * units + 4 * rows * units),
        name="down_grads",
    )(hidden, own, away)


def grad_normed_kernel(parts, *refs):
    grads, weights = refs[:parts], refs[parts : 2 * parts]
    own_ref, away_ref = refs[2 * parts :]
    rows = own_ref.shape[0]
    for half, out_ref in enumerate((own_ref, away_ref)):
        here = slice(half * rows, (half + 1) * rows)
        total = nt(grads[0][here, :], weights[0][...])
        for grad_ref, weight_ref in zip(grads[1:], weights[1:]):
            total = total + nt(grad_ref[here, :], weight_ref[...])
        out_ref[...] = total.astype(out_ref.dtype)


def grad_normed(grads, weights):
    rows = grads[0].shape[0] // 2
    width = weights[0].shape[0]
    tile = tile_of(width)
    return pl.pallas_call(
        functools.partial(grad_normed_kernel, len(grads)),
        grid=(width // tile,),
        in_specs=[fixed(grad.shape) for grad in grads]
        + [pl.BlockSpec((tile, weight.shape[1]), lambda j: (j, 0)) for weight in weights],
        out_specs=[pl.BlockSpec((rows, tile), lambda j: (0, j))] * 2,
        out_shape=(
            jax.ShapeDtypeStruct((rows, width), jnp.float32),
            jax.ShapeDtypeStruct((rows, width), jnp.bfloat16),
        ),
        compiler_params=arbitrary(1, 60),
        cost_estimate=cost(
            sum(2 * grad.size * width for grad in grads),
            sum(2 * grad.size + 2 * weight.size for grad, weight in zip(grads, weights)),
        ),
        name="grad_normed",
    )(*grads, *weights)


def mlp_out_kernel(hidden_ref, *refs):
    own_ref, away_ref = refs[-2:]
    rows = own_ref.shape[0]
    for half, out_ref in enumerate((own_ref, away_ref)):
        here = slice(half * rows, (half + 1) * rows)
        at, total = 0, None
        for down_ref in refs[:-2]:
            units = down_ref.shape[0]
            part = nn(hidden_ref[here, at : at + units], down_ref[...])
            total = part if total is None else total + part
            at += units
        out_ref[...] = total.astype(out_ref.dtype)


def mlp_out(hidden, downs):
    rows = hidden.shape[0] // 2
    width = downs[0].shape[1]
    tile = tile_of(width)
    return pl.pallas_call(
        mlp_out_kernel,
        grid=(width // tile,),
        in_specs=[fixed(hidden.shape)]
        + [pl.BlockSpec((down.shape[0], tile), lambda j: (0, j)) for down in downs],
        out_specs=[pl.BlockSpec((rows, tile), lambda j: (0, j))] * 2,
        out_shape=(
            jax.ShapeDtypeStruct((rows, width), jnp.float32),
            jax.ShapeDtypeStruct((rows, width), jnp.bfloat16),
        ),
        compiler_params=arbitrary(1, 56),
        cost_estimate=cost(2 * hidden.size * width, 4 * hidden.size + 6 * rows * width),
        name="mlp_out",
    )(hidden, *downs)


def resid_back_kernel(
    place_ref,
    own_ref,
    away_ref,
    resid_ref,
    cotangent_ref,
    gain_ref,
    weight_ref,
    grad_ref,
    low_ref,
    sums_ref,
    *piece_refs,
):
    block = own_ref.shape[0]
    part = piece_refs[0].shape[-1]
    first = place_ref[1] + pl.program_id(0) * block
    at = first + lax.broadcasted_iota(jnp.int32, (block, 1), 0)
    valid = (at < place_ref[0]).astype(jnp.float32)
    grads = own_ref[...] + away_ref[...].astype(jnp.float32)
    back, sums = norm_back(resid_ref[...], gain_ref[...], grads)
    grad_resid = valid * cotangent_ref[...].astype(jnp.float32) + back
    grad_ref[...] = grad_resid
    low = grad_resid.astype(jnp.bfloat16)
    low_ref[...] = low
    for k, piece_ref in enumerate(piece_refs):
        piece_ref[...] = nt(low, weight_ref[k * part : (k + 1) * part, :]).astype(piece_ref.dtype)

    @pl.when(pl.program_id(0) == 0)
    def _():
        sums_ref[...] = jnp.zeros_like(sums_ref)

    sums_ref[...] += sums


def resid_back(own, away, resid, cotangent, gain, weight, length, start, count):
    rows, width = own.shape
    part = weight.shape[0] // count
    block = min(256, rows)
    across = pl.BlockSpec((block, width), lambda i, s: (i, 0))
    return pl.pallas_call(
        resid_back_kernel,
        grid_spec=pltpu.PrefetchScalarGridSpec(
            num_scalar_prefetch=1,
            grid=(rows // block,),
            in_specs=[across] * 4 + [fixed(gain.shape), fixed(weight.shape)],
            out_specs=[across, across, fixed(gain.shape)]
            + [pl.BlockSpec((block, part), lambda i, s: (i, 0))] * count,
        ),
        out_shape=(
            jax.ShapeDtypeStruct((rows, width), jnp.float32),
            jax.ShapeDtypeStruct((rows, width), jnp.bfloat16),
            jax.ShapeDtypeStruct(gain.shape, jnp.float32),
        )
        + (jax.ShapeDtypeStruct((rows, part), jnp.bfloat16),) * count,
        compiler_params=arbitrary(1, 56),
        cost_estimate=cost(2 * rows * weight.size, 2 * weight.size + 20 * rows * width),
        name="resid_back",
    )(jnp.stack([length, start]), own, away, resid, cotangent, gain, weight)


def out_grads_kernel(count, grads_ref, *refs):
    out_ref = refs[count]
    part = refs[0].shape[-1]
    for k in range(count):
        at = (count - k) % count * part
        out_ref[at : at + part, :] = tn(refs[k][...], grads_ref[...]).astype(out_ref.dtype)


def out_grads(pieces, grads):
    count = len(pieces)
    rows, part = pieces[0].shape
    width = grads.shape[1]
    tile = tile_of(width)
    return pl.pallas_call(
        functools.partial(out_grads_kernel, count),
        grid=(width // tile,),
        in_specs=[pl.BlockSpec((rows, tile), lambda j: (0, j))]
        + [fixed(piece.shape) for piece in pieces],
        out_specs=pl.BlockSpec((count * part, tile), lambda j: (0, j)),
        out_shape=jax.ShapeDtypeStruct((count * part, width), jnp.bfloat16),
        compiler_params=arbitrary(1, 48),
        cost_estimate=cost(
            2 * rows * count * part * width, 2 * count * part * (rows + width) + 2 * rows * width
        ),
        name="out_grads",
    )(grads, *pieces)


def pack_heads_kernel(groups, query_ref, key_ref, value_ref, gain_ref, out_ref):
    size = HEAD_SIZE
    at = 0
    for h in range(key_ref.shape[1] // size):
        for ref, start, columns in (
            (query_ref, h * groups * size, groups * size),
            (key_ref, h * size, size),
            (value_ref, h * size, size),
        ):
            out_ref[:, at : at + columns] = ref[:, start : start + columns]
            at += columns
    out_ref[:, at:] = gain_ref[...]


def pack_heads(query, key, value, gain, groups):
    rows = query.shape[0]
    columns = query.shape[1] + key.shape[1] + value.shape[1] + gain.shape[1]
    args = (query, key, value, gain)
    return pl.pallas_call(
        functools.partial(pack_heads_kernel, groups),
        grid=(1,),
        in_specs=[fixed(arg.shape) for arg in args],
        out_specs=fixed((rows, columns)),
        out_shape=jax.ShapeDtypeStruct((rows, columns), jnp.bfloat16),
        compiler_params=arbitrary(1, 16),
        cost_estimate=cost(0, 4 * rows * columns),
        name="pack_heads",
    )(*args)


def pack_units_kernel(tile, gate_ref, up_ref, out_ref):
    for at in range(0, gate_ref.shape[1], tile):
        out_ref[:, 2 * at : 2 * at + tile] = gate_ref[:, at : at + tile]
        out_ref[:, 2 * at + tile : 2 * at + 2 * tile] = up_ref[:, at : at + tile]


def pack_units(gate, up, tile):
    rows, columns = gate.shape
    return pl.pallas_call(
        functools.partial(pack_units_kernel, tile),
        grid=(1,),
        in_specs=[fixed(gate.shape), fixed(up.shape)],
        out_specs=fixed((rows, 2 * columns)),
        out_shape=jax.ShapeDtypeStruct((rows, 2 * columns), jnp.bfloat16),
        compiler_params=arbitrary(1, 16),
        cost_estimate=cost(0, 8 * rows * columns),
        name="pack_units",
    )(gate, up)


def heads_back_kernel(normed_ref, grad_ref, weight_ref, out_ref, sums_ref):
    partial = tn(normed_ref[...], grad_ref[...])
    out_ref[...] = partial.astype(out_ref.dtype)
    sums = jnp.sum(partial * weight_ref[...].astype(jnp.float32), axis=1, keepdims=True)
    sums_ref[...] = jnp.broadcast_to(sums, sums_ref.shape)


def heads_back(normed, grads, weight):
    positions, width = normed.shape
    columns = grads.shape[1]
    block = min(512, width)
    return pl.pallas_call(
        heads_back_kernel,
        grid=(width // block,),
        in_specs=[
            pl.BlockSpec((positions, block), lambda j: (0, j)),
            pl.BlockSpec((positions, columns), lambda j: (0, 0)),
            pl.BlockSpec((block, columns), lambda j: (j, 0)),
        ],
        out_specs=[
            pl.BlockSpec((block, columns), lambda j: (j, 0)),
            pl.BlockSpec((block, LANES), lambda j: (j, 0)),
        ],
        out_shape=(
            jax.ShapeDtypeStruct((width, columns), jnp.bfloat16),
            jax.ShapeDtypeStruct((width, LANES), jnp.float32),
        ),
        compiler_params=arbitrary(1, 48),
        cost_estimate=cost(
            2 * positions * width * columns, 2 * positions * (width + columns) + 4 * width * columns
        ),
        name="heads_back",
    )(normed, grads, weight)


def norm_back(value_rows, gain, grads):
    scale = lax.rsqrt(jnp.mean(value_rows * value_rows, axis=-1, keepdims=True) + EPS)
    unit = value_rows * scale
    scaled = grads * gain
    inner = jnp.mean(scaled * unit, axis=-1, keepdims=True)
    return scale * (scaled - unit * inner), jnp.sum(grads * unit, axis=0)


def after(value, *others):
    return lax.optimization_barrier((value, others))[0]


def hop_right(value, count, hop):
    return lax.ppermute(value, "seq", [(i, i + 1) for i in range(hop - 1, count - 1)])


def hop_left(value, count, hop):
    return lax.ppermute(value, "seq", [(i, i - 1) for i in range(1, count - hop + 1)])


def line_scatter(parts, first_before=()):
    count = len(parts)
    right, left = None, None
    for hop in range(count - 1):
        to_right, to_left = parts[count - 1 - hop], parts[hop + 1]
        if hop:
            to_right, to_left = to_right + right, to_left + left
        if hop == 1:
            to_right, to_left = after((to_right, to_left), *first_before)
        right = lax.ppermute(
            to_right.astype(jnp.bfloat16), "seq", [(i, i + 1) for i in range(hop + 1)]
        ).astype(jnp.float32)
        left = lax.ppermute(
            to_left.astype(jnp.bfloat16),
            "seq",
            [(i, i - 1) for i in range(count - 1 - hop, count)],
        ).astype(jnp.float32)
    return parts[0] + right + left


def sum_over(value, axis):
    flat = value.reshape(-1, LANES)
    size = lax.axis_size(axis)
    assert size & (size - 1) == 0
    step = 1
    while step < size:
        flat = flat + lax.ppermute(flat, axis, [(i, i ^ step) for i in range(size)])
        step *= 2
    return flat.reshape(-1)


def swap(value, count):
    return lax.ppermute(value, "seq", [(i, i ^ 1) for i in range(count)])


def fetch(value, count, step):
    return lax.ppermute(value, "seq", [((i + step) % count, i) for i in range(count)])


def give(value, count, step):
    return lax.ppermute(value, "seq", [(i, (i + step) % count) for i in range(count)])


def on_device(
    tokens,
    lengths,
    cotangent,
    w_query,
    key_weight,
    value_weight,
    w_out,
    w_gate,
    w_up,
    w_down,
    norm_attn,
    norm_mlp,
    norm_query,
    norm_key,
):
    slots, rows, width = tokens.shape
    assert slots == 1
    count = lax.axis_size("seq")
    positions = count * rows
    me = lax.axis_index("seq")
    tokens_low = tokens.reshape(rows, width)
    cotangent_low = cotangent.reshape(rows, width)
    length = lengths[0]
    low = jnp.bfloat16
    groups = w_query.shape[1] // key_weight.shape[1]
    kv_count = key_weight.shape[1] // HEAD_SIZE
    units = w_gate.shape[1]
    tile = tile_of(units)
    steps = range(0, count, PAIR)

    def from_groups(both):
        size = HEAD_SIZE
        starts = [h * (groups + 2) * size for h in range(kv_count)]
        ends = (0, groups * size, (groups + 1) * size, (groups + 2) * size)
        return [
            jnp.concatenate([both[:, s + low_end : s + high_end] for s in starts], axis=1)
            for low_end, high_end in zip(ends, ends[1:])
        ]

    weight_rows = w_query.shape[0]
    gain_parts = (norm_attn, norm_mlp, norm_query, norm_key)
    gain_sizes = [part.shape[0] for part in gain_parts]
    own_gains = jnp.concatenate(gain_parts)
    gain_block = jnp.pad(own_gains, (0, weight_rows * LANES - own_gains.shape[0])).reshape(
        weight_rows, LANES
    )
    own_heads = pack_heads(w_query, key_weight, value_weight, gain_block, groups)
    head_columns = own_heads.shape[1] - LANES
    gathered_heads = lax.all_gather(own_heads, "dp", axis=0, tiled=True)
    heads_weight = gathered_heads[:, :head_columns]
    gathered_gains = gathered_heads[:, head_columns:].reshape(-1, weight_rows * LANES)
    rights = [hop_right(tokens_low, count, 1)]
    lefts = [hop_left(tokens_low, count, 1)]
    gains, at = [], 0
    for part_size in gain_sizes:
        gains.append(gathered_gains[:, at : at + part_size].reshape(1, -1).astype(jnp.float32))
        at += part_size
    gain_attn, gain_mlp = gains[:2]
    head_gains = jnp.concatenate(gains[2:], axis=0)
    cosine, sine_table = angles(jnp.arange(positions, dtype=jnp.float32))

    places = [
        jnp.stack([lax.rem(me + k, count), (me + k < count).astype(jnp.int32)])
        for k in range(count)
    ]
    slot_place = jnp.stack([length, me])

    def project_block(k, whole):
        first, second = tokens_low, tokens_low
        if k:
            first, second = lefts[k - 1], rights[count - k - 1]
        return project(
            places[k],
            first,
            second,
            gain_attn,
            heads_weight,
            cosine,
            sine_table,
            head_gains,
            groups,
            whole,
            count,
        )

    own_both = pack_units(w_gate, w_up, tile)
    first_hop = (rights[0], lefts[0])
    both_weights = [lax.all_gather(after(own_both, *first_hop), "dp", axis=0, tiled=True)]
    down_weights = [lax.all_gather(after(w_down, *first_hop), "dp", axis=1, tiled=True)]
    whole = project_block(0, None)
    for hop in range(2, count - 1):
        rights.append(hop_right(rights[-1], count, hop))
        lefts.append(hop_left(lefts[-1], count, hop))
    right, left = after((rights[-1], lefts[-1]), whole[1])
    out_blocks = [w_out] + [
        fetch(after(w_out, rights[-1], lefts[-1]), count, k) for k in range(1, count)
    ]
    rights.append(hop_right(right, count, count - 1))
    lefts.append(hop_left(left, count, count - 1))
    for k in range(2, count - 1):
        whole = project_block(k, whole)
    gathered = (rights[-1], lefts[-1])
    out_weight = lax.all_gather(
        after(
            jnp.concatenate(out_blocks, axis=0), both_weights[0], down_weights[0], *gathered
        ),
        "dp",
        axis=1,
        tiled=True,
    )

    fetched_both = [
        fetch(after(own_both, whole[1], *gathered), count, step) for step in steps[1:]
    ]
    for k in [1, count - 1] if count > 2 else [1]:
        whole = project_block(k, whole)
    normed_attn, heads, raw = whole
    context, totals = attend_forward(slot_place, heads, groups, count)
    sent = after(context, *fetched_both)
    context_pieces = [context[0]] + [give(sent[k], count, k) for k in range(1, count)]
    fetched_down = [fetch(after(w_down, *context_pieces[1:]), count, step) for step in steps[1:]]
    resid, normed_mlp = out_norm(context_pieces, out_weight, tokens_low, gain_mlp)
    away_normed = swap(normed_mlp, count)
    for both, down in zip(fetched_both, fetched_down):
        both_weights.append(lax.all_gather(after(both, context), "dp", axis=0, tiled=True))
        down_weights.append(lax.all_gather(after(down, away_normed), "dp", axis=1, tiled=True))

    place = jnp.arange(rows, dtype=jnp.int32)[:, None] + me * rows
    valid_rows = (place < length).astype(low)
    grad_rows = cotangent_low * valid_rows
    away_grads = swap(after(grad_rows, away_normed), count)
    hidden, boths = None, []
    for at, weight in enumerate(both_weights):
        both, hidden = hidden_units(
            normed_mlp, away_normed, weight, tile, at, len(steps) * units, hidden
        )
        boths.append(both)

    def spread(partial, axis):
        return lax.psum_scatter(partial, "dp", scatter_dimension=axis, tiled=True)

    mlp_own, mlp_away = mlp_out(hidden, down_weights)
    mlp_away = swap(after(mlp_away, away_grads), count)
    hidden = after(hidden, mlp_own)
    down_partial = down_grads(hidden, grad_rows, away_grads)
    grad_rows, away_grads = after((grad_rows, away_grads), down_partial)
    down_sums = spread(down_partial, 1)
    grad_boths = [
        hidden_back(grad_rows, away_grads, down, both, tile)
        for down, both in zip(down_weights, boths)
    ]
    mate_partials = [unit_grads(normed_mlp, away_normed, grad) for grad in grad_boths[1:]]
    mate_sums = [spread(partial, 0) for partial in mate_partials]
    grad_normed_own, grad_normed_away = grad_normed(
        after(grad_boths, *mate_partials), both_weights
    )
    own_partial = unit_grads(normed_mlp, away_normed, grad_boths[0])
    own_sum = spread(own_partial, 0)
    grad_resid, grad_attn_low, gain_mlp_sums, *pieces = resid_back(
        grad_normed_own,
        after(swap(after(grad_normed_away, mlp_away), count), own_partial),
        resid,
        cotangent_low,
        gain_mlp,
        out_weight,
        length,
        me * rows,
        count,
    )
    pieces = [pieces[0]] + [give(pieces[k], count, k) for k in range(1, count)]
    out_partial = out_grads(context_pieces, grad_attn_low)
    out_sums = spread(out_partial, 1)
    pieces = after(pieces, out_partial, down_sums, *mate_sums)
    grad_raw, head_gain_terms = attend_backward(
        slot_place,
        heads,
        raw,
        cosine,
        sine_table,
        head_gains,
        groups,
        context,
        totals,
        pieces,
    )
    given_both = [give(piece, count, step) for step, piece in zip(steps[1:], mate_sums)]
    down_pieces = jnp.split(down_sums, len(steps), axis=0)
    given_down = [give(piece, count, step) for step, piece in zip(steps[1:], down_pieces[1:])]
    grad_raw = after(grad_raw, *given_down)
    shares = [
        nt(
            lax.dynamic_slice_in_dim(grad_raw, lax.rem(me + k, count) * rows, rows, 0),
            heads_weight,
        )
        for k in range(count)
    ]
    heads_partial, gain_attn_sums = heads_back(
        normed_attn, after(grad_raw, shares[1], shares[-1]), heads_weight
    )
    grad_heads = spread(heads_partial, 0)
    grad_normed_attn = line_scatter(shares, (heads_partial, *given_both))
    grad_heads = grad_heads.astype(jnp.float32)
    grad_query, grad_key, grad_value = from_groups(grad_heads)
    layer_output = (
        (valid_rows.astype(jnp.float32) * (resid + mlp_own + mlp_away.astype(jnp.float32)))
        .astype(low)
        .reshape(slots, rows, width)
    )
    grad_input_norm = norm_back(tokens_low.astype(jnp.float32), gain_attn, grad_normed_attn)[0]
    grad_tokens = (grad_resid + grad_input_norm).astype(low).reshape(slots, rows, width)
    gain_attn_term = gain_attn_sums[:, 0] / gain_attn[0]

    out_parts = [
        give(part, count, k) if k else part for k, part in enumerate(jnp.split(out_sums, count))
    ]
    grad_out = sum(part.astype(jnp.float32) for part in out_parts)
    both_total = sum([part.astype(jnp.float32) for part in [own_sum, *given_both]])
    grad_gate, grad_up = separate(both_total, tile)
    grad_down = sum([part.astype(jnp.float32) for part in [down_pieces[0], *given_down]])

    head_gain_sums = jnp.sum(head_gain_terms, axis=0)
    terms = (gain_attn_term, gain_mlp_sums[0], head_gain_sums[0], head_gain_sums[1])
    sums = sum_over(jnp.concatenate(terms), "dp")
    sums = sum_over(after(sums, grad_normed_attn), "seq")
    gain_grads, at = [], 0
    for term, part_size in zip(terms, gain_sizes):
        gain_grads.append(
            lax.dynamic_slice_in_dim(
                sums[at : at + term.shape[0]], lax.axis_index("dp") * part_size, part_size, 0
            )
        )
        at += term.shape[0]
    return (
        layer_output,
        grad_tokens,
        grad_query,
        grad_key,
        grad_value,
        grad_out,
        grad_gate,
        grad_up,
        grad_down,
        *gain_grads,
    )


def solution(mesh):
    return jax.shard_map(
        on_device,
        mesh=mesh,
        in_specs=(
            P("dp", "seq", None),
            P("dp"),
            P("dp", "seq", None),
            P("dp", "seq"),
            P("dp", "seq"),
            P("dp", "seq"),
            P("seq", "dp"),
            P("dp", "seq"),
            P("dp", "seq"),
            P("seq", "dp"),
            P("dp"),
            P("dp"),
            P("dp"),
            P("dp"),
        ),
        out_specs=(
            P("dp", "seq", None),
            P("dp", "seq", None),
            P("dp", "seq"),
            P("dp", "seq"),
            P("dp", "seq"),
            P("seq", "dp"),
            P("dp", "seq"),
            P("dp", "seq"),
            P("seq", "dp"),
            P("dp"),
            P("dp"),
            P("dp"),
            P("dp"),
        ),
        check_vma=False,
    )
```

time: 1460 us -> 1050 us (0.72)
  Pallas kernels: 65.3 us -> 336 us
  matrix products: 254 us -> 30.3 us
  other arithmetic: 200 us -> 43.6 us
  starting transfers between devices: 186 us -> 86.1 us
  waiting for transfers between devices: 564 us -> 486 us
  blocking collectives: 74.8 us -> 0 us
  local copies, waits for them, and re-layouts: 85.6 us -> 41.5 us
    pallas_call x0 -> x19, Pallas kernels: none -> 260 us  [the longest x2 40.1 us: hidden_units(): pl.pallas_call(functools.partial(hidden_kernel, tile), grid=(tiles,), in_...]
    dot_general x10 -> x0, matrix products: 168 us -> none  [the longest x5 84.9 us: nn(): lax.dot_general(left, right, (((1,), (0,)), ((), ())), preferred_element_...]
    ppermute x3 -> x11, waiting for transfers between devices: 58.5 us -> 171 us  [give(): lax.ppermute(value, 'seq', [(i, (i + step) % count) for i in range(count)])]
    ppermute x4, waiting for transfers between devices: 114 us -> 28.3 us  [swap(): return lax.ppermute(value, 'seq', [(i, i ^ 1) for i in range(count)])]
    ppermute x6 -> x3, starting transfers between devices: 112 us -> 26.4 us  [line_scatter(): lax.ppermute(to_right.astype(jnp.bfloat16), 'seq', [(i, i + 1) for i in r...]
    reduce_sum x9 -> x3, other arithmetic: 85.6 us -> 4.02 us  [the longest x1 3.53 us: norm_back(): inner = jnp.mean(scaled * unit, axis=-1, keepdims=True)]
    all_to_all x2 -> x0, waiting for transfers between devices: 78.3 us -> none  [the longest x1 42.8 us: on_device(): lax.all_to_all(context, 'seq', split_axis=0, concat_axis=1, tiled=True)]
    ppermute x3 -> x5, waiting for transfers between devices: 68.9 us -> 139 us  [fetch(): lax.ppermute(value, 'seq', [((i + step) % count, i) for i in range(count)])]
  transfers between devices with their start and end apart: 46 -> 48, of which waited for: 22 -> 21; matrix products, arithmetic and copies ran while one was open for 30% -> 8% of each run, Pallas kernels for 5% -> 30%
where the time goes in v2:
time: 1050 us; the launch traced here: 1040 us
  waiting for transfers between devices  486 us (46%)
  Pallas kernels  336 us (32%)
  starting transfers between devices  86.1 us (8%)
  other arithmetic  43.6 us (4%)
  local copies, waits for them, and re-layouts  41.5 us (4%)
  matrix products  30.3 us (3%)
  between operations  15.4 us (1%)
    ppermute x11, waiting for transfers between devices, give(): lax.ppermute(value, 'seq', [(i, (i + step) % count) for i in range(count)])  171 us
    ppermute x5, waiting for transfers between devices, fetch(): lax.ppermute(value, 'seq', [((i + step) % count, i) for i in range(count)])  139 us
    pallas_call x1, Pallas kernels, attend_backward(): pl.pallas_call(functools.partial(backward_kernel, block, groups, position...  49.4 us
    ppermute x3, waiting for transfers between devices, hop_right(): lax.ppermute(value, 'seq', [(i, i + 1) for i in range(hop - 1, count - 1)])  43.8 us
    pallas_call x2, Pallas kernels, hidden_units(): pl.pallas_call(functools.partial(hidden_kernel, tile), grid=(tiles,), in_...  40.1 us
    pallas_call x2, Pallas kernels, unit_grads(): pl.pallas_call(unit_grads_kernel, grid=(columns // tile,), in_specs=[fixe...  37.5 us
    ppermute x3, waiting for transfers between devices, line_scatter(): lax.ppermute(to_right.astype(jnp.bfloat16), 'seq', [(i, i + 1) for i in r...  35.9 us
    pallas_call x1, Pallas kernels, grad_normed(): pl.pallas_call(functools.partial(grad_normed_kernel, len(grads)), grid=(w...  34.4 us
  transfers between devices with their start and end apart: 48, of which 21 were waited for; matrix products, arithmetic and copies ran while one was open for 8% of the time, Pallas kernels for 30%

profile of v2, /device:TPU:0, one launch (start us, length us, event | category | flops | bytes accessed | tf_op | source)
XLA Modules:
  0.0 1038.8 jit_solution(7114547258098577305)
XLA Ops:
  18.1 43.8 %collective-permute-done.second_ref = bf16[512,2048]{1,0:T(8,128)(2,1)S(1)} collective-permute-done((bf16[512,2048]{1,0:T(8,128)(2,1)}, bf16[512,2048]{1,0:T(8,128)(2,1)S(1)}, u32[]{:S(2)}, u32[]{:S(2)}) %collective-permute-start) | collective-permute-done | bytes 2097184 | tf_op jit(solution)/shard_map/ppermute | solution.py:862
  95.1 27.3 %collective-permute-done.3.first_ref = bf16[512,2048]{1,0:T(8,128)(2,1)} collective-permute-done((bf16[512,2048]{1,0:T(8,128)(2,1)}, bf16[512,2048]{1,0:T(8,128)(2,1)}, u32[]{:S(2)}, u32[]{:S(2)}) %collective-permute-start.3) | collective-permute-done | bytes 2097184 | tf_op jit(solution)/shard_map/ppermute | solution.py:866
  144.8 43.7 %collective-permute-done.4 = bf16[512,256]{1,0:T(8,128)(2,1)S(1)} collective-permute-done((bf16[512,256]{1,0:T(8,128)(2,1)S(1)}, bf16[512,256]{1,0:T(8,128)(2,1)S(1)}, u32[]{:S(2)}, u32[]{:S(2)}) %collective-permute-start.4) | collective-permute-done | bytes 262176 | tf_op jit(solution)/shard_map/ppermute | solution.py:905
  226.9 26.5 %attend_forward.1 = (bf16[4,512,512]{2,1,0:T(8,128)(2,1)S(1)}, f32[4,8,2048]{2,1,0:T(8,128)S(1)}) custom-call(s32[2]{0:T(128)S(1)} %pad_add_fusion.1.place_ref, bf16[2048,1024]{1,0:T(8,128)(2,1)} %copy-done.5), custom_call_target="tpu_custom_call" | custom-call | flops 429496736 | bytes 419430 | tf_op jit(solution)/shard_map/attend_forward/pallas_call | solution.py:216
  254.1 19.9 %collective-permute-done.9 = bf16[256,3072]{1,0:T(8,128)(2,1)} collective-permute-done((bf16[256,3072]{1,0:T(8,128)(2,1)}, bf16[256,3072]{1,0:T(8,128)(2,1)}, u32[]{:S(2)}, u32[]{:S(2)}) %collective-permute-start.9) | collective-permute-done | bytes 1572896 | tf_op jit(solution)/shard_map/ppermute | solution.py:905
  291.0 21.5 %collective-permute-done.11.refs_2_ = bf16[512,512]{1,0:T(8,128)(2,1)S(1)} collective-permute-done((bf16[512,512]{1,0:T(8,128)(2,1)S(1)}, bf16[512,512]{1,0:T(8,128)(2,1)S(1)}, u32[]{:S(2)}, u32[]{:S(2)}) %collective-permute-start.11) | collective-permute-done | bytes 524320 | tf_op jit(solution)/shard_map/ppermute | solution.py:909
  336.6 61.1 %collective-permute-done.14 = bf16[1536,256]{1,0:T(8,128)(2,1)} collective-permute-done((bf16[1536,256]{1,0:T(8,128)(2,1)S(1)}, bf16[1536,256]{1,0:T(8,128)(2,1)}, u32[]{:S(2)}, u32[]{:S(2)}) %collective-permute-start.14) | collective-permute-done | bytes 786464 | tf_op jit(solution)/shard_map/ppermute | solution.py:905
  402.7 19.6 %hidden_units.2 = (f32[1024,3072]{1,0:T(8,128)}, bf16[1024,3072]{1,0:T(8,128)(2,1)}) custom-call(bf16[512,2048]{1,0:T(8,128)(2,1)} %copy-done.12, bf16[512,2048]{1,0:T(8,128)(2,1)} %collective-permute-done.13.away_ref, bf16[2048,3072]{1,0:T(8,128)(2,1)} %all-gather.7.cloned.1.call-done.weight_ref.refs_2_), custom_call_target="tpu_custom_call" | custom-call | flops 644245120 | bytes 1415577 | tf_op jit(solution)/shard_map/hidden_units/pallas_call | solution.py:499
  422.3 20.4 %hidden_units.3 = (f32[1024,3072]{1,0:T(8,128)}, bf16[1024,3072]{1,0:T(8,128)(2,1)}) custom-call(bf16[512,2048]{1,0:T(8,128)(2,1)} %copy-done.12, bf16[512,2048]{1,0:T(8,128)(2,1)} %collective-permute-done.13.away_ref, bf16[2048,3072]{1,0:T(8,128)(2,1)} %all-gather.15.cloned.1.call-done.weight_ref.refs_3_, ...), custom_call_target="tpu_custom_call", output_to_operand_aliasing={{1}: (3, {})} | custom-call | flops 644245120 | bytes 1415577 | tf_op jit(solution)/shard_map/hidden_units/pallas_call | solution.py:499
  445.7 18.3 %mlp_out.1 = (f32[512,2048]{1,0:T(8,128)}, bf16[512,2048]{1,0:T(8,128)(2,1)}) custom-call(bf16[1024,3072]{1,0:T(8,128)(2,1)} %get-tuple-element.107.hidden_ref, bf16[1536,2048]{1,0:T(8,128)(2,1)} %all-gather.9.cloned.1.call-done.refs_0_.down_ref, bf16[1536,2048]{1,0:T(8,128)(2,1)} %all-gather.17.cloned.1.call-done.refs_1_.down_ref), custom_call_target="tpu_custom_call" | custom-call | flops 644245120 | bytes 943718 | tf_op jit(solution)/shard_map/mlp_out/pallas_call | solution.py:660
  463.9 18.2 %down_grads.1 = bf16[3072,2048]{1,0:T(8,128)(2,1)} custom-call(bf16[1024,3072]{1,0:T(8,128)(2,1)} %get-tuple-element.107.hidden_ref, bf16[512,2048]{1,0:T(8,128)(2,1)} %broadcast_multiply_fusion.own_ref, bf16[512,2048]{1,0:T(8,128)(2,1)} %collective-permute-done.15.away_ref), custom_call_target="tpu_custom_call" | custom-call | flops 644245120 | bytes 943718 | tf_op jit(solution)/shard_map/down_grads/pallas_call | solution.py:591
  482.4 16.7 %hidden_back.3.grads_ref.refs_1_ = bf16[1024,3072]{1,0:T(8,128)(2,1)} custom-call(bf16[512,2048]{1,0:T(8,128)(2,1)} %broadcast_multiply_fusion.own_ref, bf16[512,2048]{1,0:T(8,128)(2,1)} %collective-permute-done.15.away_ref, bf16[1536,2048]{1,0:T(8,128)(2,1)} %all-gather.17.cloned.1.call-done.refs_1_.down_ref, f32[1024,3072]{1,0:T(8,128)} %get-tuple-element.111.both_ref), custom_call_target="tpu_custom_call" | custom-call | flops 322122560 | bytes 1258291 | tf_op jit(solution)/shard_map/hidden_back/pallas_call | solution.py:536
  499.2 19.0 %unit_grads.2 = bf16[2048,3072]{1,0:T(8,128)(2,1)} custom-call(bf16[512,2048]{1,0:T(8,128)(2,1)} %copy-done.12, bf16[512,2048]{1,0:T(8,128)(2,1)} %collective-permute-done.13.away_ref, bf16[1024,3072]{1,0:T(8,128)(2,1)} %hidden_back.3.grads_ref.refs_1_), custom_call_target="tpu_custom_call" | custom-call | flops 644245120 | bytes 943718 | tf_op jit(solution)/shard_map/unit_grads/pallas_call | solution.py:564
  534.6 34.4 %grad_normed.1 = (f32[512,2048]{1,0:T(8,128)}, bf16[512,2048]{1,0:T(8,128)(2,1)}) custom-call(bf16[1024,3072]{1,0:T(8,128)(2,1)} %hidden_back.2.refs_0_.grads_ref, bf16[1024,3072]{1,0:T(8,128)(2,1)} %hidden_back.3.grads_ref.refs_1_, bf16[2048,3072]{1,0:T(8,128)(2,1)} %all-gather.7.cloned.1.call-done.weight_ref.refs_2_, ...), custom_call_target="tpu_custom_call" | custom-call | flops 1288490240 | bytes 1887436 | tf_op jit(solution)/shard_map/grad_normed/pallas_call | solution.py:623
  571.0 18.5 %unit_grads.3 = bf16[2048,3072]{1,0:T(8,128)(2,1)} custom-call(bf16[512,2048]{1,0:T(8,128)(2,1)} %copy-done.12, bf16[512,2048]{1,0:T(8,128)(2,1)} %collective-permute-done.13.away_ref, bf16[1024,3072]{1,0:T(8,128)(2,1)} %hidden_back.2.refs_0_.grads_ref), custom_call_target="tpu_custom_call" | custom-call | flops 644245120 | bytes 943718 | tf_op jit(solution)/shard_map/unit_grads/pallas_call | solution.py:564
  589.6 27.4 %collective-permute-done.17.away_ref = bf16[512,2048]{1,0:T(8,128)(2,1)} collective-permute-done((bf16[512,2048]{1,0:T(8,128)(2,1)}, bf16[512,2048]{1,0:T(8,128)(2,1)}, u32[]{:S(2)}, u32[]{:S(2)}) %collective-permute-start.17) | collective-permute-done | bytes 2097184 | tf_op jit(solution)/shard_map/ppermute | solution.py:901
  617.0 16.2 %resid_back.1 = (f32[512,2048]{1,0:T(8,128)}, bf16[512,2048]{1,0:T(8,128)(2,1)}, f32[1,2048]{1,0:T(1,128)}, bf16[512,512]{1,0:T(8,128)(2,1)}, bf16[512,512]{1,0:...) custom-call(s32[2]{0:T(128)} %pad_add_fusion.5.place_ref, f32[512,2048]{1,0:T(8,128)} %get-tuple-element.114.own_ref, ...), custom_call_target="tpu_custom_call" | custom-call | flops 214748368 | bytes 1468006 | tf_op jit(solution)/shard_map/resid_back/pallas_call | solution.py:715
  649.8 26.6 %collective-permute-done.18.refs_1_ = bf16[512,512]{1,0:T(8,128)(2,1)S(1)} collective-permute-done((bf16[512,512]{1,0:T(8,128)(2,1)}, bf16[512,512]{1,0:T(8,128)(2,1)S(1)}, u32[]{:S(2)}, u32[]{:S(2)}) %collective-permute-start.18) | collective-permute-done | bytes 524320 | tf_op jit(solution)/shard_map/ppermute | solution.py:909
  676.4 37.1 %collective-permute-done.19.refs_2_ = bf16[512,512]{1,0:T(8,128)(2,1)S(1)} collective-permute-done((bf16[512,512]{1,0:T(8,128)(2,1)}, bf16[512,512]{1,0:T(8,128)(2,1)S(1)}, u32[]{:S(2)}, u32[]{:S(2)}) %collective-permute-start.19) | collective-permute-done | bytes 524320 | tf_op jit(solution)/shard_map/ppermute | solution.py:909
  714.3 49.4 %attend_backward.1 = (bf16[2048,1024]{1,0:T(8,128)(2,1)}, f32[2,2,128]{2,1,0:T(2,128)}) custom-call(s32[2]{0:T(128)} %copy-done.34, bf16[2048,1024]{1,0:T(8,128)(2,1)} %copy-done.5, f32[2048,768]{1,0:T(8,128)} %get-tuple-element.119.raw_ref, f32[2048,128]{1,0:T(8,128)} %copy-done.8, f32[2048,128]{1,0:T(8,128)} %get-tuple-element.182.sine_ref, ...), custom_call_target="tpu_custom_call" | custom-call | flops 107374184 | bytes 104857 | tf_op jit(solution)/shard_map/attend_backward/pallas_call | solution.py:382
  809.0 30.7 %collective-permute-done.22 = bf16[512,2048]{1,0:T(8,128)(2,1)} collective-permute-done((bf16[512,2048]{1,0:T(8,128)(2,1)}, bf16[512,2048]{1,0:T(8,128)(2,1)}, u32[]{:S(2)}, u32[]{:S(2)}) %collective-permute-start.22) | collective-permute-done | bytes 2097184 | tf_op jit(solution)/shard_map/ppermute | solution.py:878
  848.2 24.3 %collective-permute-done.24 = bf16[256,3072]{1,0:T(8,128)(2,1)} collective-permute-done((bf16[256,3072]{1,0:T(8,128)(2,1)}, bf16[256,3072]{1,0:T(8,128)(2,1)}, u32[]{:S(2)}, u32[]{:S(2)}) %collective-permute-start.24) | collective-permute-done | bytes 1572896 | tf_op jit(solution)/shard_map/ppermute | solution.py:909
  896.6 49.0 %collective-permute-done.30 = bf16[512,256]{1,0:T(8,128)(2,1)} collective-permute-done((bf16[512,256]{1,0:T(8,128)(2,1)}, bf16[512,256]{1,0:T(8,128)(2,1)}, u32[]{:S(2)}, u32[]{:S(2)}) %collective-permute-start.30) | collective-permute-done | bytes 262176 | tf_op jit(solution)/shard_map/ppermute | solution.py:909
  977.3 30.3 %collective-permute-done.28 = bf16[512,2048]{1,0:T(8,128)(2,1)} collective-permute-done((bf16[512,2048]{1,0:T(8,128)(2,1)}, bf16[512,2048]{1,0:T(8,128)(2,1)}, u32[]{:S(2)}, u32[]{:S(2)}) %collective-permute-start.28) | collective-permute-done | bytes 2097184 | tf_op jit(solution)/shard_map/ppermute | solution.py:881
  (275 shorter events, 323.4 us)
Async XLA Ops:
  7.2 71.5 %all-gather.11.cloned.1.call-start = ((), (), s32[]{:S(2)}) async-start(), calls=%async_computation.7 | async-start | bytes 5308416 | tf_op jit(solution)/shard_map/all_gather | solution.py:961
  11.7 179.3 %all-gather.9.cloned.1.call-start = ((), (), s32[]{:S(2)}) async-start(), calls=%async_computation.6 | async-start | bytes 7077888 | tf_op jit(solution)/shard_map/all_gather | solution.py:1001
  66.2 124.8 %all-gather.7.cloned.1.call-start = ((), (), s32[]{:S(2)}) async-start(), calls=%async_computation.5 | async-start | bytes 14155776 | tf_op jit(solution)/shard_map/all_gather | solution.py:1000
  69.8 244.4 %all-gather.13.cloned.1.call-start = ((), (), s32[]{:S(2)}) async-start(), calls=%async_computation.8 | async-start | bytes 9437184 | tf_op jit(solution)/shard_map/all_gather | solution.py:1015
  122.4 67.2 %collective-permute-start.7 = (bf16[512,2048]{1,0:T(8,128)(2,1)}, bf16[512,2048]{1,0:T(8,128)(2,1)}, u32[]{:S(2)}, u32[]{:S(2)}) collective-permute-start(bf16[512,2048]{1,0:T(8,128)(2,1)} %collective-permute-done.1.second_ref), channel_id=1, source_target_pairs={{2,3},{6,7},{10,11},{14,15},{18,19},{22,23},{26,27},{30,31}} | collective-permute-start | bytes 6291464 | tf_op jit(solution)/shard_map/ppermute | solution.py:862
  124.4 65.2 %collective-permute-start.8 = (bf16[512,2048]{1,0:T(8,128)(2,1)}, bf16[512,2048]{1,0:T(8,128)(2,1)S(1)}, u32[]{:S(2)}, u32[]{:S(2)}) collective-permute-start(bf16[512,2048]{1,0:T(8,128)(2,1)} %collective-permute-done.3.first_ref), channel_id=1, source_target_pairs={{1,0},{5,4},{9,8},{13,12},{17,16},{21,20},{25,24},{29,28}} | collective-permute-start | bytes 6291464 | tf_op jit(solution)/shard_map/ppermute | solution.py:866
  128.5 60.1 %collective-permute-start.4 = (bf16[512,256]{1,0:T(8,128)(2,1)S(1)}, bf16[512,256]{1,0:T(8,128)(2,1)S(1)}, u32[]{:S(2)}, u32[]{:S(2)}) collective-permute-start(bf16[512,256]{1,0:T(8,128)(2,1)S(1)} %copy-done.46), channel_id=1, source_target_pairs={{1,0},{2,1},{3,2},{0,3},{5,4},{6,5},{7,6},{4,7},{9,8},{10,9},{11,1... | collective-permute-start | bytes 786440 | tf_op jit(solution)/shard_map/ppermute | solution.py:905
  191.0 231.3 %all-gather.15.cloned.1.call-start = ((), (), s32[]{:S(2)}) async-start(), calls=%async_computation.9 | async-start | bytes 14155776 | tf_op jit(solution)/shard_map/all_gather | solution.py:1037
  205.6 68.5 %collective-permute-start.9 = (bf16[256,3072]{1,0:T(8,128)(2,1)}, bf16[256,3072]{1,0:T(8,128)(2,1)}, u32[]{:S(2)}, u32[]{:S(2)}) collective-permute-start(bf16[256,3072]{1,0:T(8,128)(2,1)} %pack_units.1), channel_id=1, source_target_pairs={{2,0},{3,1},{0,2},{1,3},{6,4},{7,5},{4,6},{5,7},{10,8},{11,9},{8,1... | collective-permute-start | bytes 4718600 | tf_op jit(solution)/shard_map/ppermute | solution.py:905
  274.1 171.6 %all-gather.17.cloned.1.call-start = ((), (), s32[]{:S(2)}) async-start(), calls=%async_computation.10 | async-start | bytes 7077888 | tf_op jit(solution)/shard_map/all_gather | solution.py:1038
  326.4 72.1 %collective-permute-start.13 = (bf16[512,2048]{1,0:T(8,128)(2,1)S(1)}, bf16[512,2048]{1,0:T(8,128)(2,1)}, u32[]{:S(2)}, u32[]{:S(2)}) collective-permute-start(bf16[512,2048]{1,0:T(8,128)(2,1)S(1)} %get-tuple-element.97.own_ref), channel_id=1, source_target_pairs={{0,1},{1,0},{2,3},{3,2},{4,5},{5,4},{6,7},{7,6},{8,9},{9,8},{10,11... | collective-permute-start | bytes 6291464 | tf_op jit(solution)/shard_map/ppermute | solution.py:901
  336.6 61.2 %collective-permute-start.14 = (bf16[1536,256]{1,0:T(8,128)(2,1)S(1)}, bf16[1536,256]{1,0:T(8,128)(2,1)}, u32[]{:S(2)}, u32[]{:S(2)}) collective-permute-start(bf16[1536,256]{1,0:T(8,128)(2,1)S(1)} %copy-done.41), channel_id=1, source_target_pairs={{2,0},{3,1},{0,2},{1,3},{6,4},{7,5},{4,6},{5,7},{10,8},{11,9},{8,1... | collective-permute-start | bytes 2359304 | tf_op jit(solution)/shard_map/ppermute | solution.py:905
  398.6 243.7 %reduce-scatter.6.cloned.1.call-start = ((), (), s32[]{:S(2)}) async-start(), calls=%async_computation.11 | async-start | bytes 14155776 | tf_op jit(solution)/shard_map/reduce_scatter | solution.py:1052
  402.2 61.8 %collective-permute-start.15 = (bf16[512,2048]{1,0:T(8,128)(2,1)}, bf16[512,2048]{1,0:T(8,128)(2,1)}, u32[]{:S(2)}, u32[]{:S(2)}) collective-permute-start(bf16[512,2048]{1,0:T(8,128)(2,1)} %broadcast_multiply_fusion.own_ref), channel_id=1, source_target_pairs={{0,1},{1,0},{2,3},{3,2},{4,5},{5,4},{6,7},{7,6},{8,9},{9,8},{10,11... | collective-permute-start | bytes 6291464 | tf_op jit(solution)/shard_map/ppermute | solution.py:901
  482.2 231.3 %reduce-scatter.8.cloned.1.call-start = ((), (), s32[]{:S(2)}) async-start(), calls=%async_computation.12 | async-start | bytes 14155776 | tf_op jit(solution)/shard_map/reduce_scatter | solution.py:1052
  518.2 363.1 %reduce-scatter.12.cloned.1.call-start = ((), (), s32[]{:S(2)}) async-start(), calls=%async_computation.14 | async-start | bytes 9437184 | tf_op jit(solution)/shard_map/reduce_scatter | solution.py:1052
  641.7 330.4 %reduce-scatter.14.cloned.1.call-start = ((), (), s32[]{:S(2)}) async-start(), calls=%async_computation.15 | async-start | bytes 14155776 | tf_op jit(solution)/shard_map/reduce_scatter | solution.py:1052
  642.3 379.0 %reduce-scatter.10.cloned.1.call-start = ((), (), s32[]{:S(2)}) async-start(), calls=%async_computation.13 | async-start | bytes 4718592 | tf_op jit(solution)/shard_map/reduce_scatter | solution.py:1052
  643.5 120.2 %collective-permute-start.21 = (bf16[1536,256]{1,0:T(8,128)(2,1)S(1)}, bf16[1536,256]{1,0:T(8,128)(2,1)S(1)}, u32[]{:S(2)}, u32[]{:S(2)}) collective-permute-start(bf16[1536,256]{1,0:T(8,128)(2,1)S(1)} %split.24), channel_id=1, source_target_pairs={{0,2},{1,3},{2,0},{3,1},{4,6},{5,7},{6,4},{7,5},{8,10},{9,11},{10,... | collective-permute-start | bytes 2359304 | tf_op jit(solution)/shard_map/ppermute | solution.py:909
  646.7 66.8 %collective-permute-start.19 = (bf16[512,512]{1,0:T(8,128)(2,1)}, bf16[512,512]{1,0:T(8,128)(2,1)S(1)}, u32[]{:S(2)}, u32[]{:S(2)}) collective-permute-start(bf16[512,512]{1,0:T(8,128)(2,1)} %get-tuple-element.123), channel_id=1, source_target_pairs={{0,2},{1,3},{2,0},{3,1},{4,6},{5,7},{6,4},{7,5},{8,10},{9,11},{10,... | collective-permute-start | bytes 1572872 | tf_op jit(solution)/shard_map/ppermute | solution.py:909
  647.2 66.3 %collective-permute-start.20 = (bf16[512,512]{1,0:T(8,128)(2,1)}, bf16[512,512]{1,0:T(8,128)(2,1)}, u32[]{:S(2)}, u32[]{:S(2)}) collective-permute-start(bf16[512,512]{1,0:T(8,128)(2,1)} %get-tuple-element.124), channel_id=1, source_target_pairs={{0,3},{1,0},{2,1},{3,2},{4,7},{5,4},{6,5},{7,6},{8,11},{9,8},{10,9... | collective-permute-start | bytes 1572872 | tf_op jit(solution)/shard_map/ppermute | solution.py:909
  794.7 77.7 %collective-permute-start.24 = (bf16[256,3072]{1,0:T(8,128)(2,1)}, bf16[256,3072]{1,0:T(8,128)(2,1)}, u32[]{:S(2)}, u32[]{:S(2)}) collective-permute-start(bf16[256,3072]{1,0:T(8,128)(2,1)} %reduce-scatter.8.cloned.1.call-done), channel_id=1, source_target_pairs={{0,2},{1,3},{2,0},{3,1},{4,6},{5,7},{6,4},{7,5},{8,10},{9,11},{10,... | collective-permute-start | bytes 4718600 | tf_op jit(solution)/shard_map/ppermute | solution.py:909
  872.5 82.9 %collective-permute-start.27 = (bf16[512,2048]{1,0:T(8,128)(2,1)}, bf16[512,2048]{1,0:T(8,128)(2,1)}, u32[]{:S(2)}, u32[]{:S(2)}) collective-permute-start(bf16[512,2048]{1,0:T(8,128)(2,1)} %get-tuple-element.136), channel_id=1, source_target_pairs={{2,1},{3,2},{6,5},{7,6},{10,9},{11,10},{14,13},{15,14},{18,17},{19... | collective-permute-start | bytes 6291464 | tf_op jit(solution)/shard_map/ppermute | solution.py:881
  889.9 71.1 %collective-permute-start.25 = (bf16[512,2048]{1,0:T(8,128)(2,1)}, bf16[512,2048]{1,0:T(8,128)(2,1)}, u32[]{:S(2)}, u32[]{:S(2)}) collective-permute-start(bf16[512,2048]{1,0:T(8,128)(2,1)} %get-tuple-element.135), channel_id=1, source_target_pairs={{0,1},{1,2},{4,5},{5,6},{8,9},{9,10},{12,13},{13,14},{16,17},{17,1... | collective-permute-start | bytes 6291464 | tf_op jit(solution)/shard_map/ppermute | solution.py:878
  (75 other events, 1932.1 us)
Sparse Core Ops, SparseCore 0:
  11.8 41.6 all-gather.10
  66.3 46.7 all-gather.8
  115.5 72.1 all-gather.6
  191.1 54.8 all-gather.12
  274.2 71.1 all-gather.14
  398.7 46.9 all-gather.16
  482.3 92.3 reduce-scatter.5
  578.2 92.3 reduce-scatter.7
  674.1 71.2 reduce-scatter.11
  749.2 92.3 reduce-scatter.13
  947.8 47.2 reduce-scatter.9

commit v3 on v2

--- a/solution.py
+++ b/solution.py
@@ -811,6 +811,70 @@
     )(gate, up)
 
 
+def tokens_back_kernel(
+    own_ref, right_ref, left_ref, rows_ref, gain_ref, resid_ref, out_ref, beside_ref
+):
+    width = rows_ref.shape[1]
+    total = (
+        own_ref[...] + right_ref[...].astype(jnp.float32) + left_ref[...].astype(jnp.float32)
+    )
+    back = norm_back(rows_ref[...].astype(jnp.float32), gain_ref[...], total[:, :width])[0]
+    out_ref[...] = (resid_ref[...] + back).astype(out_ref.dtype)
+    beside_ref[...] = total[:, width:]
+
+
+def tokens_back(parts, tokens, gain, grad_resid):
+    rows, width = tokens.shape
+    more = parts[0].shape[1] - width
+    block = min(256, rows)
+    across = pl.BlockSpec((block, width), lambda i: (i, 0))
+    both = pl.BlockSpec((block, width + more), lambda i: (i, 0))
+    return pl.pallas_call(
+        tokens_back_kernel,
+        grid=(rows // block,),
+        in_specs=[both] * 3 + [across, fixed(gain.shape), across],
+        out_specs=[across, pl.BlockSpec((block, more), lambda i: (i, 0))],
+        out_shape=(
+            jax.ShapeDtypeStruct((rows, width), jnp.bfloat16),
+            jax.ShapeDtypeStruct((rows, more), jnp.float32),
+        ),
+        compiler_params=arbitrary(1, 40),
+        cost_estimate=cost(20 * rows * width, 16 * rows * width),
+        name="tokens_back",
+    )(*parts, tokens, gain, grad_resid)
+
+
+def share_kernel(slot_ref, grads_ref, weight_ref, beside_ref, out_ref):
+    width = weight_ref.shape[0]
+    out_ref[:, :width] = nt(grads_ref[...], weight_ref[...]).astype(out_ref.dtype)
+    out_ref[:, width:] = beside_ref[...].astype(out_ref.dtype)
+
+
+def share(slot, grads, weight, beside, k, count, dtype):
+    positions, columns = grads.shape
+    rows = positions // count
+    width, more = weight.shape[0], beside.shape[1]
+    block = min(256, rows)
+    parts = rows // block
+    return pl.pallas_call(
+        share_kernel,
+        grid_spec=pltpu.PrefetchScalarGridSpec(
+            num_scalar_prefetch=1,
+            grid=(parts,),
+            in_specs=[
+                pl.BlockSpec((block, columns), lambda i, s: (s[0] * parts + i, 0)),
+                fixed(weight.shape),
+                pl.BlockSpec((block, more), lambda i, s: (k * parts + i, 0)),
+            ],
+            out_specs=pl.BlockSpec((block, width + more), lambda i, s: (i, 0)),
+        ),
+        out_shape=jax.ShapeDtypeStruct((rows, width + more), dtype),
+        compiler_params=arbitrary(1, 40),
+        cost_estimate=cost(2 * rows * columns * width, 2 * width * columns),
+        name="share",
+    )(slot, grads, weight, beside)
+
+
 def heads_back_kernel(normed_ref, grad_ref, weight_ref, out_ref, sums_ref):
     partial = tn(normed_ref[...], grad_ref[...])
     out_ref[...] = partial.astype(out_ref.dtype)
@@ -866,24 +930,25 @@
     return lax.ppermute(value, "seq", [(i, i - 1) for i in range(1, count - hop + 1)])
 
 
-def line_scatter(parts, first_before=()):
+def line_scatter(parts, before):
     count = len(parts)
     right, left = None, None
     for hop in range(count - 1):
         to_right, to_left = parts[count - 1 - hop], parts[hop + 1]
         if hop:
-            to_right, to_left = to_right + right, to_left + left
-        if hop == 1:
-            to_right, to_left = after((to_right, to_left), *first_before)
+            to_right = to_right.astype(jnp.float32) + right.astype(jnp.float32)
+            to_left = to_left.astype(jnp.float32) + left.astype(jnp.float32)
+        if hop in before:
+            to_right, to_left = after((to_right, to_left), *before[hop])
         right = lax.ppermute(
             to_right.astype(jnp.bfloat16), "seq", [(i, i + 1) for i in range(hop + 1)]
-        ).astype(jnp.float32)
+        )
         left = lax.ppermute(
             to_left.astype(jnp.bfloat16),
             "seq",
             [(i, i - 1) for i in range(count - 1 - hop, count)],
-        ).astype(jnp.float32)
-    return parts[0] + right + left
+        )
+    return parts[0], right, left
 
 
 def sum_over(value, axis):
@@ -1004,9 +1069,11 @@
         rights.append(hop_right(rights[-1], count, hop))
         lefts.append(hop_left(lefts[-1], count, hop))
     right, left = after((rights[-1], lefts[-1]), whole[1])
+    before_last = (rights[-1], lefts[-1])
     out_blocks = [w_out] + [
-        fetch(after(w_out, rights[-1], lefts[-1]), count, k) for k in range(1, count)
+        fetch(after(w_out, *before_last), count, k) for k in range(1, count)
     ]
+    fetched_down = [fetch(after(w_down, *before_last), count, step) for step in steps[1:]]
     rights.append(hop_right(right, count, count - 1))
     lefts.append(hop_left(left, count, count - 1))
     for k in range(2, count - 1):
@@ -1014,7 +1081,11 @@
     gathered = (rights[-1], lefts[-1])
     out_weight = lax.all_gather(
         after(
-            jnp.concatenate(out_blocks, axis=0), both_weights[0], down_weights[0], *gathered
+            jnp.concatenate(out_blocks, axis=0),
+            both_weights[0],
+            down_weights[0],
+            *gathered,
+            *fetched_down,
         ),
         "dp",
         axis=1,
@@ -1022,7 +1093,7 @@
     )
 
     fetched_both = [
-        fetch(after(own_both, whole[1], *gathered), count, step) for step in steps[1:]
+        fetch(after(own_both, *gathered), count, step) for step in steps[1:]
     ]
     for k in [1, count - 1] if count > 2 else [1]:
         whole = project_block(k, whole)
@@ -1030,12 +1101,11 @@
     context, totals = attend_forward(slot_place, heads, groups, count)
     sent = after(context, *fetched_both)
     context_pieces = [context[0]] + [give(sent[k], count, k) for k in range(1, count)]
-    fetched_down = [fetch(after(w_down, *context_pieces[1:]), count, step) for step in steps[1:]]
     resid, normed_mlp = out_norm(context_pieces, out_weight, tokens_low, gain_mlp)
     away_normed = swap(normed_mlp, count)
     for both, down in zip(fetched_both, fetched_down):
         both_weights.append(lax.all_gather(after(both, context), "dp", axis=0, tiled=True))
-        down_weights.append(lax.all_gather(after(down, away_normed), "dp", axis=1, tiled=True))
+        down_weights.append(lax.all_gather(after(down, heads), "dp", axis=1, tiled=True))
 
     place = jnp.arange(rows, dtype=jnp.int32)[:, None] + me * rows
     valid_rows = (place < length).astype(low)
@@ -1051,9 +1121,6 @@
     def spread(partial, axis):
         return lax.psum_scatter(partial, "dp", scatter_dimension=axis, tiled=True)
 
-    mlp_own, mlp_away = mlp_out(hidden, down_weights)
-    mlp_away = swap(after(mlp_away, away_grads), count)
-    hidden = after(hidden, mlp_own)
     down_partial = down_grads(hidden, grad_rows, away_grads)
     grad_rows, away_grads = after((grad_rows, away_grads), down_partial)
     down_sums = spread(down_partial, 1)
@@ -1066,11 +1133,11 @@
     grad_normed_own, grad_normed_away = grad_normed(
         after(grad_boths, *mate_partials), both_weights
     )
-    own_partial = unit_grads(normed_mlp, away_normed, grad_boths[0])
-    own_sum = spread(own_partial, 0)
+    own_partial = unit_grads(normed_mlp, away_normed, after(grad_boths[0], grad_normed_away))
+    mlp_own, mlp_away = mlp_out(after(hidden, own_partial), down_weights)
     grad_resid, grad_attn_low, gain_mlp_sums, *pieces = resid_back(
         grad_normed_own,
-        after(swap(after(grad_normed_away, mlp_away), count), own_partial),
+        after(swap(grad_normed_away, count), own_partial, mlp_own, down_sums),
         resid,
         cotangent_low,
         gain_mlp,
@@ -1082,6 +1149,7 @@
     pieces = [pieces[0]] + [give(pieces[k], count, k) for k in range(1, count)]
     out_partial = out_grads(context_pieces, grad_attn_low)
     out_sums = spread(out_partial, 1)
+    own_sum = spread(after(own_partial, *pieces, out_partial), 0)
     pieces = after(pieces, out_partial, down_sums, *mate_sums)
     grad_raw, head_gain_terms = attend_backward(
         slot_place,
@@ -1095,22 +1163,42 @@
         totals,
         pieces,
     )
-    given_both = [give(piece, count, step) for step, piece in zip(steps[1:], mate_sums)]
-    down_pieces = jnp.split(down_sums, len(steps), axis=0)
+    away_both, away_down, mlp_away = after((mate_sums, down_sums, mlp_away), *pieces)
+    mlp_away = swap(mlp_away, count)
+    given_first, given_second = [
+        [give(half, count, step) for step, half in zip(steps[1:], halves)]
+        for halves in zip(*(jnp.split(piece, 2, axis=0) for piece in away_both))
+    ]
+    down_pieces = jnp.split(away_down, len(steps), axis=0)
     given_down = [give(piece, count, step) for step, piece in zip(steps[1:], down_pieces[1:])]
-    grad_raw = after(grad_raw, *given_down)
-    shares = [
-        nt(
-            lax.dynamic_slice_in_dim(grad_raw, lax.rem(me + k, count) * rows, rows, 0),
+    shares = {}
+    for k in [count - 1, 1, *range(2, count - 1), 0]:
+        shares[k] = share(
+            places[k][:1],
+            grad_raw,
             heads_weight,
+            out_sums,
+            k,
+            count,
+            low if k else jnp.float32,
         )
-        for k in range(count)
-    ]
+    shares[1], shares[count - 1] = after(
+        (shares[1], shares[count - 1]), *given_down, *given_first, mlp_away
+    )
+    shares = [shares[k] for k in range(count)]
     heads_partial, gain_attn_sums = heads_back(
         normed_attn, after(grad_raw, shares[1], shares[-1]), heads_weight
     )
     grad_heads = spread(heads_partial, 0)
-    grad_normed_attn = line_scatter(shares, (heads_partial, *given_both))
+    gain_attn_term = gain_attn_sums[:, 0] / gain_attn[0]
+    head_gain_sums = jnp.sum(head_gain_terms, axis=0)
+    terms = (gain_attn_term, gain_mlp_sums[0], head_gain_sums[0], head_gain_sums[1])
+    gain_sums = sum_over(jnp.concatenate(terms), "dp").reshape(-1, LANES)
+    sums = sum([give(gain_sums, count, k) if k else gain_sums for k in range(count)]).reshape(-1)
+    last_parts = line_scatter(
+        shares,
+        {1: (heads_partial, shares[0], sums, *given_second), 2: (own_sum,)},
+    )
     grad_heads = grad_heads.astype(jnp.float32)
     grad_query, grad_key, grad_value = from_groups(grad_heads)
     layer_output = (
@@ -1118,22 +1206,16 @@
         .astype(low)
         .reshape(slots, rows, width)
     )
-    grad_input_norm = norm_back(tokens_low.astype(jnp.float32), gain_attn, grad_normed_attn)[0]
-    grad_tokens = (grad_resid + grad_input_norm).astype(low).reshape(slots, rows, width)
-    gain_attn_term = gain_attn_sums[:, 0] / gain_attn[0]
-
-    out_parts = [
-        give(part, count, k) if k else part for k, part in enumerate(jnp.split(out_sums, count))
-    ]
-    grad_out = sum(part.astype(jnp.float32) for part in out_parts)
-    both_total = sum([part.astype(jnp.float32) for part in [own_sum, *given_both]])
+    grad_tokens, grad_out = tokens_back(last_parts, tokens_low, gain_attn, grad_resid)
+    grad_tokens = grad_tokens.reshape(slots, rows, width)
+
+    both_total = own_sum.astype(jnp.float32) + sum(
+        jnp.concatenate(halves, axis=0).astype(jnp.float32)
+        for halves in zip(given_first, given_second)
+    )
     grad_gate, grad_up = separate(both_total, tile)
     grad_down = sum([part.astype(jnp.float32) for part in [down_pieces[0], *given_down]])
 
-    head_gain_sums = jnp.sum(head_gain_terms, axis=0)
-    terms = (gain_attn_term, gain_mlp_sums[0], head_gain_sums[0], head_gain_sums[1])
-    sums = sum_over(jnp.concatenate(terms), "dp")
-    sums = sum_over(after(sums, grad_normed_attn), "seq")
     gain_grads, at = [], 0
     for term, part_size in zip(terms, gain_sizes):
         gain_grads.append(

time: 1050 us -> 950 us (0.905)
  waiting for transfers between devices: 486 us -> 412 us
  matrix products: 30.3 us -> 0 us
  Pallas kernels: 336 us -> 350 us
    ppermute x5, waiting for transfers between devices: 139 us -> 89.9 us  [fetch(): lax.ppermute(value, 'seq', [((i + step) % count, i) for i in range(count)])]
    ppermute x11 -> x12, waiting for transfers between devices: 171 us -> 123 us  [give(): lax.ppermute(value, 'seq', [(i, (i + step) % count) for i in range(count)])]
    dot_general x4 -> x0, matrix products: 30.3 us -> none  [nt(): lax.dot_general(left, right, (((1,), (1,)), ((), ())), preferred_element_...]
    ppermute x3, waiting for transfers between devices: 30.3 us -> 4.27 us  [line_scatter(): lax.ppermute(to_left.astype(jnp.bfloat16), 'seq', [(i, i - 1) for i in ra...]
    ppermute x4, waiting for transfers between devices: 28.3 us -> 52.1 us  [swap(): return lax.ppermute(value, 'seq', [(i, i ^ 1) for i in range(count)])]
    ppermute x3, waiting for transfers between devices: 35.9 us -> 56.5 us  [line_scatter(): lax.ppermute(to_right.astype(jnp.bfloat16), 'seq', [(i, i + 1) for i in r...]
    pallas_call x0 -> x5, Pallas kernels: none -> 17.8 us  [the longest x4 11.5 us: share(): pl.pallas_call(share_kernel, grid_spec=pltpu.PrefetchScalarGridSpec(num_s...]
    ppermute x3, starting transfers between devices: 26.4 us -> 9.2 us  [line_scatter(): lax.ppermute(to_right.astype(jnp.bfloat16), 'seq', [(i, i + 1) for i in r...]
  transfers between devices with their start and end apart: 48 -> 47, of which waited for: 21 -> 23; matrix products, arithmetic and copies ran while one was open for 8% -> 5% of each run, Pallas kernels for 30% -> 36%
where the time goes in v3:
time: 950 us; the launch traced here: 942 us
  waiting for transfers between devices  412 us (43%)
  Pallas kernels  350 us (37%)
  starting transfers between devices  85.6 us (9%)
  local copies, waits for them, and re-layouts  45.2 us (5%)
  other arithmetic  33.9 us (4%)
  between operations  15.8 us (2%)
    ppermute x12, waiting for transfers between devices, give(): lax.ppermute(value, 'seq', [(i, (i + step) % count) for i in range(count)])  123 us
    ppermute x5, waiting for transfers between devices, fetch(): lax.ppermute(value, 'seq', [((i + step) % count, i) for i in range(count)])  89.9 us
    ppermute x3, waiting for transfers between devices, line_scatter(): lax.ppermute(to_right.astype(jnp.bfloat16), 'seq', [(i, i + 1) for i in r...  56.5 us
    ppermute x4, waiting for transfers between devices, swap(): return lax.ppermute(value, 'seq', [(i, i ^ 1) for i in range(count)])  52.1 us
    pallas_call x1, Pallas kernels, attend_backward(): pl.pallas_call(functools.partial(backward_kernel, block, groups, position...  46 us
    ppermute x3, waiting for transfers between devices, hop_right(): lax.ppermute(value, 'seq', [(i, i + 1) for i in range(hop - 1, count - 1)])  42.6 us
    pallas_call x2, Pallas kernels, hidden_units(): pl.pallas_call(functools.partial(hidden_kernel, tile), grid=(tiles,), in_...  39.2 us
    pallas_call x2, Pallas kernels, unit_grads(): pl.pallas_call(unit_grads_kernel, grid=(columns // tile,), in_specs=[fixe...  37.3 us
  transfers between devices with their start and end apart: 47, of which 23 were waited for; matrix products, arithmetic and copies ran while one was open for 5% of the time, Pallas kernels for 36%

profile of v3, /device:TPU:0, one launch (start us, length us, event | category | flops | bytes accessed | tf_op | source)
XLA Modules:
  0.0 942.0 jit_solution(16650955401051618145)
XLA Ops:
  19.4 42.6 %collective-permute-done.second_ref = bf16[512,2048]{1,0:T(8,128)(2,1)} collective-permute-done((bf16[512,2048]{1,0:T(8,128)(2,1)}, bf16[512,2048]{1,0:T(8,128)(2,1)}, u32[]{:S(2)}, u32[]{:S(2)}) %collective-permute-start) | collective-permute-done | bytes 2097184 | tf_op jit(solution)/shard_map/ppermute | solution.py:926
  89.2 31.2 %collective-permute-done.3.first_ref = bf16[512,2048]{1,0:T(8,128)(2,1)} collective-permute-done((bf16[512,2048]{1,0:T(8,128)(2,1)}, bf16[512,2048]{1,0:T(8,128)(2,1)}, u32[]{:S(2)}, u32[]{:S(2)}) %collective-permute-start.3) | collective-permute-done | bytes 2097184 | tf_op jit(solution)/shard_map/ppermute | solution.py:930
  129.9 67.8 %collective-permute-done.4 = bf16[512,256]{1,0:T(8,128)(2,1)S(1)} collective-permute-done((bf16[512,256]{1,0:T(8,128)(2,1)S(1)}, bf16[512,256]{1,0:T(8,128)(2,1)S(1)}, u32[]{:S(2)}, u32[]{:S(2)}) %collective-permute-start.4) | collective-permute-done | bytes 262176 | tf_op jit(solution)/shard_map/ppermute | solution.py:970
  239.7 24.8 %attend_forward.1 = (bf16[4,512,512]{2,1,0:T(8,128)(2,1)S(1)}, f32[4,8,2048]{2,1,0:T(8,128)S(1)}) custom-call(s32[2]{0:T(128)S(1)} %pad_add_fusion.1.place_ref, bf16[2048,1024]{1,0:T(8,128)(2,1)} %copy-done.5), custom_call_target="tpu_custom_call" | custom-call | flops 429496736 | bytes 419430 | tf_op jit(solution)/shard_map/attend_forward/pallas_call | solution.py:216
  282.6 12.4 %collective-permute-done.11.refs_1_ = bf16[512,512]{1,0:T(8,128)(2,1)S(1)} collective-permute-done((bf16[512,512]{1,0:T(8,128)(2,1)S(1)}, bf16[512,512]{1,0:T(8,128)(2,1)S(1)}, u32[]{:S(2)}, u32[]{:S(2)}) %collective-permute-start.11) | collective-permute-done | bytes 524320 | tf_op jit(solution)/shard_map/ppermute | solution.py:974
  295.0 21.5 %collective-permute-done.12.refs_2_ = bf16[512,512]{1,0:T(8,128)(2,1)S(1)} collective-permute-done((bf16[512,512]{1,0:T(8,128)(2,1)S(1)}, bf16[512,512]{1,0:T(8,128)(2,1)S(1)}, u32[]{:S(2)}, u32[]{:S(2)}) %collective-permute-start.12) | collective-permute-done | bytes 524320 | tf_op jit(solution)/shard_map/ppermute | solution.py:974
  343.7 42.1 %collective-permute-done.14.away_ref = bf16[512,2048]{1,0:T(8,128)(2,1)} collective-permute-done((bf16[512,2048]{1,0:T(8,128)(2,1)S(1)}, bf16[512,2048]{1,0:T(8,128)(2,1)}, u32[]{:S(2)}, u32[]{:S(2)}) %collective-permute-start.14) | collective-permute-done | bytes 2097184 | tf_op jit(solution)/shard_map/ppermute | solution.py:966
  387.5 19.6 %hidden_units.2 = (f32[1024,3072]{1,0:T(8,128)}, bf16[1024,3072]{1,0:T(8,128)(2,1)}) custom-call(bf16[512,2048]{1,0:T(8,128)(2,1)} %copy-done.12, bf16[512,2048]{1,0:T(8,128)(2,1)} %collective-permute-done.14.away_ref, bf16[2048,3072]{1,0:T(8,128)(2,1)} %all-gather.7.cloned.1.call-done.weight_ref.refs_2_), custom_call_target="tpu_custom_call" | custom-call | flops 644245120 | bytes 1415577 | tf_op jit(solution)/shard_map/hidden_units/pallas_call | solution.py:499
  407.1 19.6 %hidden_units.3 = (f32[1024,3072]{1,0:T(8,128)}, bf16[1024,3072]{1,0:T(8,128)(2,1)}) custom-call(bf16[512,2048]{1,0:T(8,128)(2,1)} %copy-done.12, bf16[512,2048]{1,0:T(8,128)(2,1)} %collective-permute-done.14.away_ref, bf16[2048,3072]{1,0:T(8,128)(2,1)} %all-gather.15.cloned.1.call-done.weight_ref.refs_3_, ...), custom_call_target="tpu_custom_call", output_to_operand_aliasing={{1}: (3, {})} | custom-call | flops 644245120 | bytes 1415577 | tf_op jit(solution)/shard_map/hidden_units/pallas_call | solution.py:499
  432.3 18.2 %down_grads.1 = bf16[3072,2048]{1,0:T(8,128)(2,1)} custom-call(bf16[1024,3072]{1,0:T(8,128)(2,1)} %get-tuple-element.119.hidden_ref, bf16[512,2048]{1,0:T(8,128)(2,1)} %broadcast_multiply_fusion.own_ref, bf16[512,2048]{1,0:T(8,128)(2,1)} %collective-permute-done.15.away_ref), custom_call_target="tpu_custom_call" | custom-call | flops 644245120 | bytes 943718 | tf_op jit(solution)/shard_map/down_grads/pallas_call | solution.py:591
  450.6 16.7 %hidden_back.3.grads_ref.refs_1_ = bf16[1024,3072]{1,0:T(8,128)(2,1)} custom-call(bf16[512,2048]{1,0:T(8,128)(2,1)} %broadcast_multiply_fusion.own_ref, bf16[512,2048]{1,0:T(8,128)(2,1)} %collective-permute-done.15.away_ref, bf16[1536,2048]{1,0:T(8,128)(2,1)} %all-gather.17.cloned.1.call-done.down_ref.refs_1_, f32[1024,3072]{1,0:T(8,128)} %get-tuple-element.114.both_ref), custom_call_target="tpu_custom_call" | custom-call | flops 322122560 | bytes 1258291 | tf_op jit(solution)/shard_map/hidden_back/pallas_call | solution.py:536
  467.3 18.8 %unit_grads.2 = bf16[2048,3072]{1,0:T(8,128)(2,1)} custom-call(bf16[512,2048]{1,0:T(8,128)(2,1)} %copy-done.12, bf16[512,2048]{1,0:T(8,128)(2,1)} %collective-permute-done.14.away_ref, bf16[1024,3072]{1,0:T(8,128)(2,1)} %hidden_back.3.grads_ref.refs_1_), custom_call_target="tpu_custom_call" | custom-call | flops 644245120 | bytes 943718 | tf_op jit(solution)/shard_map/unit_grads/pallas_call | solution.py:564
  486.3 15.7 %hidden_back.2.refs_0_.grads_ref = bf16[1024,3072]{1,0:T(8,128)(2,1)} custom-call(bf16[512,2048]{1,0:T(8,128)(2,1)} %broadcast_multiply_fusion.own_ref, bf16[512,2048]{1,0:T(8,128)(2,1)} %collective-permute-done.15.away_ref, bf16[1536,2048]{1,0:T(8,128)(2,1)} %all-gather.9.cloned.1.call-done.down_ref.refs_0_, f32[1024,3072]{1,0:T(8,128)} %get-tuple-element.112.both_ref), custom_call_target="tpu_custom_call" | custom-call | flops 322122560 | bytes 1258291 | tf_op jit(solution)/shard_map/hidden_back/pallas_call | solution.py:536
  501.9 34.3 %grad_normed.1 = (f32[512,2048]{1,0:T(8,128)}, bf16[512,2048]{1,0:T(8,128)(2,1)}) custom-call(bf16[1024,3072]{1,0:T(8,128)(2,1)} %hidden_back.2.refs_0_.grads_ref, bf16[1024,3072]{1,0:T(8,128)(2,1)} %hidden_back.3.grads_ref.refs_1_, bf16[2048,3072]{1,0:T(8,128)(2,1)} %all-gather.7.cloned.1.call-done.weight_ref.refs_2_, ...), custom_call_target="tpu_custom_call" | custom-call | flops 1288490240 | bytes 1887436 | tf_op jit(solution)/shard_map/grad_normed/pallas_call | solution.py:623
  538.4 18.5 %unit_grads.3 = bf16[2048,3072]{1,0:T(8,128)(2,1)} custom-call(bf16[512,2048]{1,0:T(8,128)(2,1)} %copy-done.12, bf16[512,2048]{1,0:T(8,128)(2,1)} %collective-permute-done.14.away_ref, bf16[1024,3072]{1,0:T(8,128)(2,1)} %hidden_back.2.refs_0_.grads_ref), custom_call_target="tpu_custom_call" | custom-call | flops 644245120 | bytes 943718 | tf_op jit(solution)/shard_map/unit_grads/pallas_call | solution.py:564
  556.9 20.4 %mlp_out.1 = (f32[512,2048]{1,0:T(8,128)}, bf16[512,2048]{1,0:T(8,128)(2,1)}) custom-call(bf16[1024,3072]{1,0:T(8,128)(2,1)} %get-tuple-element.119.hidden_ref, bf16[1536,2048]{1,0:T(8,128)(2,1)} %all-gather.9.cloned.1.call-done.down_ref.refs_0_, bf16[1536,2048]{1,0:T(8,128)(2,1)} %all-gather.17.cloned.1.call-done.down_ref.refs_1_), custom_call_target="tpu_custom_call" | custom-call | flops 644245120 | bytes 943718 | tf_op jit(solution)/shard_map/mlp_out/pallas_call | solution.py:660
  582.4 15.8 %resid_back.1 = (f32[512,2048]{1,0:T(8,128)}, bf16[512,2048]{1,0:T(8,128)(2,1)}, f32[1,2048]{1,0:T(1,128)}, bf16[512,512]{1,0:T(8,128)(2,1)}, bf16[512,512]{1,0:...) custom-call(s32[2]{0:T(128)} %pad_add_fusion.5.place_ref, f32[512,2048]{1,0:T(8,128)} %get-tuple-element.122.own_ref, ...), custom_call_target="tpu_custom_call" | custom-call | flops 214748368 | bytes 1468006 | tf_op jit(solution)/shard_map/resid_back/pallas_call | solution.py:715
  611.7 12.8 %collective-permute-done.17.refs_1_ = bf16[512,512]{1,0:T(8,128)(2,1)S(1)} collective-permute-done((bf16[512,512]{1,0:T(8,128)(2,1)S(1)}, bf16[512,512]{1,0:T(8,128)(2,1)S(1)}, u32[]{:S(2)}, u32[]{:S(2)}) %collective-permute-start.17) | collective-permute-done | bytes 524320 | tf_op jit(solution)/shard_map/ppermute | solution.py:974
  624.5 18.1 %collective-permute-done.18.refs_2_ = bf16[512,512]{1,0:T(8,128)(2,1)} collective-permute-done((bf16[512,512]{1,0:T(8,128)(2,1)S(1)}, bf16[512,512]{1,0:T(8,128)(2,1)}, u32[]{:S(2)}, u32[]{:S(2)}) %collective-permute-start.18) | collective-permute-done | bytes 524320 | tf_op jit(solution)/shard_map/ppermute | solution.py:974
  661.3 46.0 %attend_backward.1 = (bf16[2048,1024]{1,0:T(8,128)(2,1)}, f32[2,2,128]{2,1,0:T(2,128)}) custom-call(s32[2]{0:T(128)} %copy-done.35, bf16[2048,1024]{1,0:T(8,128)(2,1)} %copy-done.5, f32[2048,768]{1,0:T(8,128)} %get-tuple-element.134.raw_ref, f32[2048,128]{1,0:T(8,128)} %copy-done.8, f32[2048,128]{1,0:T(8,128)} %copy-done.9, f32[2,128]{1,0:T(2,128)} %copy-done.34, ...), custom_call_target="tpu_custom_call" | custom-call | flops 107374184 | bytes 104857 | tf_op jit(solution)/shard_map/attend_backward/pallas_call | solution.py:382
  740.7 13.6 %heads_back.1 = (bf16[2048,1024]{1,0:T(8,128)(2,1)S(1)}, f32[2048,128]{1,0:T(8,128)S(1)}) custom-call(bf16[2048,2048]{1,0:T(8,128)(2,1)} %get-tuple-element.141.normed_ref, bf16[2048,1024]{1,0:T(8,128)(2,1)} %get-tuple-element.142.grads_ref.grad_ref, bf16[2048,1024]{1,0:T(8,128)(2,1)} %copy-done), custom_call_target="tpu_custom_call" | custom-call | flops 429496736 | bytes 1048576 | tf_op jit(solution)/shard_map/heads_back/pallas_call | solution.py:889
  770.7 18.4 %collective-permute-done.23 = bf16[512,2304]{1,0:T(8,128)(2,1)} collective-permute-done((bf16[512,2304]{1,0:T(8,128)(2,1)}, bf16[512,2304]{1,0:T(8,128)(2,1)}, u32[]{:S(2)}, u32[]{:S(2)}) %collective-permute-start.23) | collective-permute-done | bytes 2359328 | tf_op jit(solution)/shard_map/ppermute | solution.py:943
  826.8 34.6 %collective-permute-done.33 = f32[34,128]{1,0:T(8,128)S(1)} collective-permute-done((f32[34,128]{1,0:T(8,128)S(1)}, f32[34,128]{1,0:T(8,128)S(1)}, u32[]{:S(2)}, u32[]{:S(2)}) %collective-permute-start.33) | collective-permute-done | bytes 17440 | tf_op jit(solution)/shard_map/ppermute | solution.py:974
  886.2 38.2 %collective-permute-done.28.right_ref = bf16[512,2304]{1,0:T(8,128)(2,1)S(1)} collective-permute-done((bf16[512,2304]{1,0:T(8,128)(2,1)}, bf16[512,2304]{1,0:T(8,128)(2,1)S(1)}, u32[]{:S(2)}, u32[]{:S(2)}) %collective-permute-start.28) | collective-permute-done | bytes 2359328 | tf_op jit(solution)/shard_map/ppermute | solution.py:943
  (271 shorter events, 304.6 us)
Async XLA Ops:
  7.2 69.7 %all-gather.11.cloned.1.call-start = ((), (), s32[]{:S(2)}) async-start(), calls=%async_computation.7 | async-start | bytes 5308416 | tf_op jit(solution)/shard_map/all_gather | solution.py:1026
  11.8 196.9 %all-gather.9.cloned.1.call-start = ((), (), s32[]{:S(2)}) async-start(), calls=%async_computation.6 | async-start | bytes 7077888 | tf_op jit(solution)/shard_map/all_gather | solution.py:1066
  67.5 141.2 %all-gather.7.cloned.1.call-start = ((), (), s32[]{:S(2)}) async-start(), calls=%async_computation.5 | async-start | bytes 14155776 | tf_op jit(solution)/shard_map/all_gather | solution.py:1065
  68.8 249.3 %all-gather.13.cloned.1.call-start = ((), (), s32[]{:S(2)}) async-start(), calls=%async_computation.8 | async-start | bytes 9437184 | tf_op jit(solution)/shard_map/all_gather | solution.py:1082
  120.3 88.3 %collective-permute-start.7 = (bf16[512,2048]{1,0:T(8,128)(2,1)}, bf16[512,2048]{1,0:T(8,128)(2,1)}, u32[]{:S(2)}, u32[]{:S(2)}) collective-permute-start(bf16[512,2048]{1,0:T(8,128)(2,1)} %collective-permute-done.1.second_ref), channel_id=1, source_target_pairs={{2,3},{6,7},{10,11},{14,15},{18,19},{22,23},{26,27},{30,31}} | collective-permute-start | bytes 6291464 | tf_op jit(solution)/shard_map/ppermute | solution.py:926
  122.3 86.3 %collective-permute-start.8 = (bf16[512,2048]{1,0:T(8,128)(2,1)}, bf16[512,2048]{1,0:T(8,128)(2,1)}, u32[]{:S(2)}, u32[]{:S(2)}) collective-permute-start(bf16[512,2048]{1,0:T(8,128)(2,1)} %collective-permute-done.3.first_ref), channel_id=1, source_target_pairs={{1,0},{5,4},{9,8},{13,12},{17,16},{21,20},{25,24},{29,28}} | collective-permute-start | bytes 6291464 | tf_op jit(solution)/shard_map/ppermute | solution.py:930
  123.6 85.0 %collective-permute-start.9 = (bf16[1536,256]{1,0:T(8,128)(2,1)S(1)}, bf16[1536,256]{1,0:T(8,128)(2,1)}, u32[]{:S(2)}, u32[]{:S(2)}) collective-permute-start(bf16[1536,256]{1,0:T(8,128)(2,1)S(1)} %copy-done.45), channel_id=1, source_target_pairs={{2,0},{3,1},{0,2},{1,3},{6,4},{7,5},{4,6},{5,7},{10,8},{11,9},{8,1... | collective-permute-start | bytes 2359304 | tf_op jit(solution)/shard_map/ppermute | solution.py:970
  125.7 72.1 %collective-permute-start.4 = (bf16[512,256]{1,0:T(8,128)(2,1)S(1)}, bf16[512,256]{1,0:T(8,128)(2,1)S(1)}, u32[]{:S(2)}, u32[]{:S(2)}) collective-permute-start(bf16[512,256]{1,0:T(8,128)(2,1)S(1)} %copy-done.47), channel_id=1, source_target_pairs={{1,0},{2,1},{3,2},{0,3},{5,4},{6,5},{7,6},{4,7},{9,8},{10,9},{11,1... | collective-permute-start | bytes 786440 | tf_op jit(solution)/shard_map/ppermute | solution.py:970
  129.9 67.9 %collective-permute-start.5 = (bf16[512,256]{1,0:T(8,128)(2,1)S(1)}, bf16[512,256]{1,0:T(8,128)(2,1)S(1)}, u32[]{:S(2)}, u32[]{:S(2)}) collective-permute-start(bf16[512,256]{1,0:T(8,128)(2,1)S(1)} %copy-done.47), channel_id=1, source_target_pairs={{2,0},{3,1},{0,2},{1,3},{6,4},{7,5},{4,6},{5,7},{10,8},{11,9},{8,1... | collective-permute-start | bytes 786440 | tf_op jit(solution)/shard_map/ppermute | solution.py:970
  208.8 198.3 %all-gather.15.cloned.1.call-start = ((), (), s32[]{:S(2)}) async-start(), calls=%async_computation.9 | async-start | bytes 14155776 | tf_op jit(solution)/shard_map/all_gather | solution.py:1107
  209.0 68.5 %collective-permute-start.10 = (bf16[256,3072]{1,0:T(8,128)(2,1)}, bf16[256,3072]{1,0:T(8,128)(2,1)}, u32[]{:S(2)}, u32[]{:S(2)}) collective-permute-start(bf16[256,3072]{1,0:T(8,128)(2,1)} %pack_units.1), channel_id=1, source_target_pairs={{2,0},{3,1},{0,2},{1,3},{6,4},{7,5},{4,6},{5,7},{10,8},{11,9},{8,1... | collective-permute-start | bytes 4718600 | tf_op jit(solution)/shard_map/ppermute | solution.py:970
  277.5 173.0 %all-gather.17.cloned.1.call-start = ((), (), s32[]{:S(2)}) async-start(), calls=%async_computation.10 | async-start | bytes 7077888 | tf_op jit(solution)/shard_map/all_gather | solution.py:1108
  278.1 303.0 %reduce-scatter.8.cloned.1.call-start = ((), (), s32[]{:S(2)}) async-start(), calls=%async_computation.12 | async-start | bytes 14155776 | tf_op jit(solution)/shard_map/reduce_scatter | solution.py:1122
  330.4 55.3 %collective-permute-start.14 = (bf16[512,2048]{1,0:T(8,128)(2,1)S(1)}, bf16[512,2048]{1,0:T(8,128)(2,1)}, u32[]{:S(2)}, u32[]{:S(2)}) collective-permute-start(bf16[512,2048]{1,0:T(8,128)(2,1)S(1)} %get-tuple-element.105.own_ref), channel_id=1, source_target_pairs={{0,1},{1,0},{2,3},{3,2},{4,5},{5,4},{6,7},{7,6},{8,9},{9,8},{10,11... | collective-permute-start | bytes 6291464 | tf_op jit(solution)/shard_map/ppermute | solution.py:966
  450.5 192.2 %reduce-scatter.6.cloned.1.call-start = ((), (), s32[]{:S(2)}) async-start(), calls=%async_computation.11 | async-start | bytes 14155776 | tf_op jit(solution)/shard_map/reduce_scatter | solution.py:1122
  486.0 226.9 %reduce-scatter.10.cloned.1.call-start = ((), (), s32[]{:S(2)}) async-start(), calls=%async_computation.13 | async-start | bytes 9437184 | tf_op jit(solution)/shard_map/reduce_scatter | solution.py:1122
  606.8 266.4 %reduce-scatter.12.cloned.1.call-start = ((), (), s32[]{:S(2)}) async-start(), calls=%async_computation.14 | async-start | bytes 14155776 | tf_op jit(solution)/shard_map/reduce_scatter | solution.py:1122
  642.6 235.6 %reduce-scatter.14.cloned.1.call-start = ((), (), s32[]{:S(2)}) async-start(), calls=%async_computation.15 | async-start | bytes 4718592 | tf_op jit(solution)/shard_map/reduce_scatter | solution.py:1122
  642.7 91.6 %collective-permute-start.20 = (bf16[512,2048]{1,0:T(8,128)(2,1)}, bf16[512,2048]{1,0:T(8,128)(2,1)}, u32[]{:S(2)}, u32[]{:S(2)}) collective-permute-start(bf16[512,2048]{1,0:T(8,128)(2,1)} %get-tuple-element.133), channel_id=1, source_target_pairs={{0,1},{1,0},{2,3},{3,2},{4,5},{5,4},{6,7},{7,6},{8,9},{9,8},{10,11... | collective-permute-start | bytes 6291464 | tf_op jit(solution)/shard_map/ppermute | solution.py:966
  657.4 67.4 %collective-permute-start.22 = (bf16[128,3072]{1,0:T(8,128)(2,1)}, bf16[128,3072]{1,0:T(8,128)(2,1)S(1)}, u32[]{:S(2)}, u32[]{:S(2)}) collective-permute-start(bf16[128,3072]{1,0:T(8,128)(2,1)} %get-tuple-element.167), channel_id=1, source_target_pairs={{0,2},{1,3},{2,0},{3,1},{4,6},{5,7},{6,4},{7,5},{8,10},{9,11},{10,... | collective-permute-start | bytes 2359304 | tf_op jit(solution)/shard_map/ppermute | solution.py:974
  658.4 75.2 %collective-permute-start.21 = (bf16[1536,256]{1,0:T(8,128)(2,1)}, bf16[1536,256]{1,0:T(8,128)(2,1)}, u32[]{:S(2)}, u32[]{:S(2)}) collective-permute-start(bf16[1536,256]{1,0:T(8,128)(2,1)} %split.12), channel_id=1, source_target_pairs={{0,2},{1,3},{2,0},{3,1},{4,6},{5,7},{6,4},{7,5},{8,10},{9,11},{10,... | collective-permute-start | bytes 2359304 | tf_op jit(solution)/shard_map/ppermute | solution.py:974
  734.3 54.8 %collective-permute-start.23 = (bf16[512,2304]{1,0:T(8,128)(2,1)}, bf16[512,2304]{1,0:T(8,128)(2,1)}, u32[]{:S(2)}, u32[]{:S(2)}) collective-permute-start(bf16[512,2304]{1,0:T(8,128)(2,1)} %share.6), channel_id=1, source_target_pairs={{0,1},{4,5},{8,9},{12,13},{16,17},{20,21},{24,25},{28,29}} | collective-permute-start | bytes 7077896 | tf_op jit(solution)/shard_map/ppermute | solution.py:943
  804.1 63.2 %collective-permute-start.27 = (bf16[512,2304]{1,0:T(8,128)(2,1)S(1)}, bf16[512,2304]{1,0:T(8,128)(2,1)S(1)}, u32[]{:S(2)}, u32[]{:S(2)}) collective-permute-start(bf16[512,2304]{1,0:T(8,128)(2,1)S(1)} %get-tuple-element.145), channel_id=1, source_target_pairs={{2,1},{3,2},{6,5},{7,6},{10,9},{11,10},{14,13},{15,14},{18,17},{19... | collective-permute-start | bytes 7077896 | tf_op jit(solution)/shard_map/ppermute | solution.py:946
  808.8 52.7 %collective-permute-start.33 = (f32[34,128]{1,0:T(8,128)S(1)}, f32[34,128]{1,0:T(8,128)S(1)}, u32[]{:S(2)}, u32[]{:S(2)}) collective-permute-start(f32[34,128]{1,0:T(8,128)S(1)} %add.103), channel_id=1, source_target_pairs={{0,1},{1,2},{2,3},{3,0},{4,5},{5,6},{6,7},{7,4},{8,9},{9,10},{10,1... | collective-permute-start | bytes 52232 | tf_op jit(solution)/shard_map/ppermute | solution.py:974
  (76 other events, 2025.5 us)
Sparse Core Ops, SparseCore 0:
  11.9 41.6 all-gather.10
  67.6 45.5 all-gather.8
  115.7 72.1 all-gather.6
  208.9 54.1 all-gather.12
  277.6 71.1 all-gather.14
  350.5 46.6 all-gather.16
  450.6 91.5 reduce-scatter.7
  545.7 92.4 reduce-scatter.5
  641.6 71.2 reduce-scatter.9
  716.7 92.7 reduce-scatter.11
  813.2 51.2 reduce-scatter.13

commit v4 on v3

--- a/solution.py
+++ b/solution.py
@@ -477,7 +477,7 @@
     for half, rows_ref in enumerate((own_ref, away_ref)):
         here = slice(half * rows, (half + 1) * rows)
         both = nn(rows_ref[...], weight_ref[...])
-        both_ref[here, :] = both
+        both_ref[here, :] = both.astype(both_ref.dtype)
         gate, up = both[:, :tile], both[:, tile:]
         hidden_ref[here, :] = (gate * jax.nn.sigmoid(gate) * up).astype(hidden_ref.dtype)
 
@@ -505,7 +505,7 @@
             pl.BlockSpec((2 * rows, tile), lambda j: (0, at * tiles + j)),
         ],
         out_shape=(
-            jax.ShapeDtypeStruct((2 * rows, columns), jnp.float32),
+            jax.ShapeDtypeStruct((2 * rows, columns), jnp.bfloat16),
             jax.ShapeDtypeStruct((2 * rows, total), jnp.bfloat16),
         ),
         input_output_aliases=aliases,
@@ -520,7 +520,8 @@
     for half, grads_ref in enumerate((own_ref, away_ref)):
         here = slice(half * rows, (half + 1) * rows)
         grad_hidden = nt(grads_ref[...], down_ref[...])
-        gate, up = both_ref[here, :tile], both_ref[here, tile:]
+        gate = both_ref[here, :tile].astype(jnp.float32)
+        up = both_ref[here, tile:].astype(jnp.float32)
         sigmoid = jax.nn.sigmoid(gate)
         silu = gate * sigmoid
         out_ref[here, :tile] = (grad_hidden * up * (sigmoid + silu * (1.0 - sigmoid))).astype(
@@ -933,6 +934,7 @@
 def line_scatter(parts, before):
     count = len(parts)
     right, left = None, None
+    hops = []
     for hop in range(count - 1):
         to_right, to_left = parts[count - 1 - hop], parts[hop + 1]
         if hop:
@@ -948,7 +950,8 @@
             "seq",
             [(i, i - 1) for i in range(count - 1 - hop, count)],
         )
-    return parts[0], right, left
+        hops.append((right, left))
+    return (parts[0], right, left), hops
 
 
 def sum_over(value, axis):
@@ -1070,14 +1073,14 @@
         lefts.append(hop_left(lefts[-1], count, hop))
     right, left = after((rights[-1], lefts[-1]), whole[1])
     before_last = (rights[-1], lefts[-1])
-    out_blocks = [w_out] + [
-        fetch(after(w_out, *before_last), count, k) for k in range(1, count)
-    ]
     fetched_down = [fetch(after(w_down, *before_last), count, step) for step in steps[1:]]
     rights.append(hop_right(right, count, count - 1))
     lefts.append(hop_left(left, count, count - 1))
     for k in range(2, count - 1):
         whole = project_block(k, whole)
+    out_blocks = [w_out] + [
+        fetch(after(w_out, *before_last, whole[1]), count, k) for k in range(1, count)
+    ]
     gathered = (rights[-1], lefts[-1])
     out_weight = lax.all_gather(
         after(
@@ -1099,7 +1102,7 @@
         whole = project_block(k, whole)
     normed_attn, heads, raw = whole
     context, totals = attend_forward(slot_place, heads, groups, count)
-    sent = after(context, *fetched_both)
+    sent = context
     context_pieces = [context[0]] + [give(sent[k], count, k) for k in range(1, count)]
     resid, normed_mlp = out_norm(context_pieces, out_weight, tokens_low, gain_mlp)
     away_normed = swap(normed_mlp, count)
@@ -1194,10 +1197,10 @@
     head_gain_sums = jnp.sum(head_gain_terms, axis=0)
     terms = (gain_attn_term, gain_mlp_sums[0], head_gain_sums[0], head_gain_sums[1])
     gain_sums = sum_over(jnp.concatenate(terms), "dp").reshape(-1, LANES)
-    sums = sum([give(gain_sums, count, k) if k else gain_sums for k in range(count)]).reshape(-1)
-    last_parts = line_scatter(
+    gain_parts = [gain_sums] + [give(gain_sums, count, k) for k in range(1, count)]
+    last_parts, hops = line_scatter(
         shares,
-        {1: (heads_partial, shares[0], sums, *given_second), 2: (own_sum,)},
+        {1: (heads_partial, shares[0], *gain_parts[1:], *given_second), 2: (own_sum,)},
     )
     grad_heads = grad_heads.astype(jnp.float32)
     grad_query, grad_key, grad_value = from_groups(grad_heads)
@@ -1209,6 +1212,7 @@
     grad_tokens, grad_out = tokens_back(last_parts, tokens_low, gain_attn, grad_resid)
     grad_tokens = grad_tokens.reshape(slots, rows, width)
 
+    sums = sum(gain_parts).reshape(-1)
     both_total = own_sum.astype(jnp.float32) + sum(
         jnp.concatenate(halves, axis=0).astype(jnp.float32)
         for halves in zip(given_first, given_second)

time: 950 us -> 935 us (0.984)
  waiting for transfers between devices: 412 us -> 354 us
  starting transfers between devices: 85.6 us -> 123 us
    ppermute x5, waiting for transfers between devices: 89.9 us -> 34.3 us  [fetch(): lax.ppermute(value, 'seq', [((i + step) % count, i) for i in range(count)])]
    ppermute x5, starting transfers between devices: 6.37 us -> 57.1 us  [fetch(): lax.ppermute(value, 'seq', [((i + step) % count, i) for i in range(count)])]
    ppermute x3, waiting for transfers between devices: 42.6 us -> 1.19 us  [hop_right(): lax.ppermute(value, 'seq', [(i, i + 1) for i in range(hop - 1, count - 1)])]
    ppermute x3, waiting for transfers between devices: 36.6 us -> 71.6 us  [hop_left(): lax.ppermute(value, 'seq', [(i, i - 1) for i in range(1, count - hop + 1)])]
    ppermute x12, waiting for transfers between devices: 123 us -> 88.4 us  [give(): lax.ppermute(value, 'seq', [(i, (i + step) % count) for i in range(count)])]
    ppermute x3, waiting for transfers between devices: 56.5 us -> 82.9 us  [line_scatter(): lax.ppermute(to_right.astype(jnp.bfloat16), 'seq', [(i, i + 1) for i in r...]
    ppermute x4, starting transfers between devices: 25.1 us -> 13.5 us  [swap(): return lax.ppermute(value, 'seq', [(i, i ^ 1) for i in range(count)])]
    unnamed x109 -> x119, local copies, waits for them, and re-layouts: 30.9 us -> 38.6 us
  transfers between devices with their start and end apart: 47 -> 47, of which waited for: 23 -> 24; matrix products, arithmetic and copies ran while one was open for 5% -> 5% of each run, Pallas kernels for 36% -> 36%
where the time goes in v4:
time: 935 us; the launch traced here: 927 us
  waiting for transfers between devices  354 us (38%)
  Pallas kernels  345 us (37%)
  starting transfers between devices  123 us (13%)
  local copies, waits for them, and re-layouts  51.5 us (6%)
  other arithmetic  37.7 us (4%)
  between operations  15.6 us (2%)
    ppermute x12, waiting for transfers between devices, give(): lax.ppermute(value, 'seq', [(i, (i + step) % count) for i in range(count)])  88.4 us
    ppermute x3, waiting for transfers between devices, line_scatter(): lax.ppermute(to_right.astype(jnp.bfloat16), 'seq', [(i, i + 1) for i in r...  82.9 us
    ppermute x3, waiting for transfers between devices, hop_left(): lax.ppermute(value, 'seq', [(i, i - 1) for i in range(1, count - hop + 1)])  71.6 us
    ppermute x5, starting transfers between devices, fetch(): lax.ppermute(value, 'seq', [((i + step) % count, i) for i in range(count)])  57.1 us
    ppermute x4, waiting for transfers between devices, swap(): return lax.ppermute(value, 'seq', [(i, i ^ 1) for i in range(count)])  56 us
    pallas_call x1, Pallas kernels, attend_backward(): pl.pallas_call(functools.partial(backward_kernel, block, groups, position...  46.4 us
    unnamed x119, local copies, waits for them, and re-layouts  38.6 us
    pallas_call x2, Pallas kernels, unit_grads(): pl.pallas_call(unit_grads_kernel, grid=(columns // tile,), in_specs=[fixe...  38.4 us
  transfers between devices with their start and end apart: 47, of which 24 were waited for; matrix products, arithmetic and copies ran while one was open for 5% of the time, Pallas kernels for 36%

profile of v4, /device:TPU:0, one launch (start us, length us, event | category | flops | bytes accessed | tf_op | source)
XLA Modules:
  0.0 926.5 jit_solution(16671405474363673528)
XLA Ops:
  20.0 42.7 %collective-permute-done.2.first_ref = bf16[512,2048]{1,0:T(8,128)(2,1)} collective-permute-done((bf16[512,2048]{1,0:T(8,128)(2,1)}, bf16[512,2048]{1,0:T(8,128)(2,1)}, u32[]{:S(2)}, u32[]{:S(2)}) %collective-permute-start.2) | collective-permute-done | bytes 2097184 | tf_op jit(solution)/shard_map/ppermute | solution.py:931
  85.9 28.9 %collective-permute-done.3.first_ref = bf16[512,2048]{1,0:T(8,128)(2,1)} collective-permute-done((bf16[512,2048]{1,0:T(8,128)(2,1)}, bf16[512,2048]{1,0:T(8,128)(2,1)}, u32[]{:S(2)}, u32[]{:S(2)}) %collective-permute-start.3) | collective-permute-done | bytes 2097184 | tf_op jit(solution)/shard_map/ppermute | solution.py:931
  150.7 46.4 %collective-permute-start.4 = (bf16[512,256]{1,0:T(8,128)(2,1)S(1)}, bf16[512,256]{1,0:T(8,128)(2,1)S(1)}, u32[]{:S(2)}, u32[]{:S(2)}) collective-permute-start(bf16[512,256]{1,0:T(8,128)(2,1)S(1)} %copy-done.52), channel_id=1, source_target_pairs={{1,0},{2,1},{3,2},{0,3},{5,4},{6,5},{7,6},{4,7},{9,8},{10,9},{11,1... | collective-permute-start | bytes 786440 | tf_op jit(solution)/shard_map/ppermute | solution.py:973
  225.2 24.8 %attend_forward.1 = (bf16[4,512,512]{2,1,0:T(8,128)(2,1)S(1)}, f32[4,8,2048]{2,1,0:T(8,128)S(1)}) custom-call(s32[2]{0:T(128)S(1)} %pad_add_fusion.2.place_ref, bf16[2048,1024]{1,0:T(8,128)(2,1)} %copy-done.9), custom_call_target="tpu_custom_call" | custom-call | flops 429496736 | bytes 419430 | tf_op jit(solution)/shard_map/attend_forward/pallas_call | solution.py:216
  250.7 20.0 %collective-permute-done.14 = bf16[256,3072]{1,0:T(8,128)(2,1)} collective-permute-done((bf16[256,3072]{1,0:T(8,128)(2,1)}, bf16[256,3072]{1,0:T(8,128)(2,1)}, u32[]{:S(2)}, u32[]{:S(2)}) %collective-permute-start.14) | collective-permute-done | bytes 1572896 | tf_op jit(solution)/shard_map/ppermute | solution.py:973
  274.7 11.4 %collective-permute-done.12.refs_3_ = bf16[512,512]{1,0:T(8,128)(2,1)S(1)} collective-permute-done((bf16[512,512]{1,0:T(8,128)(2,1)S(1)}, bf16[512,512]{1,0:T(8,128)(2,1)S(1)}, u32[]{:S(2)}, u32[]{:S(2)}) %collective-permute-start.12) | collective-permute-done | bytes 524320 | tf_op jit(solution)/shard_map/ppermute | solution.py:977
  286.1 31.8 %collective-permute-done.11.refs_2_ = bf16[512,512]{1,0:T(8,128)(2,1)S(1)} collective-permute-done((bf16[512,512]{1,0:T(8,128)(2,1)S(1)}, bf16[512,512]{1,0:T(8,128)(2,1)S(1)}, u32[]{:S(2)}, u32[]{:S(2)}) %collective-permute-start.11) | collective-permute-done | bytes 524320 | tf_op jit(solution)/shard_map/ppermute | solution.py:977
  336.1 42.9 %collective-permute-done.13.away_ref = bf16[512,2048]{1,0:T(8,128)(2,1)} collective-permute-done((bf16[512,2048]{1,0:T(8,128)(2,1)S(1)}, bf16[512,2048]{1,0:T(8,128)(2,1)}, u32[]{:S(2)}, u32[]{:S(2)}) %collective-permute-start.13) | collective-permute-done | bytes 2097184 | tf_op jit(solution)/shard_map/ppermute | solution.py:969
  379.7 18.9 %hidden_units.2 = (bf16[1024,3072]{1,0:T(8,128)(2,1)}, bf16[1024,3072]{1,0:T(8,128)(2,1)}) custom-call(bf16[512,2048]{1,0:T(8,128)(2,1)} %copy-done.14, bf16[512,2048]{1,0:T(8,128)(2,1)} %collective-permute-done.13.away_ref, bf16[2048,3072]{1,0:T(8,128)(2,1)} %all-gather.9.cloned.1.call-done.weight_ref.refs_2_), custom_call_target="tpu_custom_call" | custom-call | flops 644245120 | bytes 1415577 | tf_op jit(solution)/shard_map/hidden_units/pallas_call | solution.py:499
  398.6 18.8 %hidden_units.3 = (bf16[1024,3072]{1,0:T(8,128)(2,1)}, bf16[1024,3072]{1,0:T(8,128)(2,1)}) custom-call(bf16[512,2048]{1,0:T(8,128)(2,1)} %copy-done.14, bf16[512,2048]{1,0:T(8,128)(2,1)} %collective-permute-done.13.away_ref, bf16[2048,3072]{1,0:T(8,128)(2,1)} %all-gather.15.cloned.1.call-done.weight_ref.refs_3_, ...), custom_call_target="tpu_custom_call", output_to_operand_aliasing={{1}: (3, {})} | custom-call | flops 644245120 | bytes 1415577 | tf_op jit(solution)/shard_map/hidden_units/pallas_call | solution.py:499
  425.1 18.2 %down_grads.1 = bf16[3072,2048]{1,0:T(8,128)(2,1)} custom-call(bf16[1024,3072]{1,0:T(8,128)(2,1)} %get-tuple-element.117.hidden_ref, bf16[512,2048]{1,0:T(8,128)(2,1)} %broadcast_multiply_fusion.own_ref, bf16[512,2048]{1,0:T(8,128)(2,1)} %collective-permute-done.15.away_ref), custom_call_target="tpu_custom_call" | custom-call | flops 644245120 | bytes 943718 | tf_op jit(solution)/shard_map/down_grads/pallas_call | solution.py:592
  443.4 14.1 %hidden_back.3.grads_ref.refs_1_ = bf16[1024,3072]{1,0:T(8,128)(2,1)} custom-call(bf16[512,2048]{1,0:T(8,128)(2,1)} %broadcast_multiply_fusion.own_ref, bf16[512,2048]{1,0:T(8,128)(2,1)} %collective-permute-done.15.away_ref, bf16[1536,2048]{1,0:T(8,128)(2,1)} %all-gather.17.cloned.1.call-done.down_ref.refs_1_, bf16[1024,3072]{1,0:T(8,128)(2,1)} %get-tuple-element.112.both_ref), custom_call_target="tpu_custom_call" | custom-call | flops 322122560 | bytes 1258291 | tf_op jit(solution)/shard_map/hidden_back/pallas_call | solution.py:537
  457.5 19.8 %unit_grads.2 = bf16[2048,3072]{1,0:T(8,128)(2,1)} custom-call(bf16[512,2048]{1,0:T(8,128)(2,1)} %copy-done.14, bf16[512,2048]{1,0:T(8,128)(2,1)} %collective-permute-done.13.away_ref, bf16[1024,3072]{1,0:T(8,128)(2,1)} %hidden_back.3.grads_ref.refs_1_), custom_call_target="tpu_custom_call" | custom-call | flops 644245120 | bytes 943718 | tf_op jit(solution)/shard_map/unit_grads/pallas_call | solution.py:565
  477.5 13.9 %hidden_back.2.refs_0_.grads_ref = bf16[1024,3072]{1,0:T(8,128)(2,1)} custom-call(bf16[512,2048]{1,0:T(8,128)(2,1)} %broadcast_multiply_fusion.own_ref, bf16[512,2048]{1,0:T(8,128)(2,1)} %collective-permute-done.15.away_ref, bf16[1536,2048]{1,0:T(8,128)(2,1)} %all-gather.11.cloned.1.call-done.down_ref.refs_0_, bf16[1024,3072]{1,0:T(8,128)(2,1)} %get-tuple-element.110.both_ref), custom_call_target="tpu_custom_call" | custom-call | flops 322122560 | bytes 1258291 | tf_op jit(solution)/shard_map/hidden_back/pallas_call | solution.py:537
  491.4 34.5 %grad_normed.1 = (f32[512,2048]{1,0:T(8,128)}, bf16[512,2048]{1,0:T(8,128)(2,1)}) custom-call(bf16[1024,3072]{1,0:T(8,128)(2,1)} %hidden_back.2.refs_0_.grads_ref, bf16[1024,3072]{1,0:T(8,128)(2,1)} %hidden_back.3.grads_ref.refs_1_, bf16[2048,3072]{1,0:T(8,128)(2,1)} %all-gather.9.cloned.1.call-done.weight_ref.refs_2_, ...), custom_call_target="tpu_custom_call" | custom-call | flops 1288490240 | bytes 1887436 | tf_op jit(solution)/shard_map/grad_normed/pallas_call | solution.py:624
  527.5 18.6 %unit_grads.3 = bf16[2048,3072]{1,0:T(8,128)(2,1)} custom-call(bf16[512,2048]{1,0:T(8,128)(2,1)} %copy-done.14, bf16[512,2048]{1,0:T(8,128)(2,1)} %collective-permute-done.13.away_ref, bf16[1024,3072]{1,0:T(8,128)(2,1)} %hidden_back.2.refs_0_.grads_ref), custom_call_target="tpu_custom_call" | custom-call | flops 644245120 | bytes 943718 | tf_op jit(solution)/shard_map/unit_grads/pallas_call | solution.py:565
  546.1 19.9 %mlp_out.1 = (f32[512,2048]{1,0:T(8,128)}, bf16[512,2048]{1,0:T(8,128)(2,1)}) custom-call(bf16[1024,3072]{1,0:T(8,128)(2,1)} %get-tuple-element.117.hidden_ref, bf16[1536,2048]{1,0:T(8,128)(2,1)} %all-gather.11.cloned.1.call-done.down_ref.refs_0_, bf16[1536,2048]{1,0:T(8,128)(2,1)} %all-gather.17.cloned.1.call-done.down_ref.refs_1_), custom_call_target="tpu_custom_call" | custom-call | flops 644245120 | bytes 943718 | tf_op jit(solution)/shard_map/mlp_out/pallas_call | solution.py:661
  572.2 15.8 %resid_back.1 = (f32[512,2048]{1,0:T(8,128)}, bf16[512,2048]{1,0:T(8,128)(2,1)}, f32[1,2048]{1,0:T(1,128)}, bf16[512,512]{1,0:T(8,128)(2,1)}, bf16[512,512]{1,0:...) custom-call(s32[2]{0:T(128)} %pad_add_fusion.5.place_ref, f32[512,2048]{1,0:T(8,128)} %get-tuple-element.120.own_ref, ...), custom_call_target="tpu_custom_call" | custom-call | flops 214748368 | bytes 1468006 | tf_op jit(solution)/shard_map/resid_back/pallas_call | solution.py:716
  603.1 11.1 %collective-permute-done.17.refs_1_ = bf16[512,512]{1,0:T(8,128)(2,1)S(1)} collective-permute-done((bf16[512,512]{1,0:T(8,128)(2,1)S(1)}, bf16[512,512]{1,0:T(8,128)(2,1)S(1)}, u32[]{:S(2)}, u32[]{:S(2)}) %collective-permute-start.17) | collective-permute-done | bytes 524320 | tf_op jit(solution)/shard_map/ppermute | solution.py:977
  614.2 17.8 %collective-permute-done.18.refs_2_ = bf16[512,512]{1,0:T(8,128)(2,1)S(1)} collective-permute-done((bf16[512,512]{1,0:T(8,128)(2,1)S(1)}, bf16[512,512]{1,0:T(8,128)(2,1)S(1)}, u32[]{:S(2)}, u32[]{:S(2)}) %collective-permute-start.18) | collective-permute-done | bytes 524320 | tf_op jit(solution)/shard_map/ppermute | solution.py:977
  649.9 46.4 %attend_backward.1 = (bf16[2048,1024]{1,0:T(8,128)(2,1)}, f32[2,2,128]{2,1,0:T(2,128)}) custom-call(s32[2]{0:T(128)} %copy-done.37, bf16[2048,1024]{1,0:T(8,128)(2,1)} %copy-done.9, f32[2048,768]{1,0:T(8,128)} %get-tuple-element.132.raw_ref, f32[2048,128]{1,0:T(8,128)} %copy-done.10, f32[2048,128]{1,0:T(8,128)} %copy-done.11, f32[2,128]{1,0:T(2,128)} %copy-done.36, ...), custom_call_target="tpu_custom_call" | custom-call | flops 107374184 | bytes 104857 | tf_op jit(solution)/shard_map/attend_backward/pallas_call | solution.py:382
  730.7 13.8 %heads_back.1 = (bf16[2048,1024]{1,0:T(8,128)(2,1)S(1)}, f32[2048,128]{1,0:T(8,128)S(1)}) custom-call(bf16[2048,2048]{1,0:T(8,128)(2,1)} %get-tuple-element.139.normed_ref, bf16[2048,1024]{1,0:T(8,128)(2,1)} %get-tuple-element.140.grads_ref.grad_ref, bf16[2048,1024]{1,0:T(8,128)(2,1)} %copy-done), custom_call_target="tpu_custom_call" | custom-call | flops 429496736 | bytes 1048576 | tf_op jit(solution)/shard_map/heads_back/pallas_call | solution.py:890
  816.1 34.3 %collective-permute-done.32 = bf16[512,2304]{1,0:T(8,128)(2,1)} collective-permute-done((bf16[512,2304]{1,0:T(8,128)(2,1)}, bf16[512,2304]{1,0:T(8,128)(2,1)}, u32[]{:S(2)}, u32[]{:S(2)}) %collective-permute-start.32) | collective-permute-done | bytes 2359328 | tf_op jit(solution)/shard_map/ppermute | solution.py:945
  869.8 39.1 %collective-permute-done.34.right_ref = bf16[512,2304]{1,0:T(8,128)(2,1)S(1)} collective-permute-done((bf16[512,2304]{1,0:T(8,128)(2,1)}, bf16[512,2304]{1,0:T(8,128)(2,1)S(1)}, u32[]{:S(2)}, u32[]{:S(2)}) %collective-permute-start.34) | collective-permute-done | bytes 2359328 | tf_op jit(solution)/shard_map/ppermute | solution.py:945
  (280 shorter events, 306.9 us)
Async XLA Ops:
  7.2 66.1 %all-gather.7.cloned.1.call-start = ((), (), s32[]{:S(2)}) async-start(), calls=%async_computation.5 | async-start | bytes 5308416 | tf_op jit(solution)/shard_map/all_gather | solution.py:1029
  11.8 190.5 %all-gather.11.cloned.1.call-start = ((), (), s32[]{:S(2)}) async-start(), calls=%async_computation.7 | async-start | bytes 7077888 | tf_op jit(solution)/shard_map/all_gather | solution.py:1069
  11.9 50.9 %collective-permute-start.2 = (bf16[512,2048]{1,0:T(8,128)(2,1)}, bf16[512,2048]{1,0:T(8,128)(2,1)}, u32[]{:S(2)}, u32[]{:S(2)}) collective-permute-start(bf16[512,2048]{1,0:T(8,128)(2,1)} %bitcast.59), channel_id=1, source_target_pairs={{1,0},{2,1},{3,2},{5,4},{6,5},{7,6},{9,8},{10,9},{11,10},{13,12},{... | collective-permute-start | bytes 6291464 | tf_op jit(solution)/shard_map/ppermute | solution.py:931
  63.9 138.3 %all-gather.9.cloned.1.call-start = ((), (), s32[]{:S(2)}) async-start(), calls=%async_computation.6 | async-start | bytes 14155776 | tf_op jit(solution)/shard_map/all_gather | solution.py:1068
  65.3 254.1 %all-gather.13.cloned.1.call-start = ((), (), s32[]{:S(2)}) async-start(), calls=%async_computation.8 | async-start | bytes 9437184 | tf_op jit(solution)/shard_map/all_gather | solution.py:1085
  114.8 87.4 %collective-permute-start.7 = (bf16[512,2048]{1,0:T(8,128)(2,1)}, bf16[512,2048]{1,0:T(8,128)(2,1)}, u32[]{:S(2)}, u32[]{:S(2)}) collective-permute-start(bf16[512,2048]{1,0:T(8,128)(2,1)} %collective-permute-done.1.second_ref), channel_id=1, source_target_pairs={{2,3},{6,7},{10,11},{14,15},{18,19},{22,23},{26,27},{30,31}} | collective-permute-start | bytes 6291464 | tf_op jit(solution)/shard_map/ppermute | solution.py:927
  116.8 85.4 %collective-permute-start.8 = (bf16[512,2048]{1,0:T(8,128)(2,1)}, bf16[512,2048]{1,0:T(8,128)(2,1)}, u32[]{:S(2)}, u32[]{:S(2)}) collective-permute-start(bf16[512,2048]{1,0:T(8,128)(2,1)} %collective-permute-done.3.first_ref), channel_id=1, source_target_pairs={{1,0},{5,4},{9,8},{13,12},{17,16},{21,20},{25,24},{29,28}} | collective-permute-start | bytes 6291464 | tf_op jit(solution)/shard_map/ppermute | solution.py:931
  118.1 84.1 %collective-permute-start.9 = (bf16[1536,256]{1,0:T(8,128)(2,1)S(1)}, bf16[1536,256]{1,0:T(8,128)(2,1)}, u32[]{:S(2)}, u32[]{:S(2)}) collective-permute-start(bf16[1536,256]{1,0:T(8,128)(2,1)S(1)} %copy-done.48), channel_id=1, source_target_pairs={{2,0},{3,1},{0,2},{1,3},{6,4},{7,5},{4,6},{5,7},{10,8},{11,9},{8,1... | collective-permute-start | bytes 2359304 | tf_op jit(solution)/shard_map/ppermute | solution.py:973
  140.0 57.1 %collective-permute-start.5 = (bf16[512,256]{1,0:T(8,128)(2,1)S(1)}, bf16[512,256]{1,0:T(8,128)(2,1)S(1)}, u32[]{:S(2)}, u32[]{:S(2)}) collective-permute-start(bf16[512,256]{1,0:T(8,128)(2,1)S(1)} %copy-done.52), channel_id=1, source_target_pairs={{2,0},{3,1},{0,2},{1,3},{6,4},{7,5},{4,6},{5,7},{10,8},{11,9},{8,1... | collective-permute-start | bytes 786440 | tf_op jit(solution)/shard_map/ppermute | solution.py:973
  202.3 196.3 %all-gather.15.cloned.1.call-start = ((), (), s32[]{:S(2)}) async-start(), calls=%async_computation.9 | async-start | bytes 14155776 | tf_op jit(solution)/shard_map/all_gather | solution.py:1110
  202.6 68.1 %collective-permute-start.14 = (bf16[256,3072]{1,0:T(8,128)(2,1)}, bf16[256,3072]{1,0:T(8,128)(2,1)}, u32[]{:S(2)}, u32[]{:S(2)}) collective-permute-start(bf16[256,3072]{1,0:T(8,128)(2,1)} %pack_units.1), channel_id=1, source_target_pairs={{2,0},{3,1},{0,2},{1,3},{6,4},{7,5},{4,6},{5,7},{10,8},{11,9},{8,1... | collective-permute-start | bytes 4718600 | tf_op jit(solution)/shard_map/ppermute | solution.py:973
  270.7 172.7 %all-gather.17.cloned.1.call-start = ((), (), s32[]{:S(2)}) async-start(), calls=%async_computation.10 | async-start | bytes 7077888 | tf_op jit(solution)/shard_map/all_gather | solution.py:1111
  271.3 299.7 %reduce-scatter.8.cloned.1.call-start = ((), (), s32[]{:S(2)}) async-start(), calls=%async_computation.12 | async-start | bytes 14155776 | tf_op jit(solution)/shard_map/reduce_scatter | solution.py:1125
  443.3 190.4 %reduce-scatter.6.cloned.1.call-start = ((), (), s32[]{:S(2)}) async-start(), calls=%async_computation.11 | async-start | bytes 14155776 | tf_op jit(solution)/shard_map/reduce_scatter | solution.py:1125
  477.3 230.0 %reduce-scatter.10.cloned.1.call-start = ((), (), s32[]{:S(2)}) async-start(), calls=%async_computation.13 | async-start | bytes 9437184 | tf_op jit(solution)/shard_map/reduce_scatter | solution.py:1125
  596.5 260.3 %reduce-scatter.12.cloned.1.call-start = ((), (), s32[]{:S(2)}) async-start(), calls=%async_computation.14 | async-start | bytes 14155776 | tf_op jit(solution)/shard_map/reduce_scatter | solution.py:1125
  633.7 229.2 %reduce-scatter.14.cloned.1.call-start = ((), (), s32[]{:S(2)}) async-start(), calls=%async_computation.15 | async-start | bytes 4718592 | tf_op jit(solution)/shard_map/reduce_scatter | solution.py:1125
  633.8 90.8 %collective-permute-start.20 = (bf16[512,2048]{1,0:T(8,128)(2,1)}, bf16[512,2048]{1,0:T(8,128)(2,1)}, u32[]{:S(2)}, u32[]{:S(2)}) collective-permute-start(bf16[512,2048]{1,0:T(8,128)(2,1)} %get-tuple-element.131), channel_id=1, source_target_pairs={{0,1},{1,0},{2,3},{3,2},{4,5},{5,4},{6,7},{7,6},{8,9},{9,8},{10,11... | collective-permute-start | bytes 6291464 | tf_op jit(solution)/shard_map/ppermute | solution.py:969
  645.7 73.5 %collective-permute-start.21 = (bf16[1536,256]{1,0:T(8,128)(2,1)}, bf16[1536,256]{1,0:T(8,128)(2,1)}, u32[]{:S(2)}, u32[]{:S(2)}) collective-permute-start(bf16[1536,256]{1,0:T(8,128)(2,1)} %split.12), channel_id=1, source_target_pairs={{0,2},{1,3},{2,0},{3,1},{4,6},{5,7},{6,4},{7,5},{8,10},{9,11},{10,... | collective-permute-start | bytes 2359304 | tf_op jit(solution)/shard_map/ppermute | solution.py:977
  649.5 74.4 %collective-permute-start.22 = (bf16[128,3072]{1,0:T(8,128)(2,1)}, bf16[128,3072]{1,0:T(8,128)(2,1)S(1)}, u32[]{:S(2)}, u32[]{:S(2)}) collective-permute-start(bf16[128,3072]{1,0:T(8,128)(2,1)} %get-tuple-element.166), channel_id=1, source_target_pairs={{0,2},{1,3},{2,0},{3,1},{4,6},{5,7},{6,4},{7,5},{8,10},{9,11},{10,... | collective-permute-start | bytes 2359304 | tf_op jit(solution)/shard_map/ppermute | solution.py:977
  726.7 54.2 %collective-permute-start.23 = (bf16[512,2304]{1,0:T(8,128)(2,1)S(1)}, bf16[512,2304]{1,0:T(8,128)(2,1)}, u32[]{:S(2)}, u32[]{:S(2)}) collective-permute-start(bf16[512,2304]{1,0:T(8,128)(2,1)S(1)} %share.6), channel_id=1, source_target_pairs={{0,1},{4,5},{8,9},{12,13},{16,17},{20,21},{24,25},{28,29}} | collective-permute-start | bytes 7077896 | tf_op jit(solution)/shard_map/ppermute | solution.py:945
  799.1 51.3 %collective-permute-start.32 = (bf16[512,2304]{1,0:T(8,128)(2,1)}, bf16[512,2304]{1,0:T(8,128)(2,1)}, u32[]{:S(2)}, u32[]{:S(2)}) collective-permute-start(bf16[512,2304]{1,0:T(8,128)(2,1)} %get-tuple-element.145), channel_id=1, source_target_pairs={{0,1},{1,2},{4,5},{5,6},{8,9},{9,10},{12,13},{13,14},{16,17},{17,1... | collective-permute-start | bytes 7077896 | tf_op jit(solution)/shard_map/ppermute | solution.py:945
  856.8 52.2 %collective-permute-start.34 = (bf16[512,2304]{1,0:T(8,128)(2,1)}, bf16[512,2304]{1,0:T(8,128)(2,1)S(1)}, u32[]{:S(2)}, u32[]{:S(2)}) collective-permute-start(bf16[512,2304]{1,0:T(8,128)(2,1)} %convert_add_fusion.3), channel_id=1, source_target_pairs={{0,1},{1,2},{2,3},{4,5},{5,6},{6,7},{8,9},{9,10},{10,11},{12,13},{... | collective-permute-start | bytes 7077896 | tf_op jit(solution)/shard_map/ppermute | solution.py:945
  861.6 51.6 %collective-permute-start.35 = (bf16[512,2304]{1,0:T(8,128)(2,1)}, bf16[512,2304]{1,0:T(8,128)(2,1)}, u32[]{:S(2)}, u32[]{:S(2)}) collective-permute-start(bf16[512,2304]{1,0:T(8,128)(2,1)} %convert_add_fusion.2), channel_id=1, source_target_pairs={{1,0},{2,1},{3,2},{5,4},{6,5},{7,6},{9,8},{10,9},{11,10},{13,12},{... | collective-permute-start | bytes 7077896 | tf_op jit(solution)/shard_map/ppermute | solution.py:948
  (81 other events, 1740.4 us)
Sparse Core Ops, SparseCore 0:
  11.9 41.6 all-gather.6
  64.1 50.2 all-gather.10
  116.9 72.1 all-gather.8
  202.4 57.8 all-gather.12
  270.8 71.9 all-gather.14
  344.5 46.6 all-gather.16
  443.4 93.1 reduce-scatter.7
  540.1 92.3 reduce-scatter.5
  636.0 71.2 reduce-scatter.9
  711.0 92.8 reduce-scatter.11
  807.7 51.3 reduce-scatter.13

commit v5 on v4

--- a/solution.py
+++ b/solution.py
@@ -99,7 +99,7 @@
             column = start + g * size
             value = raw[:, column : column + size]
             held = (h * (groups + 1) + g) * size
-            raw_ref[:, held : held + size] = value
+            raw_ref[:, held : held + size] = value.astype(raw_ref.dtype)
             which = 0 if g < groups else 1
             value = value * lax.rsqrt(jnp.mean(value * value, axis=-1, keepdims=True) + EPS)
             value = value * head_gain_ref[which : which + 1, :]
@@ -154,7 +154,7 @@
         out_shape=(
             jax.ShapeDtypeStruct((positions, width), jnp.bfloat16),
             jax.ShapeDtypeStruct((positions, columns), jnp.bfloat16),
-            jax.ShapeDtypeStruct((positions, held), jnp.float32),
+            jax.ShapeDtypeStruct((positions, held), jnp.bfloat16),
         ),
         input_output_aliases=aliases,
         compiler_params=arbitrary(1, 40),
@@ -350,7 +350,7 @@
             which = 0 if g < groups else 1
             grad = grad.astype(jnp.bfloat16).astype(jnp.float32)
             grad = grad * cosine - pltpu.roll(grad, size // 2, 1) * sine_table
-            value = raw_ref[rows, lanes]
+            value = raw_ref[rows, lanes].astype(jnp.float32)
             scale = lax.rsqrt(jnp.mean(value * value, axis=-1, keepdims=True) + EPS)
             unit = value * scale
             sums[which] = sums[which] + jnp.sum(grad * unit, axis=0, keepdims=True)

time: 935 us -> 945 us (1.011)
  waiting for transfers between devices: 354 us -> 340 us
    reduce_scatter x5, waiting for transfers between devices: 11 us -> 0.06 us  [spread(): return lax.psum_scatter(partial, 'dp', scatter_dimension=axis, tiled=True)]
    unnamed x119 -> x125, local copies, waits for them, and re-layouts: 38.6 us -> 44.4 us
  transfers between devices with their start and end apart: 47 -> 47, of which waited for: 24 -> 23; matrix products, arithmetic and copies ran while one was open for 5% -> 6% of each run, Pallas kernels for 36% -> 36%
where the time goes in v5:
time: 945 us; the launch traced here: 936 us
  Pallas kernels  349 us (37%)
  waiting for transfers between devices  340 us (36%)
  starting transfers between devices  132 us (14%)
  local copies, waits for them, and re-layouts  60.3 us (6%)
  other arithmetic  40.4 us (4%)
  between operations  15.6 us (2%)
    ppermute x12, waiting for transfers between devices, give(): lax.ppermute(value, 'seq', [(i, (i + step) % count) for i in range(count)])  95.3 us
    ppermute x3, waiting for transfers between devices, line_scatter(): lax.ppermute(to_right.astype(jnp.bfloat16), 'seq', [(i, i + 1) for i in r...  81.1 us
    ppermute x3, waiting for transfers between devices, hop_left(): lax.ppermute(value, 'seq', [(i, i - 1) for i in range(1, count - hop + 1)])  67.8 us
    ppermute x4, waiting for transfers between devices, swap(): return lax.ppermute(value, 'seq', [(i, i ^ 1) for i in range(count)])  55.9 us
    ppermute x5, starting transfers between devices, fetch(): lax.ppermute(value, 'seq', [((i + step) % count, i) for i in range(count)])  55.7 us
    pallas_call x1, Pallas kernels, attend_backward(): pl.pallas_call(functools.partial(backward_kernel, block, groups, position...  49.3 us
    unnamed x125, local copies, waits for them, and re-layouts  44.4 us
    pallas_call x2, Pallas kernels, unit_grads(): pl.pallas_call(unit_grads_kernel, grid=(columns // tile,), in_specs=[fixe...  38.5 us
  transfers between devices with their start and end apart: 47, of which 23 were waited for; matrix products, arithmetic and copies ran while one was open for 6% of the time, Pallas kernels for 36%

profile of v5, /device:TPU:0, one launch (start us, length us, event | category | flops | bytes accessed | tf_op | source)
XLA Modules:
  0.0 936.3 jit_solution(11472551251653374042)
XLA Ops:
  20.1 42.6 %collective-permute-done.2.first_ref = bf16[512,2048]{1,0:T(8,128)(2,1)} collective-permute-done((bf16[512,2048]{1,0:T(8,128)(2,1)}, bf16[512,2048]{1,0:T(8,128)(2,1)}, u32[]{:S(2)}, u32[]{:S(2)}) %collective-permute-start.2) | collective-permute-done | bytes 2097184 | tf_op jit(solution)/shard_map/ppermute | solution.py:931
  89.7 25.1 %collective-permute-done.3.first_ref = bf16[512,2048]{1,0:T(8,128)(2,1)} collective-permute-done((bf16[512,2048]{1,0:T(8,128)(2,1)}, bf16[512,2048]{1,0:T(8,128)(2,1)}, u32[]{:S(2)}, u32[]{:S(2)}) %collective-permute-start.3) | collective-permute-done | bytes 2097184 | tf_op jit(solution)/shard_map/ppermute | solution.py:931
  152.0 45.2 %collective-permute-start.4 = (bf16[512,256]{1,0:T(8,128)(2,1)S(1)}, bf16[512,256]{1,0:T(8,128)(2,1)S(1)}, u32[]{:S(2)}, u32[]{:S(2)}) collective-permute-start(bf16[512,256]{1,0:T(8,128)(2,1)S(1)} %copy-done.55), channel_id=1, source_target_pairs={{1,0},{2,1},{3,2},{0,3},{5,4},{6,5},{7,6},{4,7},{9,8},{10,9},{11,1... | collective-permute-start | bytes 786440 | tf_op jit(solution)/shard_map/ppermute | solution.py:973
  225.8 27.2 %attend_forward.1 = (bf16[4,512,512]{2,1,0:T(8,128)(2,1)S(1)}, f32[4,8,2048]{2,1,0:T(8,128)S(1)}) custom-call(s32[2]{0:T(128)S(1)} %pad_add_fusion.2.place_ref, bf16[2048,1024]{1,0:T(8,128)(2,1)} %copy-done.8), custom_call_target="tpu_custom_call" | custom-call | flops 429496736 | bytes 419430 | tf_op jit(solution)/shard_map/attend_forward/pallas_call | solution.py:216
  255.0 15.5 %collective-permute-done.14 = bf16[256,3072]{1,0:T(8,128)(2,1)} collective-permute-done((bf16[256,3072]{1,0:T(8,128)(2,1)}, bf16[256,3072]{1,0:T(8,128)(2,1)}, u32[]{:S(2)}, u32[]{:S(2)}) %collective-permute-start.14) | collective-permute-done | bytes 1572896 | tf_op jit(solution)/shard_map/ppermute | solution.py:973
  275.8 11.7 %collective-permute-done.12.refs_3_ = bf16[512,512]{1,0:T(8,128)(2,1)S(1)} collective-permute-done((bf16[512,512]{1,0:T(8,128)(2,1)S(1)}, bf16[512,512]{1,0:T(8,128)(2,1)S(1)}, u32[]{:S(2)}, u32[]{:S(2)}) %collective-permute-start.12) | collective-permute-done | bytes 524320 | tf_op jit(solution)/shard_map/ppermute | solution.py:977
  287.6 31.8 %collective-permute-done.11.refs_2_ = bf16[512,512]{1,0:T(8,128)(2,1)S(1)} collective-permute-done((bf16[512,512]{1,0:T(8,128)(2,1)S(1)}, bf16[512,512]{1,0:T(8,128)(2,1)S(1)}, u32[]{:S(2)}, u32[]{:S(2)}) %collective-permute-start.11) | collective-permute-done | bytes 524320 | tf_op jit(solution)/shard_map/ppermute | solution.py:977
  337.7 42.9 %collective-permute-done.13.away_ref = bf16[512,2048]{1,0:T(8,128)(2,1)} collective-permute-done((bf16[512,2048]{1,0:T(8,128)(2,1)S(1)}, bf16[512,2048]{1,0:T(8,128)(2,1)}, u32[]{:S(2)}, u32[]{:S(2)}) %collective-permute-start.13) | collective-permute-done | bytes 2097184 | tf_op jit(solution)/shard_map/ppermute | solution.py:969
  381.5 18.9 %hidden_units.2 = (bf16[1024,3072]{1,0:T(8,128)(2,1)}, bf16[1024,3072]{1,0:T(8,128)(2,1)}) custom-call(bf16[512,2048]{1,0:T(8,128)(2,1)} %copy-done.18, bf16[512,2048]{1,0:T(8,128)(2,1)} %collective-permute-done.13.away_ref, bf16[2048,3072]{1,0:T(8,128)(2,1)} %all-gather.9.cloned.1.call-done.weight_ref.refs_2_), custom_call_target="tpu_custom_call" | custom-call | flops 644245120 | bytes 1415577 | tf_op jit(solution)/shard_map/hidden_units/pallas_call | solution.py:499
  400.3 18.9 %hidden_units.3 = (bf16[1024,3072]{1,0:T(8,128)(2,1)}, bf16[1024,3072]{1,0:T(8,128)(2,1)}) custom-call(bf16[512,2048]{1,0:T(8,128)(2,1)} %copy-done.18, bf16[512,2048]{1,0:T(8,128)(2,1)} %collective-permute-done.13.away_ref, bf16[2048,3072]{1,0:T(8,128)(2,1)} %all-gather.15.cloned.1.call-done.weight_ref.refs_3_, ...), custom_call_target="tpu_custom_call", output_to_operand_aliasing={{1}: (3, {})} | custom-call | flops 644245120 | bytes 1415577 | tf_op jit(solution)/shard_map/hidden_units/pallas_call | solution.py:499
  426.7 18.2 %down_grads.1 = bf16[3072,2048]{1,0:T(8,128)(2,1)} custom-call(bf16[1024,3072]{1,0:T(8,128)(2,1)} %get-tuple-element.117.hidden_ref, bf16[512,2048]{1,0:T(8,128)(2,1)} %broadcast_multiply_fusion.own_ref, bf16[512,2048]{1,0:T(8,128)(2,1)} %collective-permute-done.15.away_ref), custom_call_target="tpu_custom_call" | custom-call | flops 644245120 | bytes 943718 | tf_op jit(solution)/shard_map/down_grads/pallas_call | solution.py:592
  445.1 14.1 %hidden_back.3.grads_ref.refs_1_ = bf16[1024,3072]{1,0:T(8,128)(2,1)} custom-call(bf16[512,2048]{1,0:T(8,128)(2,1)} %broadcast_multiply_fusion.own_ref, bf16[512,2048]{1,0:T(8,128)(2,1)} %collective-permute-done.15.away_ref, bf16[1536,2048]{1,0:T(8,128)(2,1)} %all-gather.17.cloned.1.call-done.down_ref.refs_1_, bf16[1024,3072]{1,0:T(8,128)(2,1)} %get-tuple-element.112.both_ref), custom_call_target="tpu_custom_call" | custom-call | flops 322122560 | bytes 1258291 | tf_op jit(solution)/shard_map/hidden_back/pallas_call | solution.py:537
  459.2 19.8 %unit_grads.2 = bf16[2048,3072]{1,0:T(8,128)(2,1)} custom-call(bf16[512,2048]{1,0:T(8,128)(2,1)} %copy-done.18, bf16[512,2048]{1,0:T(8,128)(2,1)} %collective-permute-done.13.away_ref, bf16[1024,3072]{1,0:T(8,128)(2,1)} %hidden_back.3.grads_ref.refs_1_), custom_call_target="tpu_custom_call" | custom-call | flops 644245120 | bytes 943718 | tf_op jit(solution)/shard_map/unit_grads/pallas_call | solution.py:565
  487.3 14.0 %hidden_back.2.refs_0_.grads_ref = bf16[1024,3072]{1,0:T(8,128)(2,1)} custom-call(bf16[512,2048]{1,0:T(8,128)(2,1)} %broadcast_multiply_fusion.own_ref, bf16[512,2048]{1,0:T(8,128)(2,1)} %collective-permute-done.15.away_ref, bf16[1536,2048]{1,0:T(8,128)(2,1)} %all-gather.11.cloned.1.call-done.down_ref.refs_0_, bf16[1024,3072]{1,0:T(8,128)(2,1)} %get-tuple-element.110.both_ref), custom_call_target="tpu_custom_call" | custom-call | flops 322122560 | bytes 1258291 | tf_op jit(solution)/shard_map/hidden_back/pallas_call | solution.py:537
  501.3 34.2 %grad_normed.1 = (f32[512,2048]{1,0:T(8,128)}, bf16[512,2048]{1,0:T(8,128)(2,1)}) custom-call(bf16[1024,3072]{1,0:T(8,128)(2,1)} %hidden_back.2.refs_0_.grads_ref, bf16[1024,3072]{1,0:T(8,128)(2,1)} %hidden_back.3.grads_ref.refs_1_, bf16[2048,3072]{1,0:T(8,128)(2,1)} %all-gather.9.cloned.1.call-done.weight_ref.refs_2_, ...), custom_call_target="tpu_custom_call" | custom-call | flops 1288490240 | bytes 1887436 | tf_op jit(solution)/shard_map/grad_normed/pallas_call | solution.py:624
  537.1 18.7 %unit_grads.3 = bf16[2048,3072]{1,0:T(8,128)(2,1)} custom-call(bf16[512,2048]{1,0:T(8,128)(2,1)} %copy-done.18, bf16[512,2048]{1,0:T(8,128)(2,1)} %collective-permute-done.13.away_ref, bf16[1024,3072]{1,0:T(8,128)(2,1)} %hidden_back.2.refs_0_.grads_ref), custom_call_target="tpu_custom_call" | custom-call | flops 644245120 | bytes 943718 | tf_op jit(solution)/shard_map/unit_grads/pallas_call | solution.py:565
  555.7 20.0 %mlp_out.1 = (f32[512,2048]{1,0:T(8,128)}, bf16[512,2048]{1,0:T(8,128)(2,1)}) custom-call(bf16[1024,3072]{1,0:T(8,128)(2,1)} %get-tuple-element.117.hidden_ref, bf16[1536,2048]{1,0:T(8,128)(2,1)} %all-gather.11.cloned.1.call-done.down_ref.refs_0_, bf16[1536,2048]{1,0:T(8,128)(2,1)} %all-gather.17.cloned.1.call-done.down_ref.refs_1_), custom_call_target="tpu_custom_call" | custom-call | flops 644245120 | bytes 943718 | tf_op jit(solution)/shard_map/mlp_out/pallas_call | solution.py:661
  581.9 15.8 %resid_back.1 = (f32[512,2048]{1,0:T(8,128)}, bf16[512,2048]{1,0:T(8,128)(2,1)}, f32[1,2048]{1,0:T(1,128)}, bf16[512,512]{1,0:T(8,128)(2,1)}, bf16[512,512]{1,0:...) custom-call(s32[2]{0:T(128)} %pad_add_fusion.5.place_ref, f32[512,2048]{1,0:T(8,128)} %get-tuple-element.120.own_ref, ...), custom_call_target="tpu_custom_call" | custom-call | flops 214748368 | bytes 1468006 | tf_op jit(solution)/shard_map/resid_back/pallas_call | solution.py:716
  624.0 18.4 %collective-permute-done.18.refs_2_ = bf16[512,512]{1,0:T(8,128)(2,1)S(1)} collective-permute-done((bf16[512,512]{1,0:T(8,128)(2,1)S(1)}, bf16[512,512]{1,0:T(8,128)(2,1)S(1)}, u32[]{:S(2)}, u32[]{:S(2)}) %collective-permute-start.18) | collective-permute-done | bytes 524320 | tf_op jit(solution)/shard_map/ppermute | solution.py:977
  660.9 49.3 %attend_backward.1 = (bf16[2048,1024]{1,0:T(8,128)(2,1)}, f32[2,2,128]{2,1,0:T(2,128)}) custom-call(s32[2]{0:T(128)} %copy-done.41, bf16[2048,1024]{1,0:T(8,128)(2,1)} %copy-done.8, bf16[2048,768]{1,0:T(8,128)(2,1)} %copy-done.9, f32[2048,128]{1,0:T(8,128)} %get-tuple-element.187.cosine_ref, f32[2048,128]{1,0:T(8,128)} %get-tuple-element.188.sine_ref, ...), custom_call_target="tpu_custom_call" | custom-call | flops 107374184 | bytes 104857 | tf_op jit(solution)/shard_map/attend_backward/pallas_call | solution.py:382
  722.2 12.1 %collective-permute-done.22 = bf16[128,3072]{1,0:T(8,128)(2,1)S(1)} collective-permute-done((bf16[128,3072]{1,0:T(8,128)(2,1)}, bf16[128,3072]{1,0:T(8,128)(2,1)S(1)}, u32[]{:S(2)}, u32[]{:S(2)}) %collective-permute-start.22) | collective-permute-done | bytes 786464 | tf_op jit(solution)/shard_map/ppermute | solution.py:977
  741.1 14.2 %heads_back.1 = (bf16[2048,1024]{1,0:T(8,128)(2,1)S(1)}, f32[2048,128]{1,0:T(8,128)S(1)}) custom-call(bf16[2048,2048]{1,0:T(8,128)(2,1)} %get-tuple-element.139.normed_ref, bf16[2048,1024]{1,0:T(8,128)(2,1)} %get-tuple-element.140.grads_ref.grad_ref, bf16[2048,1024]{1,0:T(8,128)(2,1)} %slice.128.weight_ref), custom_call_target="tpu_custom_call" | custom-call | flops 429496736 | bytes 1048576 | tf_op jit(solution)/shard_map/heads_back/pallas_call | solution.py:890
  827.5 32.8 %collective-permute-done.32 = bf16[512,2304]{1,0:T(8,128)(2,1)} collective-permute-done((bf16[512,2304]{1,0:T(8,128)(2,1)}, bf16[512,2304]{1,0:T(8,128)(2,1)}, u32[]{:S(2)}, u32[]{:S(2)}) %collective-permute-start.32) | collective-permute-done | bytes 2359328 | tf_op jit(solution)/shard_map/ppermute | solution.py:945
  879.8 39.0 %collective-permute-done.34.right_ref = bf16[512,2304]{1,0:T(8,128)(2,1)S(1)} collective-permute-done((bf16[512,2304]{1,0:T(8,128)(2,1)}, bf16[512,2304]{1,0:T(8,128)(2,1)S(1)}, u32[]{:S(2)}, u32[]{:S(2)}) %collective-permute-start.34) | collective-permute-done | bytes 2359328 | tf_op jit(solution)/shard_map/ppermute | solution.py:945
  (286 shorter events, 320.2 us)
Async XLA Ops:
  7.2 67.4 %all-gather.7.cloned.1.call-start = ((), (), s32[]{:S(2)}) async-start(), calls=%async_computation.5 | async-start | bytes 5308416 | tf_op jit(solution)/shard_map/all_gather | solution.py:1029
  11.8 190.6 %all-gather.11.cloned.1.call-start = ((), (), s32[]{:S(2)}) async-start(), calls=%async_computation.7 | async-start | bytes 7077888 | tf_op jit(solution)/shard_map/all_gather | solution.py:1069
  11.9 50.9 %collective-permute-start.2 = (bf16[512,2048]{1,0:T(8,128)(2,1)}, bf16[512,2048]{1,0:T(8,128)(2,1)}, u32[]{:S(2)}, u32[]{:S(2)}) collective-permute-start(bf16[512,2048]{1,0:T(8,128)(2,1)} %bitcast.59), channel_id=1, source_target_pairs={{1,0},{2,1},{3,2},{5,4},{6,5},{7,6},{9,8},{10,9},{11,10},{13,12},{... | collective-permute-start | bytes 6291464 | tf_op jit(solution)/shard_map/ppermute | solution.py:931
  63.9 138.5 %all-gather.9.cloned.1.call-start = ((), (), s32[]{:S(2)}) async-start(), calls=%async_computation.6 | async-start | bytes 14155776 | tf_op jit(solution)/shard_map/all_gather | solution.py:1068
  65.3 255.6 %all-gather.13.cloned.1.call-start = ((), (), s32[]{:S(2)}) async-start(), calls=%async_computation.8 | async-start | bytes 9437184 | tf_op jit(solution)/shard_map/all_gather | solution.py:1085
  114.8 87.6 %collective-permute-start.7 = (bf16[512,2048]{1,0:T(8,128)(2,1)}, bf16[512,2048]{1,0:T(8,128)(2,1)}, u32[]{:S(2)}, u32[]{:S(2)}) collective-permute-start(bf16[512,2048]{1,0:T(8,128)(2,1)} %collective-permute-done.1.second_ref), channel_id=1, source_target_pairs={{2,3},{6,7},{10,11},{14,15},{18,19},{22,23},{26,27},{30,31}} | collective-permute-start | bytes 6291464 | tf_op jit(solution)/shard_map/ppermute | solution.py:927
  116.8 85.5 %collective-permute-start.8 = (bf16[512,2048]{1,0:T(8,128)(2,1)}, bf16[512,2048]{1,0:T(8,128)(2,1)}, u32[]{:S(2)}, u32[]{:S(2)}) collective-permute-start(bf16[512,2048]{1,0:T(8,128)(2,1)} %collective-permute-done.3.first_ref), channel_id=1, source_target_pairs={{1,0},{5,4},{9,8},{13,12},{17,16},{21,20},{25,24},{29,28}} | collective-permute-start | bytes 6291464 | tf_op jit(solution)/shard_map/ppermute | solution.py:931
  118.1 84.2 %collective-permute-start.9 = (bf16[1536,256]{1,0:T(8,128)(2,1)}, bf16[1536,256]{1,0:T(8,128)(2,1)}, u32[]{:S(2)}, u32[]{:S(2)}) collective-permute-start(bf16[1536,256]{1,0:T(8,128)(2,1)} %param.23), channel_id=1, source_target_pairs={{2,0},{3,1},{0,2},{1,3},{6,4},{7,5},{4,6},{5,7},{10,8},{11,9},{8,1... | collective-permute-start | bytes 2359304 | tf_op jit(solution)/shard_map/ppermute | solution.py:973
  141.3 55.8 %collective-permute-start.5 = (bf16[512,256]{1,0:T(8,128)(2,1)S(1)}, bf16[512,256]{1,0:T(8,128)(2,1)S(1)}, u32[]{:S(2)}, u32[]{:S(2)}) collective-permute-start(bf16[512,256]{1,0:T(8,128)(2,1)S(1)} %copy-done.55), channel_id=1, source_target_pairs={{2,0},{3,1},{0,2},{1,3},{6,4},{7,5},{4,6},{5,7},{10,8},{11,9},{8,1... | collective-permute-start | bytes 786440 | tf_op jit(solution)/shard_map/ppermute | solution.py:973
  202.4 197.9 %all-gather.15.cloned.1.call-start = ((), (), s32[]{:S(2)}) async-start(), calls=%async_computation.9 | async-start | bytes 14155776 | tf_op jit(solution)/shard_map/all_gather | solution.py:1110
  202.7 67.8 %collective-permute-start.14 = (bf16[256,3072]{1,0:T(8,128)(2,1)}, bf16[256,3072]{1,0:T(8,128)(2,1)}, u32[]{:S(2)}, u32[]{:S(2)}) collective-permute-start(bf16[256,3072]{1,0:T(8,128)(2,1)} %pack_units.1), channel_id=1, source_target_pairs={{2,0},{3,1},{0,2},{1,3},{6,4},{7,5},{4,6},{5,7},{10,8},{11,9},{8,1... | collective-permute-start | bytes 4718600 | tf_op jit(solution)/shard_map/ppermute | solution.py:973
  270.6 174.5 %all-gather.17.cloned.1.call-start = ((), (), s32[]{:S(2)}) async-start(), calls=%async_computation.10 | async-start | bytes 7077888 | tf_op jit(solution)/shard_map/all_gather | solution.py:1111
  271.1 309.4 %reduce-scatter.8.cloned.1.call-start = ((), (), s32[]{:S(2)}) async-start(), calls=%async_computation.12 | async-start | bytes 14155776 | tf_op jit(solution)/shard_map/reduce_scatter | solution.py:1125
  445.0 199.1 %reduce-scatter.6.cloned.1.call-start = ((), (), s32[]{:S(2)}) async-start(), calls=%async_computation.11 | async-start | bytes 14155776 | tf_op jit(solution)/shard_map/reduce_scatter | solution.py:1125
  479.1 231.2 %reduce-scatter.10.cloned.1.call-start = ((), (), s32[]{:S(2)}) async-start(), calls=%async_computation.13 | async-start | bytes 9437184 | tf_op jit(solution)/shard_map/reduce_scatter | solution.py:1125
  606.3 260.6 %reduce-scatter.12.cloned.1.call-start = ((), (), s32[]{:S(2)}) async-start(), calls=%async_computation.14 | async-start | bytes 14155776 | tf_op jit(solution)/shard_map/reduce_scatter | solution.py:1125
  644.1 228.8 %reduce-scatter.14.cloned.1.call-start = ((), (), s32[]{:S(2)}) async-start(), calls=%async_computation.15 | async-start | bytes 4718592 | tf_op jit(solution)/shard_map/reduce_scatter | solution.py:1125
  644.2 90.8 %collective-permute-start.20 = (bf16[512,2048]{1,0:T(8,128)(2,1)}, bf16[512,2048]{1,0:T(8,128)(2,1)}, u32[]{:S(2)}, u32[]{:S(2)}) collective-permute-start(bf16[512,2048]{1,0:T(8,128)(2,1)} %get-tuple-element.131), channel_id=1, source_target_pairs={{0,1},{1,0},{2,3},{3,2},{4,5},{5,4},{6,7},{7,6},{8,9},{9,8},{10,11... | collective-permute-start | bytes 6291464 | tf_op jit(solution)/shard_map/ppermute | solution.py:969
  656.3 65.8 %collective-permute-start.21 = (bf16[1536,256]{1,0:T(8,128)(2,1)}, bf16[1536,256]{1,0:T(8,128)(2,1)}, u32[]{:S(2)}, u32[]{:S(2)}) collective-permute-start(bf16[1536,256]{1,0:T(8,128)(2,1)} %split.12), channel_id=1, source_target_pairs={{0,2},{1,3},{2,0},{3,1},{4,6},{5,7},{6,4},{7,5},{8,10},{9,11},{10,... | collective-permute-start | bytes 2359304 | tf_op jit(solution)/shard_map/ppermute | solution.py:977
  660.9 73.3 %collective-permute-start.22 = (bf16[128,3072]{1,0:T(8,128)(2,1)}, bf16[128,3072]{1,0:T(8,128)(2,1)S(1)}, u32[]{:S(2)}, u32[]{:S(2)}) collective-permute-start(bf16[128,3072]{1,0:T(8,128)(2,1)} %get-tuple-element.166), channel_id=1, source_target_pairs={{0,2},{1,3},{2,0},{3,1},{4,6},{5,7},{6,4},{7,5},{8,10},{9,11},{10,... | collective-permute-start | bytes 2359304 | tf_op jit(solution)/shard_map/ppermute | solution.py:977
  737.1 54.2 %collective-permute-start.23 = (bf16[512,2304]{1,0:T(8,128)(2,1)S(1)}, bf16[512,2304]{1,0:T(8,128)(2,1)}, u32[]{:S(2)}, u32[]{:S(2)}) collective-permute-start(bf16[512,2304]{1,0:T(8,128)(2,1)S(1)} %share.6), channel_id=1, source_target_pairs={{0,1},{4,5},{8,9},{12,13},{16,17},{20,21},{24,25},{28,29}} | collective-permute-start | bytes 7077896 | tf_op jit(solution)/shard_map/ppermute | solution.py:945
  809.3 51.0 %collective-permute-start.32 = (bf16[512,2304]{1,0:T(8,128)(2,1)}, bf16[512,2304]{1,0:T(8,128)(2,1)}, u32[]{:S(2)}, u32[]{:S(2)}) collective-permute-start(bf16[512,2304]{1,0:T(8,128)(2,1)} %get-tuple-element.145), channel_id=1, source_target_pairs={{0,1},{1,2},{4,5},{5,6},{8,9},{9,10},{12,13},{13,14},{16,17},{17,1... | collective-permute-start | bytes 7077896 | tf_op jit(solution)/shard_map/ppermute | solution.py:945
  866.8 51.9 %collective-permute-start.34 = (bf16[512,2304]{1,0:T(8,128)(2,1)}, bf16[512,2304]{1,0:T(8,128)(2,1)S(1)}, u32[]{:S(2)}, u32[]{:S(2)}) collective-permute-start(bf16[512,2304]{1,0:T(8,128)(2,1)} %convert_add_fusion.3), channel_id=1, source_target_pairs={{0,1},{1,2},{2,3},{4,5},{5,6},{6,7},{8,9},{9,10},{10,11},{12,13},{... | collective-permute-start | bytes 7077896 | tf_op jit(solution)/shard_map/ppermute | solution.py:945
  871.6 51.5 %collective-permute-start.35 = (bf16[512,2304]{1,0:T(8,128)(2,1)}, bf16[512,2304]{1,0:T(8,128)(2,1)}, u32[]{:S(2)}, u32[]{:S(2)}) collective-permute-start(bf16[512,2304]{1,0:T(8,128)(2,1)} %convert_add_fusion.2), channel_id=1, source_target_pairs={{1,0},{2,1},{3,2},{5,4},{6,5},{7,6},{9,8},{10,9},{11,10},{13,12},{... | collective-permute-start | bytes 7077896 | tf_op jit(solution)/shard_map/ppermute | solution.py:948
  (84 other events, 1451.8 us)
Sparse Core Ops, SparseCore 0:
  11.9 41.6 all-gather.6
  64.1 50.2 all-gather.10
  116.8 72.1 all-gather.8
  202.6 57.8 all-gather.12
  270.7 72.0 all-gather.14
  344.5 46.6 all-gather.16
  445.1 93.0 reduce-scatter.7
  541.7 92.4 reduce-scatter.5
  637.7 71.2 reduce-scatter.9
  712.7 92.8 reduce-scatter.11
  809.3 51.2 reduce-scatter.13
